TPU v7x, 768 devices: a whole 4x8x12 slice. The times are simulated.
768 devices in a mesh: lat: 128 (over x, y, z_lo), grow: 6 (over z_hi, core).
Axes of the slice: x: 4, y: 8, z: 12 (z_hi: 3, z_lo: 4; z = z_hi * 4 + z_lo), core: 2. Of those that a mesh axis runs over, the one named last changes fastest.
Arguments:
- phase: float32 [96, 512, 1536], P('grow', 'lat'), may hold values from -1 to 1
- solute: float32 [96, 512, 1536], P('grow', 'lat'), may hold values from -3 to 3
- seed_grain: int32 [1536], replicated, may hold values 0 or 1
- writer: int32 [6, 128], replicated, may hold values from 0 to 127, each once within a row
Outputs:
- phase_out: float32 [96, 512, 1536], P('grow', 'lat')
- solute_out: float32 [96, 512, 1536], P('grow', 'lat')
- checkpoint: float32 [6, 128, 2, 4, 1, 64], P('grow', 'lat')
Inputs may be any that keep to these rules, and one draw needn't show every extreme that they name: Each row of writer is a permutation of 0 to 127.
All inputs are finite; a program needn't handle non-finite values.
Results may differ from a plain program's by a relative error of at most 0.0003.
Values sent between devices are 32-bit elements; how exact they have to be, the bound alone decides.
No kernel may reach another device: no remote copies, remote signals or barrier semaphores. Data moves between devices by JAX's collectives and lax.ppermute only.
A program may use at most 32 MiB of HBM per device.

v0:
```python
import jax
import jax.numpy as jnp
from jax import lax
from jax.sharding import PartitionSpec as P

SHIFT = 16


time_step = 0.15
aniso_strength = 0.15
coupling = 3.0
partition = 0.15
grad_floor = 0.25
solid_u = -0.5
liquid_u = 0.0
half_root = 0.7071067811865476


def padded(cells, sides, width):
    for axis, dim in sides:
        count = lax.axis_size(axis)
        head = lax.slice_in_dim(cells, 0, width, axis=dim)
        tail = lax.slice_in_dim(cells, cells.shape[dim] - width, cells.shape[dim], axis=dim)
        cells = jnp.concatenate(
            [
                lax.ppermute(tail, axis, [(i, (i + 1) % count) for i in range(count)]),
                cells,
                lax.ppermute(head, axis, [((i + 1) % count, i) for i in range(count)]),
            ],
            axis=dim,
        )
    return cells


def from_behind(block, axis, distance):
    devices = range(lax.axis_size(axis))
    route = [(i - distance, i) for i in devices if i - distance in devices]
    return lax.ppermute(block, axis, route)


def spread(block, axis, source):
    block = jnp.where(lax.axis_index(axis) == source, block, jnp.zeros_like(block))
    return lax.psum(block, axis)


def advance(ext, grain, theta):
    phi_e = ext[0]
    sol_e = ext[1]
    p = phi_e[1:-1, 1:-1]
    pzp = phi_e[2:, 1:-1]
    pzm = phi_e[:-2, 1:-1]
    pxp = phi_e[1:-1, 2:]
    pxm = phi_e[1:-1, :-2]
    pyp = jnp.roll(p, -1, 2)
    pym = jnp.roll(p, 1, 2)
    grad_z = 0.5 * (pzp - pzm)
    grad_x = 0.5 * (pxp - pxm)
    grad_y = 0.5 * (pyp - pym)
    turned_x = (grad_x + grad_y) * half_root
    turned_y = (grad_x - grad_y) * half_root
    comp_x = jnp.where(grain, turned_x, grad_x)
    comp_y = jnp.where(grain, turned_y, grad_y)
    sq_x = comp_x * comp_x
    sq_y = comp_y * comp_y
    sq_z = grad_z * grad_z
    total_sq = sq_x + sq_y + sq_z
    quartic = sq_x * sq_x + sq_y * sq_y + sq_z * sq_z
    floored = jnp.maximum(total_sq, grad_floor)
    aniso = 1.0 + aniso_strength * (4.0 * quartic / (floored * floored) - 3.0)
    aniso_sq = aniso * aniso
    laplace = pzp + pzm + pxp + pxm + pyp + pym - 6.0 * p
    u = sol_e[1:-1, 1:-1]
    drive = p - p * p * p - coupling * (1.0 - p * p) ** 2 * (u + theta[:, None, None])
    rate = (aniso_sq * laplace + drive) / aniso_sq
    q_e = 0.5 * (1.0 - jnp.clip(phi_e, -1.0, 1.0))
    q = q_e[1:-1, 1:-1]
    uzp = sol_e[2:, 1:-1]
    uzm = sol_e[:-2, 1:-1]
    uxp = sol_e[1:-1, 2:]
    uxm = sol_e[1:-1, :-2]
    uyp = jnp.roll(u, -1, 2)
    uym = jnp.roll(u, 1, 2)
    flux = 0.5 * (q + q_e[2:, 1:-1]) * (uzp - u)
    flux = flux + 0.5 * (q + q_e[:-2, 1:-1]) * (uzm - u)
    flux = flux + 0.5 * (q + q_e[1:-1, 2:]) * (uxp - u)
    flux = flux + 0.5 * (q + q_e[1:-1, :-2]) * (uxm - u)
    flux = flux + 0.5 * (q + jnp.roll(q, -1, 2)) * (uyp - u)
    flux = flux + 0.5 * (q + jnp.roll(q, 1, 2)) * (uym - u)
    weight = 0.5 * (1.0 + partition - (1.0 - partition) * jnp.clip(p, -1.0, 1.0))
    urate = (flux + 0.5 * (1.0 + (1.0 - partition) * u) * rate) / weight
    return jnp.stack([p + time_step * rate, u + time_step * urate])


def advance_blocks(ext, grain, theta):
    count = ext.shape[1] - 2
    results = []
    for index in range((count + 7) // 8):
        start = index * 8
        size = min(8, count - start)
        results.append(
            advance(ext[:, start : start + size + 2], grain, theta[start : start + size])
        )
    return jnp.concatenate(results, axis=1)


def shards(phase, solute, seed_grain, writer):
    planes, rows, width = phase.shape
    grow_count = lax.axis_size("grow")
    grow_at = lax.axis_index("grow")
    total = planes * grow_count
    grain = seed_grain > 0
    state = jnp.stack([phase, solute])
    for turn in range(2):
        ext = padded(state, (("lat", 2), ("grow", 1)), 1)
        theta_level = (grow_at * planes + 0 + jnp.arange(planes, dtype=jnp.int32)).astype(
            jnp.float32
        )
        level = grow_at * planes - 1 + jnp.arange(ext.shape[1], dtype=jnp.int32)
        below = (level < 0)[:, None, None]
        above = (level >= total)[:, None, None]
        phase_part = jnp.where(below, 1.0, jnp.where(above, -1.0, ext[0]))
        solute_part = jnp.where(below, solid_u, jnp.where(above, liquid_u, ext[1]))
        state = advance_blocks(
            jnp.stack([phase_part, solute_part]), grain, (theta_level + 0.5) / total - 0.5
        )
    arrived = from_behind(state, "grow", -1)
    liquid = jnp.stack(
        [
            jnp.full(state.shape[1:], -1.0, jnp.float32),
            jnp.full(state.shape[1:], liquid_u, jnp.float32),
        ]
    )
    arrived = jnp.where(grow_at == grow_count - 1, liquid, arrived)
    moved = jnp.concatenate([state[:, SHIFT:], arrived], axis=1)
    coarse = state.reshape(2, SHIFT // 4, 4, rows // 4, 4, width // 4, 4).mean(axis=(2, 4, 6))
    whole = spread(coarse, "grow", 0)
    piece = width // 4 // grow_count
    mine = lax.dynamic_slice_in_dim(whole, grow_at * piece, piece, axis=3)[None]
    row_ids = lax.dynamic_index_in_dim(writer, grow_at, 0, keepdims=False)
    lat_at = lax.axis_index("lat")
    picked = (row_ids == lat_at)[:, None, None, None, None]
    gathered = jnp.sum(
        jnp.where(picked, lax.all_gather(mine, "lat", axis=0, tiled=True), 0.0), axis=0
    )
    return (moved[0], moved[1], gathered[None, None])


def solution(mesh):
    placed = (P("grow", "lat", None), P("grow", "lat", None), P(), P())
    return jax.shard_map(
        shards,
        mesh=mesh,
        in_specs=placed,
        out_specs=(
            P("grow", "lat", None),
            P("grow", "lat", None),
            P("grow", "lat", None, None, None, None),
        ),
        check_vma=False,
    )
```

profile of v0, /device:TPU:64, one launch (start us, length us, event | category | flops | bytes accessed | tf_op | source)
XLA Modules:
  0.0 499.3 jit_solution(2818138299012655145)
XLA Ops:
  0.6 1.4 copy_bitcast_fusion
  2.0 10.5 %collective-permute-start.1 = (f32[2,16,1,1536]{3,1,2,0:T(8,128)S(1)}, f32[2,16,1,1536]{3,1,2,0:T(8,128)S(1)}, u32[]{:S(2)}, u32[]{:S(2)}) collective-permute-start(f32[2,16,1,1536]{3,1,2,0:T(8,128)S(1)} %get-tuple-element.41), channel_id=1, source_target_pairs={{6,0},{12,6},{18,12},{24,18},{30,24},{36,30},{42,36},{48,42},{54,4... | collective-permute-start | bytes 589832 | tf_op jit(solution)/shard_map/ppermute | solution.py:28
  12.6 1.9 collective-permute-start
  14.6 5.3 %collective-permute-done.1 = f32[2,16,1,1536]{3,1,2,0:T(8,128)S(1)} collective-permute-done((f32[2,16,1,1536]{3,1,2,0:T(8,128)S(1)}, f32[2,16,1,1536]{3,1,2,0:T(8,128)S(1)}, u32[]{:S(2)}, u32[]{:S(2)}) %collective-permute-start.1) | collective-permute-done | bytes 196640 | tf_op jit(solution)/shard_map/ppermute | solution.py:28
  20.0 3.5 collective-permute-done
  23.6 10.4 %collective-permute-start.3 = (f32[2,1,6,1536]{3,1,2,0:T(1,128)S(1)}, f32[2,1,6,1536]{3,1,2,0:T(1,128)S(1)}, u32[]{:S(2)}, u32[]{:S(2)}) collective-permute-start(f32[2,1,6,1536]{3,1,2,0:T(1,128)S(1)} %get-tuple-element.21), channel_id=1, source_target_pairs={{1,0},{2,1},{3,2},{4,3},{5,4},{0,5},{7,6},{8,7},{9,8},{10,9},{11,1... | collective-permute-start | bytes 221192 | tf_op jit(solution)/shard_map/ppermute | solution.py:28
  34.1 1.9 collective-permute-start.2
  36.0 7.7 %collective-permute-done.2 = f32[2,1,6,1536]{3,1,2,0:T(1,128)S(1)} collective-permute-done((f32[2,1,6,1536]{3,1,2,0:T(1,128)S(1)}, f32[2,1,6,1536]{3,1,2,0:T(1,128)S(1)}, u32[]{:S(2)}, u32[]{:S(2)}) %collective-permute-start.2) | collective-permute-done | bytes 73760 | tf_op jit(solution)/shard_map/ppermute | solution.py:26
  43.7 0.3 pad_maximum_fusion
  44.0 0.3 fusion.3
  44.3 0.1 slice_bitcast_fusion.6
  44.5 0.1 fusion.135
  44.7 0.1 subtract_multiply_fusion.3
  44.8 0.1 fusion.133
  45.0 0.1 slice_bitcast_fusion.7
  45.2 0.1 fusion.131
  46.0 0.5 add_bitcast_fusion.5
  46.4 0.5 add_bitcast_fusion.7
  46.9 0.4 add_bitcast_fusion.4
  47.3 0.4 add_bitcast_fusion.6
  47.7 7.0 %collective-permute-start.5 = (f32[2,16,1,1536]{3,1,2,0:T(8,128)S(1)}, f32[2,16,1,1536]{3,1,2,0:T(8,128)S(1)}, u32[]{:S(2)}, u32[]{:S(2)}) collective-permute-start(f32[2,16,1,1536]{3,1,2,0:T(8,128)S(1)} %get-tuple-element.39), channel_id=1, source_target_pairs={{6,0},{12,6},{18,12},{24,18},{30,24},{36,30},{42,36},{48,42},{54,4... | collective-permute-start | bytes 589832 | tf_op jit(solution)/shard_map/ppermute | solution.py:28
  54.7 1.9 collective-permute-start.4
  56.6 1.9 collective-permute-done.5
  58.5 3.7 collective-permute-done.4
  62.4 2.3 collective-permute-start.7
  64.7 2.1 collective-permute-start.6
  66.7 7.5 %collective-permute-done.6 = f32[2,1,6,1536]{3,1,2,0:T(1,128)S(1)} collective-permute-done((f32[2,1,6,1536]{3,1,2,0:T(1,128)S(1)}, f32[2,1,6,1536]{3,1,2,0:T(1,128)S(1)}, u32[]{:S(2)}, u32[]{:S(2)}) %collective-permute-start.6) | collective-permute-done | bytes 73760 | tf_op jit(solution)/shard_map/ppermute | solution.py:26
  74.2 0.3 pad_maximum_fusion.1
  74.6 0.3 fusion.1
  74.9 0.1 slice_bitcast_fusion.2
  75.0 0.1 fusion.123
  75.2 0.1 subtract_multiply_fusion.1
  75.6 0.1 slice_bitcast_fusion.3
  75.7 0.1 fusion.119
  76.5 0.5 add_bitcast_fusion.1
  77.0 0.5 add_bitcast_fusion.3
  77.4 0.4 add_bitcast_fusion
  77.8 0.4 add_bitcast_fusion.2
  78.3 1.3 collective-permute-start.8
  79.6 0.7 compare_bitcast_fusion
  80.3 8.2 %reduce_sum.26 = f32[2,4,4,384,4]{4,3,2,1,0:T(8,128)} reshape(f32[2,16,1536]{2,1,0:T(8,128)S(1)} %get-tuple-element.34) | data formatting | bytes 393216 | tf_op jit(solution)/shard_map/reduce_sum | solution.py:135
  88.5 3.3 reduce_sum.27
  91.8 33.7 %psum.7 = f32[2,4,1,384]{3,1,2,0:T(4,128)S(1)} all-reduce(f32[2,4,1,384]{3,1,2,0:T(4,128)S(1)} %select_bitcast_fusion), channel_id=1, replica_groups=mesh['lat'=128,'grow'=6] {'grow'}, use_global_device_ids=true, to_apply=%region_2.3 | all-reduce | flops 3072 | bytes 24576 | tf_op jit(solution)/shard_map/psum | solution.py:43
  125.6 370.7 %all-gather = f32[256,4,1,64]{3,1,2,0:T(4,128)S(1)} all-gather(f32[2,4,1,64]{3,1,2,0:T(4,128)S(1)} %constant_dynamic-slice_fusion), channel_id=2, replica_groups=mesh['lat'=128,'grow'=6] {'lat'}, dimensions={0}, use_global_device_ids=true | all-gather | bytes 264192 | tf_op jit(solution)/shard_map/all_gather | solution.py:143
  496.2 0.8 select_reduce_fusion
  497.1 0.1 broadcast_select_fusion
  497.3 1.0 copy.9
  498.3 1.0 copy.10
  (38 shorter events, 2.4 us)
Async XLA Ops:
  0.6 13.9 %copy-start = (s32[1536]{0:T(1024)S(1)}, s32[1536]{0:T(1024)}, u32[]{:S(2)}) copy-start(s32[1536]{0:T(1024)} %param.6) | copy-start | bytes 18436
  2.0 17.9 %collective-permute-start.1 = (f32[2,16,1,1536]{3,1,2,0:T(8,128)S(1)}, f32[2,16,1,1536]{3,1,2,0:T(8,128)S(1)}, u32[]{:S(2)}, u32[]{:S(2)}) collective-permute-start(f32[2,16,1,1536]{3,1,2,0:T(8,128)S(1)} %get-tuple-element.41), channel_id=1, source_target_pairs={{6,0},{12,6},{18,12},{24,18},{30,24},{36,30},{42,36},{48,42},{54,4... | collective-permute-start | bytes 589832 | tf_op jit(solution)/shard_map/ppermute | solution.py:28
  12.6 10.9 %collective-permute-start = (f32[2,16,1,1536]{3,1,2,0:T(8,128)S(1)}, f32[2,16,1,1536]{3,1,2,0:T(8,128)S(1)}, u32[]{:S(2)}, u32[]{:S(2)}) collective-permute-start(f32[2,16,1,1536]{3,1,2,0:T(8,128)S(1)} %get-tuple-element.40), channel_id=1, source_target_pairs={{0,6},{6,12},{12,18},{18,24},{24,30},{30,36},{36,42},{42,48},{48,5... | collective-permute-start | bytes 589832 | tf_op jit(solution)/shard_map/ppermute | solution.py:26
  23.6 12.4 %collective-permute-start.3 = (f32[2,1,6,1536]{3,1,2,0:T(1,128)S(1)}, f32[2,1,6,1536]{3,1,2,0:T(1,128)S(1)}, u32[]{:S(2)}, u32[]{:S(2)}) collective-permute-start(f32[2,1,6,1536]{3,1,2,0:T(1,128)S(1)} %get-tuple-element.21), channel_id=1, source_target_pairs={{1,0},{2,1},{3,2},{4,3},{5,4},{0,5},{7,6},{8,7},{9,8},{10,9},{11,1... | collective-permute-start | bytes 221192 | tf_op jit(solution)/shard_map/ppermute | solution.py:28
  34.1 9.7 %collective-permute-start.2 = (f32[2,1,6,1536]{3,1,2,0:T(1,128)S(1)}, f32[2,1,6,1536]{3,1,2,0:T(1,128)S(1)}, u32[]{:S(2)}, u32[]{:S(2)}) collective-permute-start(f32[2,1,6,1536]{3,1,2,0:T(1,128)S(1)} %get-tuple-element.20), channel_id=1, source_target_pairs={{0,1},{1,2},{2,3},{3,4},{4,5},{5,0},{6,7},{7,8},{8,9},{9,10},{10,1... | collective-permute-start | bytes 221192 | tf_op jit(solution)/shard_map/ppermute | solution.py:26
  47.7 10.8 %collective-permute-start.5 = (f32[2,16,1,1536]{3,1,2,0:T(8,128)S(1)}, f32[2,16,1,1536]{3,1,2,0:T(8,128)S(1)}, u32[]{:S(2)}, u32[]{:S(2)}) collective-permute-start(f32[2,16,1,1536]{3,1,2,0:T(8,128)S(1)} %get-tuple-element.39), channel_id=1, source_target_pairs={{6,0},{12,6},{18,12},{24,18},{30,24},{36,30},{42,36},{48,42},{54,4... | collective-permute-start | bytes 589832 | tf_op jit(solution)/shard_map/ppermute | solution.py:28
  54.7 7.6 %collective-permute-start.4 = (f32[2,16,1,1536]{3,1,2,0:T(8,128)S(1)}, f32[2,16,1,1536]{3,1,2,0:T(8,128)S(1)}, u32[]{:S(2)}, u32[]{:S(2)}) collective-permute-start(f32[2,16,1,1536]{3,1,2,0:T(8,128)S(1)} %get-tuple-element.38), channel_id=1, source_target_pairs={{0,6},{6,12},{12,18},{18,24},{24,30},{30,36},{36,42},{42,48},{48,5... | collective-permute-start | bytes 589832 | tf_op jit(solution)/shard_map/ppermute | solution.py:26
  62.4 4.3 collective-permute-start.7
  64.7 9.6 %collective-permute-start.6 = (f32[2,1,6,1536]{3,1,2,0:T(1,128)S(1)}, f32[2,1,6,1536]{3,1,2,0:T(1,128)S(1)}, u32[]{:S(2)}, u32[]{:S(2)}) collective-permute-start(f32[2,1,6,1536]{3,1,2,0:T(1,128)S(1)} %get-tuple-element.18), channel_id=1, source_target_pairs={{0,1},{1,2},{2,3},{3,4},{4,5},{5,0},{6,7},{7,8},{8,9},{9,10},{10,1... | collective-permute-start | bytes 221192 | tf_op jit(solution)/shard_map/ppermute | solution.py:26
  78.3 418.8 %collective-permute-start.8 = (f32[2,16,4,1536]{3,1,2,0:T(8,128)S(1)}, f32[2,16,4,1536]{3,1,2,0:T(8,128)S(1)}, u32[]{:S(2)}, u32[]{:S(2)}) collective-permute-start(f32[2,16,4,1536]{3,1,2,0:T(8,128)S(1)} %get-tuple-element.35), channel_id=1, source_target_pairs={{1,0},{2,1},{3,2},{4,3},{5,4},{7,6},{8,7},{9,8},{10,9},{11,10},{13... | collective-permute-start | bytes 2359304 | tf_op jit(solution)/shard_map/ppermute | solution.py:38
  88.5 408.6 %copy-start.1 = (f32[2]{0:T(128)S(1)}, f32[2]{0:T(128)}, u32[]{:S(2)}) copy-start(f32[2]{0:T(128)} %constant.29.clone.1) | copy-start | bytes 28
where the time goes:
time: 500 us; the launch traced here: 499 us
  blocking collectives  404 us (81%)
  starting transfers between devices  39.4 us (8%)
  waiting for transfers between devices  29.7 us (6%)
  local copies, waits for them, and re-layouts  14.6 us (3%)
  other arithmetic  10.2 us (2%)
    all_gather x1, blocking collectives, shards(): lax.all_gather(mine, 'lat', axis=0, tiled=True)  371 us
    psum x1, blocking collectives, spread(): return lax.psum(block, axis)  33.7 us
    ppermute x4, starting transfers between devices, padded(): lax.ppermute(head, axis, [((i + 1) % count, i) for i in range(count)])  30.2 us
    ppermute x4, waiting for transfers between devices, padded(): lax.ppermute(tail, axis, [(i, (i + 1) % count) for i in range(count)])  22.5 us
  transfers between devices with their start and end apart: 9, of which 6 were waited for; matrix products, arithmetic and copies ran while one was open for 3% of the time, Pallas kernels for 0%

commit v1 on v0

v1 whole, which is shorter than its diff:
```python
import jax
import jax.numpy as jnp
from jax import lax
from jax.sharding import PartitionSpec as P

SHIFT = 16


time_step = 0.15
aniso_strength = 0.15
coupling = 3.0
partition = 0.15
grad_floor = 0.25
solid_u = -0.5
liquid_u = 0.0
half_root = 0.7071067811865476


def advance(ext, grain, theta):
    phi_e = ext[0]
    sol_e = ext[1]
    p = phi_e[1:-1, 1:-1]
    pzp = phi_e[2:, 1:-1]
    pzm = phi_e[:-2, 1:-1]
    pxp = phi_e[1:-1, 2:]
    pxm = phi_e[1:-1, :-2]
    pyp = jnp.roll(p, -1, 2)
    pym = jnp.roll(p, 1, 2)
    grad_z = 0.5 * (pzp - pzm)
    grad_x = 0.5 * (pxp - pxm)
    grad_y = 0.5 * (pyp - pym)
    turned_x = (grad_x + grad_y) * half_root
    turned_y = (grad_x - grad_y) * half_root
    comp_x = jnp.where(grain, turned_x, grad_x)
    comp_y = jnp.where(grain, turned_y, grad_y)
    sq_x = comp_x * comp_x
    sq_y = comp_y * comp_y
    sq_z = grad_z * grad_z
    total_sq = sq_x + sq_y + sq_z
    quartic = sq_x * sq_x + sq_y * sq_y + sq_z * sq_z
    floored = jnp.maximum(total_sq, grad_floor)
    aniso = 1.0 + aniso_strength * (4.0 * quartic / (floored * floored) - 3.0)
    aniso_sq = aniso * aniso
    laplace = pzp + pzm + pxp + pxm + pyp + pym - 6.0 * p
    u = sol_e[1:-1, 1:-1]
    drive = p - p * p * p - coupling * (1.0 - p * p) ** 2 * (u + theta[:, None, None])
    rate = (aniso_sq * laplace + drive) / aniso_sq
    q_e = 0.5 * (1.0 - jnp.clip(phi_e, -1.0, 1.0))
    q = q_e[1:-1, 1:-1]
    uzp = sol_e[2:, 1:-1]
    uzm = sol_e[:-2, 1:-1]
    uxp = sol_e[1:-1, 2:]
    uxm = sol_e[1:-1, :-2]
    uyp = jnp.roll(u, -1, 2)
    uym = jnp.roll(u, 1, 2)
    flux = 0.5 * (q + q_e[2:, 1:-1]) * (uzp - u)
    flux = flux + 0.5 * (q + q_e[:-2, 1:-1]) * (uzm - u)
    flux = flux + 0.5 * (q + q_e[1:-1, 2:]) * (uxp - u)
    flux = flux + 0.5 * (q + q_e[1:-1, :-2]) * (uxm - u)
    flux = flux + 0.5 * (q + jnp.roll(q, -1, 2)) * (uyp - u)
    flux = flux + 0.5 * (q + jnp.roll(q, 1, 2)) * (uym - u)
    weight = 0.5 * (1.0 + partition - (1.0 - partition) * jnp.clip(p, -1.0, 1.0))
    urate = (flux + 0.5 * (1.0 + (1.0 - partition) * u) * rate) / weight
    return jnp.stack([p + time_step * rate, u + time_step * urate])


def shift(block, axis, step):
    count = lax.axis_size(axis)
    return lax.ppermute(block, axis, [(i, (i + step) % count) for i in range(count)])


def fields(phase, solute, like):
    return jnp.stack(
        [jnp.full(like.shape[1:], phase, jnp.float32), jnp.full(like.shape[1:], solute, jnp.float32)]
    )


def pooled(state):
    planes, rows, width = state.shape[1:]
    columns = state.reshape(2, planes // 4, 4, rows, width).sum(axis=(2, 3))
    pick = jnp.arange(128)[:, None] // 4 == jnp.arange(32)[None]
    cells = jnp.einsum(
        "fzkl,lm->fzkm",
        columns.reshape(2, planes // 4, width // 128, 128),
        jnp.where(pick, 1.0 / 64.0, 0.0).astype(jnp.float32),
        precision=lax.Precision.HIGHEST,
    )
    return cells.reshape(2, planes // 4, width // 4)


def shards(phase, solute, seed_grain, writer):
    planes, rows, width = phase.shape
    grow_count = lax.axis_size("grow")
    grow_at = lax.axis_index("grow")
    lat_count = lax.axis_size("lat")
    lat_at = lax.axis_index("lat")
    total = planes * grow_count
    grain = seed_grain > 0
    state = jnp.stack([phase, solute])
    lowest = grow_at == 0
    highest = grow_at == grow_count - 1

    below = shift(state[:, -2:], "grow", 1)
    above = shift(state[:, :2], "grow", -1)
    left = shift(state[:, :, -2:], "lat", 1)
    right = shift(state[:, :, :2], "lat", -1)
    below = jnp.where(lowest, fields(1.0, solid_u, below), below)
    above = jnp.where(highest, fields(-1.0, liquid_u, above), above)
    edges = jnp.concatenate([below[:, 1:], above[:, :1]], axis=1)
    edges_left = shift(edges[:, :, -1:], "lat", 1)
    edges_right = shift(edges[:, :, :1], "lat", -1)
    pad = ((0, 0), (0, 0), (1, 0), (0, 0))
    dap = ((0, 0), (0, 0), (0, 1), (0, 0))
    low = ((0, 0), (1, 0), (0, 0), (0, 0))
    top = ((0, 0), (0, 1), (0, 0), (0, 0))
    ext = jnp.concatenate(
        [
            jnp.concatenate(
                [
                    jnp.pad(jnp.pad(edges_left[:, :1], pad), low),
                    below,
                    jnp.pad(jnp.pad(edges_right[:, :1], dap), low),
                ],
                axis=2,
            ),
            jnp.concatenate([left, state, right], axis=2),
            jnp.concatenate(
                [
                    jnp.pad(jnp.pad(edges_left[:, 1:], pad), top),
                    above,
                    jnp.pad(jnp.pad(edges_right[:, 1:], dap), top),
                ],
                axis=2,
            ),
        ],
        axis=1,
    )
    level = (grow_at * planes - 1 + jnp.arange(planes + 2, dtype=jnp.int32)).astype(jnp.float32)
    theta = (level + 0.5) / total - 0.5
    once = advance(ext, grain, theta)
    first = jnp.where(lowest, fields(1.0, solid_u, once[:, :1]), once[:, :1])
    last = jnp.where(highest, fields(-1.0, liquid_u, once[:, -1:]), once[:, -1:])
    state = advance(jnp.concatenate([first, once[:, 1:-1], last], axis=1), grain, theta[1:-1])

    arrived = lax.ppermute(state, "grow", [(i, i - 1) for i in range(1, grow_count)])
    moved = jnp.where(highest, fields(-1.0, liquid_u, arrived), arrived)

    coarse = pooled(state)
    piece = width // 4 // grow_count
    blocks = [
        jnp.concatenate(
            [coarse[0, :, r * piece : (r + 1) * piece], coarse[1, :, r * piece : (r + 1) * piece]], axis=1
        )
        for r in range(grow_count)
    ]
    mine = jnp.where(lowest, blocks[0], 0.0)
    for r in range(1, grow_count):
        mine = mine + lax.ppermute(blocks[r], "grow", [(0, r)])
    row_ids = lax.dynamic_index_in_dim(writer, grow_at, 0, keepdims=False)
    target = lax.dynamic_index_in_dim(row_ids, lat_at, 0, keepdims=False)
    slots = jnp.where((jnp.arange(lat_count) == target)[:, None, None], mine[None], 0.0)
    landed = lax.all_to_all(slots, "lat", 0, 0, tiled=True).sum(axis=0)
    landed = jnp.stack([landed[:, :piece], landed[:, piece:]])
    return (moved[0], moved[1], landed[None, None, :, :, None])


def solution(mesh):
    placed = (P("grow", "lat", None), P("grow", "lat", None), P(), P())
    return jax.shard_map(
        shards,
        mesh=mesh,
        in_specs=placed,
        out_specs=(
            P("grow", "lat", None),
            P("grow", "lat", None),
            P("grow", "lat", None, None, None, None),
        ),
        check_vma=False,
    )
```

time: 500 us -> 128 us (0.26)
  the two profiles are of different devices: /device:TPU:64 before, /device:TPU:1 now
where the time goes in v1:
time: 128 us; the launch traced here: 127 us
  starting transfers between devices  65.9 us (51%)
  waiting for transfers between devices  38.7 us (30%)
  other arithmetic  15.4 us (12%)
  local copies, waits for them, and re-layouts  5.98 us (5%)
    ppermute x6, starting transfers between devices, shift(): lax.ppermute(block, axis, [(i, (i + step) % count) for i in range(count)])  39.6 us
    ppermute x1, waiting for transfers between devices, shards(): lax.ppermute(state, 'grow', [(i, i - 1) for i in range(1, grow_count)])  35.3 us
    all_to_all x1, starting transfers between devices, shards(): landed = lax.all_to_all(slots, 'lat', 0, 0, tiled=True).sum(axis=0)  11.4 us
    ppermute x1, starting transfers between devices, shards(): lax.ppermute(state, 'grow', [(i, i - 1) for i in range(1, grow_count)])  11 us
    another operation x4, other arithmetic, advance(): return jnp.stack([p + time_step * rate, u + time_step * urate])  4.55 us
    ppermute x5, starting transfers between devices, shards(): mine = mine + lax.ppermute(blocks[r], 'grow', [(0, r)])  3.88 us
    add x2, other arithmetic, advance(): return jnp.stack([p + time_step * rate, u + time_step * urate])  3.57 us
  transfers between devices with their start and end apart: 13, of which 4 were waited for; matrix products, arithmetic and copies ran while one was open for 4% of the time, Pallas kernels for 0%

profile of v1, /device:TPU:1, one launch (start us, length us, event | category | flops | bytes accessed | tf_op | source)
XLA Modules:
  0.0 127.3 jit_solution(8914412833988238944)
XLA Ops:
  0.7 1.0 pad_maximum_fusion.9
  1.7 12.0 %collective-permute-start = (f32[2,2,4,1536]{3,2,1,0:T(4,128)S(1)}, f32[2,2,4,1536]{3,2,1,0:T(4,128)S(1)}, u32[]{:S(2)}, u32[]{:S(2)}) collective-permute-start(f32[2,2,4,1536]{3,2,1,0:T(4,128)S(1)} %get-tuple-element.47), channel_id=1, source_target_pairs={{0,1},{1,2},{2,3},{3,4},{4,5},{5,0},{6,7},{7,8},{8,9},{9,10},{10,1... | collective-permute-start | bytes 294920 | tf_op jit(solution)/shard_map/ppermute | solution.py:69
  13.7 2.3 %collective-permute-start.1 = (f32[2,2,4,1536]{3,2,1,0:T(4,128)S(1)}, f32[2,2,4,1536]{3,2,1,0:T(4,128)S(1)}, u32[]{:S(2)}, u32[]{:S(2)}) collective-permute-start(f32[2,2,4,1536]{3,2,1,0:T(4,128)S(1)} %get-tuple-element.48), channel_id=1, source_target_pairs={{0,5},{1,0},{2,1},{3,2},{4,3},{5,4},{6,11},{7,6},{8,7},{9,8},{10,9... | collective-permute-start | bytes 294920 | tf_op jit(solution)/shard_map/ppermute | solution.py:69
  16.0 1.8 %fusion.38 = (f32[2,16,2,1536]{3,2,1,0:T(2,128)S(1)}, f32[2,16,2,1536]{3,2,1,0:T(2,128)S(1)}) fusion(f32[1,16,4,1536]{3,2,1,0:T(4,128)} %bitcast.78, f32[1,16,4,1536]{3,2,1,0:T(4,128)} %bitcast.75), kind=kLoop, calls=%fused_computation.79 | loop fusion | flops 196608 | bytes 1572864 | tf_op jit(solution)/shard_map/stack | solution.py:99
  17.8 3.6 %collective-permute-start.4 = (f32[2,16,2,1536]{3,2,1,0:T(2,128)S(1)}, f32[2,16,2,1536]{3,2,1,0:T(2,128)S(1)}, u32[]{:S(2)}, u32[]{:S(2)}) collective-permute-start(f32[2,16,2,1536]{3,2,1,0:T(2,128)S(1)} %get-tuple-element.45), channel_id=1, source_target_pairs={{0,6},{6,12},{12,18},{18,24},{24,30},{30,36},{36,42},{42,48},{48,5... | collective-permute-start | bytes 1179656 | tf_op jit(solution)/shard_map/ppermute | solution.py:69
  21.5 10.3 %collective-permute-start.5 = (f32[2,16,2,1536]{3,2,1,0:T(2,128)S(1)}, f32[2,16,2,1536]{3,2,1,0:T(2,128)S(1)}, u32[]{:S(2)}, u32[]{:S(2)}) collective-permute-start(f32[2,16,2,1536]{3,2,1,0:T(2,128)S(1)} %get-tuple-element.46), channel_id=1, source_target_pairs={{0,762},{6,0},{12,6},{18,12},{24,18},{30,24},{36,30},{42,36},{48,4... | collective-permute-start | bytes 1179656 | tf_op jit(solution)/shard_map/ppermute | solution.py:69
  32.0 1.9 %collective-permute-start.2 = (f32[2,2,1,1536]{3,2,1,0:T(1,128)S(1)}, f32[2,2,1,1536]{3,2,1,0:T(1,128)S(1)}, u32[]{:S(2)}, u32[]{:S(2)}) collective-permute-start(f32[2,2,1,1536]{3,2,1,0:T(1,128)S(1)} %get-tuple-element.49), channel_id=1, source_target_pairs={{0,6},{6,12},{12,18},{18,24},{24,30},{30,36},{36,42},{42,48},{48,5... | collective-permute-start | bytes 73736 | tf_op jit(solution)/shard_map/ppermute | solution.py:69
  34.0 1.3 dynamic_slice.6
  35.3 9.4 %collective-permute-start.3 = (f32[2,2,1,1536]{3,2,1,0:T(1,128)S(1)}, f32[2,2,1,1536]{3,2,1,0:T(1,128)S(1)}, u32[]{:S(2)}, u32[]{:S(2)}) collective-permute-start(f32[2,2,1,1536]{3,2,1,0:T(1,128)S(1)} %get-tuple-element.50), channel_id=1, source_target_pairs={{0,762},{6,0},{12,6},{18,12},{24,18},{30,24},{36,30},{42,36},{48,4... | collective-permute-start | bytes 73736 | tf_op jit(solution)/shard_map/ppermute | solution.py:69
  44.7 2.4 %collective-permute-done.2 = f32[2,2,1,1536]{3,2,1,0:T(1,128)S(1)} collective-permute-done((f32[2,2,1,1536]{3,2,1,0:T(1,128)S(1)}, f32[2,2,1,1536]{3,2,1,0:T(1,128)S(1)}, u32[]{:S(2)}, u32[]{:S(2)}) %collective-permute-start.2) | collective-permute-done | bytes 24608 | tf_op jit(solution)/shard_map/ppermute | solution.py:69
  47.1 0.7 fusion
  47.9 0.1 slice_bitcast_fusion.1
  48.0 0.1 fusion.75
  48.1 0.7 fusion.74
  48.8 0.1 subtract_multiply_fusion
  48.9 0.3 fusion.76
  49.3 0.1 fusion.77
  49.4 2.1 %add_bitcast_fusion.1 = (f32[1,18,6,1536]{3,2,1,0:T(8,128)S(1)}, f32[18,6,1536]{2,1,0:T(8,128)S(1)}) fusion(f32[20,8,1536]{2,1,0:T(8,128)S(1)} %get-tuple-element.13, f32[18]{0:T(128)S(1)} %multiply_add_fusion.2, f32[20,8,1536]{2,1,0:T(8,128)S(1)} %get-tuple-element.14, f32[18,6,1535]{2,1,0:T(8,128)S(1)} %get-tuple-element.20, ...), kind=kLoop, calls=%fused_computation.66 | loop fusion | flops 8792064 | bytes 6637128 | tf_op jit(solution)/shard_map/stack | solution.py:64
  51.5 2.1 %add_bitcast_fusion = f32[1,18,6,1536]{3,2,1,0:T(8,128)S(1)} fusion(f32[18,6,1535]{2,1,0:T(8,128)S(1)} %get-tuple-element.69, f32[18,6,1]{2,1,0:T(8,128)S(1)} %get-tuple-element.71, f32[18,6,1535]{2,1,0:T(8,128)S(1)} %get-tuple-element.24, f32[18,6,1]{2,1,0:T(8,128)S(1)} %get-tuple-element.26, f32[18,6,1]{2,1,0:T(8,128)S(1)} %get-tuple-element.72, ...), kind=kLoop, calls=%fused_computation.65 | loop fusion | flops 7464960 | bytes 11280384 | tf_op jit(solution)/shard_map/stack | solution.py:64
  53.6 0.1 fusion.6
  53.8 0.7 copy-done.4
  54.6 0.2 pad_maximum_fusion
  54.8 0.1 slice_bitcast_fusion.3
  54.9 0.3 fusion.80
  55.3 0.3 fusion.84
  55.7 0.1 subtract_multiply_fusion.1
  55.8 0.3 fusion.82
  56.2 1.7 %multiply_add_fusion.1 = (f32[16,4,1536]{2,1,0:T(4,128)S(1)}, f32[16,4,1536]{2,1,0:T(4,128)S(1)}) fusion(f32[18,6,1536]{2,1,0:T(8,128)S(1)} %get-tuple-element.15, f32[16]{0:T(128)S(1)} %slice.358, f32[18,6,1536]{2,1,0:T(8,128)S(1)} %get-tuple-element.16, f32[16,4,1535]{2,1,0:T(4,128)S(1)} %get-tuple-element.32, f32[16,4,1]{2,1,0:T(4,128)S(1)} %get-tuple-element.34, ...), kind=kLoop, calls=%fused_computation.117 | loop fusion | flops 5210112 | bytes 3933760 | tf_op jit(solution)/shard_map/add | solution.py:64
  57.9 1.9 %multiply_add_fusion = f32[16,4,1536]{2,1,0:T(4,128)S(1)} fusion(f32[16,4,1535]{2,1,0:T(4,128)S(1)} %get-tuple-element.40, f32[16,4,1]{2,1,0:T(4,128)S(1)} %get-tuple-element.42, f32[16,4,1535]{2,1,0:T(4,128)S(1)} %get-tuple-element.36, f32[16,4,1]{2,1,0:T(4,128)S(1)} %get-tuple-element.38, f32[16,4,1]{2,1,0:T(4,128)S(1)} %get-tuple-element.41, ...), kind=kLoop, calls=%fused_computation.116 | loop fusion | flops 4423680 | bytes 6684672 | tf_op jit(solution)/shard_map/add | solution.py:64
  59.8 0.3 maximum_reduce_fusion
  60.1 0.2 fusion.59
  60.6 1.3 %collective-permute-start.7 = (f32[4,128]{1,0:T(4,128)S(1)}, f32[4,128]{1,0:T(4,128)S(1)}, u32[]{:S(2)}, u32[]{:S(2)}) collective-permute-start(f32[4,128]{1,0:T(4,128)S(1)} %pad_maximum_fusion.13), channel_id=1, source_target_pairs={{0,1},{6,7},{12,13},{18,19},{24,25},{30,31},{36,37},{42,43},{48,49... | collective-permute-start | bytes 6152 | tf_op jit(solution)/shard_map/ppermute | solution.py:158
  61.9 0.7 collective-permute-start.8
  62.7 0.7 collective-permute-start.9
  63.4 0.7 collective-permute-start.10
  64.1 0.7 collective-permute-start.11
  64.8 0.7 iota_compare_fusion.6
  65.4 0.4 collective-permute-done.7
  65.9 0.9 broadcast_select_fusion.1
  66.8 11.4 %all-to-all-start = ((f32[128,4,128]{2,1,0:T(4,128)}), f32[128,4,128]{2,1,0:T(4,128)S(1)}, u32[]{:S(2)}, u32[]{:S(2)}) async-start(f32[128,4,128]{2,1,0:T(4,128)} %broadcast_select_fusion.1), calls=%async_computation | async-start | bytes 524288 | tf_op jit(solution)/shard_map/all_to_all | solution.py:162
  78.2 0.2 pad_maximum_fusion.3
  78.4 11.0 %collective-permute-start.6 = (f32[2,16,4,1536]{3,2,1,0:T(4,128)S(1)}, f32[2,16,4,1536]{3,2,1,0:T(4,128)S(1)}, u32[]{:S(2)}, u32[]{:S(2)}) collective-permute-start(f32[2,16,4,1536]{3,2,1,0:T(4,128)S(1)} %pad_maximum_fusion.3), channel_id=1, source_target_pairs={{1,0},{2,1},{3,2},{4,3},{5,4},{7,6},{8,7},{9,8},{10,9},{11,10},{13... | collective-permute-start | bytes 2359304 | tf_op jit(solution)/shard_map/ppermute | solution.py:145
  89.4 0.5 all-to-all-done
  90.0 0.1 reduce_sum.19
  90.2 0.6 pad_maximum_fusion.12
  90.8 35.3 %collective-permute-done.6 = f32[2,16,4,1536]{3,2,1,0:T(4,128)S(1)} collective-permute-done((f32[2,16,4,1536]{3,2,1,0:T(4,128)S(1)}, f32[2,16,4,1536]{3,2,1,0:T(4,128)S(1)}, u32[]{:S(2)}, u32[]{:S(2)}) %collective-permute-start.6) | collective-permute-done | bytes 786464 | tf_op jit(solution)/shard_map/ppermute | solution.py:145
  126.1 0.2 broadcast_select_fusion
  126.4 0.9 slice_bitcast_fusion.4
  (49 shorter events, 1.3 us)
Async XLA Ops:
  0.6 31.2 %copy-start.3 = (f32[2,2,4,1536]{3,2,1,0:T(4,128)S(1)}, f32[2,2,4,1536]{3,2,1,0:T(4,128)}, u32[]{:S(2)}) copy-start(f32[2,2,4,1536]{3,2,1,0:T(4,128)} %constant.39.clone.1) | copy-start | bytes 294916
  0.6 31.3 %copy-start.2 = (f32[2,2,4,1536]{3,2,1,0:T(4,128)S(1)}, f32[2,2,4,1536]{3,2,1,0:T(4,128)}, u32[]{:S(2)}) copy-start(f32[2,2,4,1536]{3,2,1,0:T(4,128)} %constant.40.clone.1) | copy-start | bytes 294916
  0.7 46.5 %copy-start.1 = (f32[16,4,1536]{2,1,0:T(4,128)S(1)}, f32[16,4,1536]{2,1,0:T(4,128)}, u32[]{:S(2)}) copy-start(f32[16,4,1536]{2,1,0:T(4,128)} %param.4) | copy-start | bytes 1179652
  0.7 46.5 %copy-start = (f32[16,4,1536]{2,1,0:T(4,128)S(1)}, f32[16,4,1536]{2,1,0:T(4,128)}, u32[]{:S(2)}) copy-start(f32[16,4,1536]{2,1,0:T(4,128)} %param.5) | copy-start | bytes 1179652
  0.7 31.1 %copy-start.6 = (s32[1536]{0:T(1024)S(1)}, s32[1536]{0:T(1024)}, u32[]{:S(2)}) copy-start(s32[1536]{0:T(1024)} %param.6) | copy-start | bytes 18436
  1.7 30.2 %collective-permute-start = (f32[2,2,4,1536]{3,2,1,0:T(4,128)S(1)}, f32[2,2,4,1536]{3,2,1,0:T(4,128)S(1)}, u32[]{:S(2)}, u32[]{:S(2)}) collective-permute-start(f32[2,2,4,1536]{3,2,1,0:T(4,128)S(1)} %get-tuple-element.47), channel_id=1, source_target_pairs={{0,1},{1,2},{2,3},{3,4},{4,5},{5,0},{6,7},{7,8},{8,9},{9,10},{10,1... | collective-permute-start | bytes 294920 | tf_op jit(solution)/shard_map/ppermute | solution.py:69
  13.7 18.2 %collective-permute-start.1 = (f32[2,2,4,1536]{3,2,1,0:T(4,128)S(1)}, f32[2,2,4,1536]{3,2,1,0:T(4,128)S(1)}, u32[]{:S(2)}, u32[]{:S(2)}) collective-permute-start(f32[2,2,4,1536]{3,2,1,0:T(4,128)S(1)} %get-tuple-element.48), channel_id=1, source_target_pairs={{0,5},{1,0},{2,1},{3,2},{4,3},{5,4},{6,11},{7,6},{8,7},{9,8},{10,9... | collective-permute-start | bytes 294920 | tf_op jit(solution)/shard_map/ppermute | solution.py:69
  17.8 29.3 %collective-permute-start.4 = (f32[2,16,2,1536]{3,2,1,0:T(2,128)S(1)}, f32[2,16,2,1536]{3,2,1,0:T(2,128)S(1)}, u32[]{:S(2)}, u32[]{:S(2)}) collective-permute-start(f32[2,16,2,1536]{3,2,1,0:T(2,128)S(1)} %get-tuple-element.45), channel_id=1, source_target_pairs={{0,6},{6,12},{12,18},{18,24},{24,30},{30,36},{36,42},{42,48},{48,5... | collective-permute-start | bytes 1179656 | tf_op jit(solution)/shard_map/ppermute | solution.py:69
  21.5 25.7 %collective-permute-start.5 = (f32[2,16,2,1536]{3,2,1,0:T(2,128)S(1)}, f32[2,16,2,1536]{3,2,1,0:T(2,128)S(1)}, u32[]{:S(2)}, u32[]{:S(2)}) collective-permute-start(f32[2,16,2,1536]{3,2,1,0:T(2,128)S(1)} %get-tuple-element.46), channel_id=1, source_target_pairs={{0,762},{6,0},{12,6},{18,12},{24,18},{30,24},{36,30},{42,36},{48,4... | collective-permute-start | bytes 1179656 | tf_op jit(solution)/shard_map/ppermute | solution.py:69
  32.0 15.1 %collective-permute-start.2 = (f32[2,2,1,1536]{3,2,1,0:T(1,128)S(1)}, f32[2,2,1,1536]{3,2,1,0:T(1,128)S(1)}, u32[]{:S(2)}, u32[]{:S(2)}) collective-permute-start(f32[2,2,1,1536]{3,2,1,0:T(1,128)S(1)} %get-tuple-element.49), channel_id=1, source_target_pairs={{0,6},{6,12},{12,18},{18,24},{24,30},{30,36},{36,42},{42,48},{48,5... | collective-permute-start | bytes 73736 | tf_op jit(solution)/shard_map/ppermute | solution.py:69
  35.3 11.8 %collective-permute-start.3 = (f32[2,2,1,1536]{3,2,1,0:T(1,128)S(1)}, f32[2,2,1,1536]{3,2,1,0:T(1,128)S(1)}, u32[]{:S(2)}, u32[]{:S(2)}) collective-permute-start(f32[2,2,1,1536]{3,2,1,0:T(1,128)S(1)} %get-tuple-element.50), channel_id=1, source_target_pairs={{0,762},{6,0},{12,6},{18,12},{24,18},{30,24},{36,30},{42,36},{48,4... | collective-permute-start | bytes 73736 | tf_op jit(solution)/shard_map/ppermute | solution.py:69
  53.6 0.9 copy-start.4
  53.6 0.9 copy-start.5
  59.8 66.3 %copy-start.7 = (f32[2]{0:T(128)S(1)}, f32[2]{0:T(128)}, u32[]{:S(2)}) copy-start(f32[2]{0:T(128)} %constant.36.clone.1) | copy-start | bytes 28
  60.6 5.3 %collective-permute-start.7 = (f32[4,128]{1,0:T(4,128)S(1)}, f32[4,128]{1,0:T(4,128)S(1)}, u32[]{:S(2)}, u32[]{:S(2)}) collective-permute-start(f32[4,128]{1,0:T(4,128)S(1)} %pad_maximum_fusion.13), channel_id=1, source_target_pairs={{0,1},{6,7},{12,13},{18,19},{24,25},{30,31},{36,37},{42,43},{48,49... | collective-permute-start | bytes 6152 | tf_op jit(solution)/shard_map/ppermute | solution.py:158
  61.9 3.9 %collective-permute-start.8 = (f32[4,128]{1,0:T(4,128)S(1)}, f32[4,128]{1,0:T(4,128)S(1)}, u32[]{:S(2)}, u32[]{:S(2)}) collective-permute-start(f32[4,128]{1,0:T(4,128)S(1)} %pad_maximum_fusion.14), channel_id=1, source_target_pairs={{0,2},{6,8},{12,14},{18,20},{24,26},{30,32},{36,38},{42,44},{48,50... | collective-permute-start | bytes 6152 | tf_op jit(solution)/shard_map/ppermute | solution.py:158
  62.7 3.2 %collective-permute-start.9 = (f32[4,128]{1,0:T(4,128)S(1)}, f32[4,128]{1,0:T(4,128)S(1)}, u32[]{:S(2)}, u32[]{:S(2)}) collective-permute-start(f32[4,128]{1,0:T(4,128)S(1)} %pad_maximum_fusion.15), channel_id=1, source_target_pairs={{0,3},{6,9},{12,15},{18,21},{24,27},{30,33},{36,39},{42,45},{48,51... | collective-permute-start | bytes 6152 | tf_op jit(solution)/shard_map/ppermute | solution.py:158
  63.4 2.4 %collective-permute-start.10 = (f32[4,128]{1,0:T(4,128)S(1)}, f32[4,128]{1,0:T(4,128)S(1)}, u32[]{:S(2)}, u32[]{:S(2)}) collective-permute-start(f32[4,128]{1,0:T(4,128)S(1)} %pad_maximum_fusion.16), channel_id=1, source_target_pairs={{0,4},{6,10},{12,16},{18,22},{24,28},{30,34},{36,40},{42,46},{48,5... | collective-permute-start | bytes 6152 | tf_op jit(solution)/shard_map/ppermute | solution.py:158
  64.1 1.7 %collective-permute-start.11 = (f32[4,128]{1,0:T(4,128)S(1)}, f32[4,128]{1,0:T(4,128)S(1)}, u32[]{:S(2)}, u32[]{:S(2)}) collective-permute-start(f32[4,128]{1,0:T(4,128)S(1)} %pad_maximum_fusion.17), channel_id=1, source_target_pairs={{0,5},{6,11},{12,17},{18,23},{24,29},{30,35},{36,41},{42,47},{48,5... | collective-permute-start | bytes 6152 | tf_op jit(solution)/shard_map/ppermute | solution.py:158
  66.8 23.1 %all-to-all-start = ((f32[128,4,128]{2,1,0:T(4,128)}), f32[128,4,128]{2,1,0:T(4,128)S(1)}, u32[]{:S(2)}, u32[]{:S(2)}) async-start(f32[128,4,128]{2,1,0:T(4,128)} %broadcast_select_fusion.1), calls=%async_computation | async-start | bytes 524288 | tf_op jit(solution)/shard_map/all_to_all | solution.py:162
  78.4 47.7 %collective-permute-start.6 = (f32[2,16,4,1536]{3,2,1,0:T(4,128)S(1)}, f32[2,16,4,1536]{3,2,1,0:T(4,128)S(1)}, u32[]{:S(2)}, u32[]{:S(2)}) collective-permute-start(f32[2,16,4,1536]{3,2,1,0:T(4,128)S(1)} %pad_maximum_fusion.3), channel_id=1, source_target_pairs={{1,0},{2,1},{3,2},{4,3},{5,4},{7,6},{8,7},{9,8},{10,9},{11,10},{13... | collective-permute-start | bytes 2359304 | tf_op jit(solution)/shard_map/ppermute | solution.py:145

commit v2 on v1

--- a/solution.py
+++ b/solution.py
@@ -2,8 +2,6 @@
 import jax.numpy as jnp
 from jax import lax
 from jax.sharding import PartitionSpec as P
-
-SHIFT = 16
 
 
 time_step = 0.15
@@ -64,9 +62,13 @@
     return jnp.stack([p + time_step * rate, u + time_step * urate])
 
 
-def shift(block, axis, step):
+def exchange(low, high, axis):
     count = lax.axis_size(axis)
-    return lax.ppermute(block, axis, [(i, (i + step) % count) for i in range(count)])
+    even = lax.axis_index(axis) % 2 == 0
+    inner = lax.ppermute(jnp.where(even, high, low), axis, [(i, i ^ 1) for i in range(count)])
+    others = [(i, (i - 1 if i % 2 == 0 else i + 1) % count) for i in range(count)]
+    outer = lax.ppermute(jnp.where(even, low, high), axis, others)
+    return jnp.where(even, outer, inner), jnp.where(even, inner, outer)
 
 
 def fields(phase, solute, like):
@@ -88,8 +90,8 @@
     return cells.reshape(2, planes // 4, width // 4)
 
 
-def shards(phase, solute, seed_grain, writer):
-    planes, rows, width = phase.shape
+def work(phase, solute, seed_grain, writer):
+    planes, _, width = phase.shape
     grow_count = lax.axis_size("grow")
     grow_at = lax.axis_index("grow")
     lat_count = lax.axis_size("lat")
@@ -100,39 +102,14 @@
     lowest = grow_at == 0
     highest = grow_at == grow_count - 1
 
-    below = shift(state[:, -2:], "grow", 1)
-    above = shift(state[:, :2], "grow", -1)
-    left = shift(state[:, :, -2:], "lat", 1)
-    right = shift(state[:, :, :2], "lat", -1)
+    below, above = exchange(state[:, :2], state[:, -2:], "grow")
     below = jnp.where(lowest, fields(1.0, solid_u, below), below)
     above = jnp.where(highest, fields(-1.0, liquid_u, above), above)
-    edges = jnp.concatenate([below[:, 1:], above[:, :1]], axis=1)
-    edges_left = shift(edges[:, :, -1:], "lat", 1)
-    edges_right = shift(edges[:, :, :1], "lat", -1)
-    pad = ((0, 0), (0, 0), (1, 0), (0, 0))
-    dap = ((0, 0), (0, 0), (0, 1), (0, 0))
-    low = ((0, 0), (1, 0), (0, 0), (0, 0))
-    top = ((0, 0), (0, 1), (0, 0), (0, 0))
+    tall = jnp.concatenate([below[:, 1:], state, above[:, :1]], axis=1)
+    left, right = exchange(tall[:, :, :2], tall[:, :, -2:], "lat")
+    pad = ((0, 0), (0, 0), (2, 2), (0, 0))
     ext = jnp.concatenate(
-        [
-            jnp.concatenate(
-                [
-                    jnp.pad(jnp.pad(edges_left[:, :1], pad), low),
-                    below,
-                    jnp.pad(jnp.pad(edges_right[:, :1], dap), low),
-                ],
-                axis=2,
-            ),
-            jnp.concatenate([left, state, right], axis=2),
-            jnp.concatenate(
-                [
-                    jnp.pad(jnp.pad(edges_left[:, 1:], pad), top),
-                    above,
-                    jnp.pad(jnp.pad(edges_right[:, 1:], dap), top),
-                ],
-                axis=2,
-            ),
-        ],
+        [jnp.pad(below[:, :1], pad), jnp.concatenate([left, tall, right], axis=2), jnp.pad(above[:, 1:], pad)],
         axis=1,
     )
     level = (grow_at * planes - 1 + jnp.arange(planes + 2, dtype=jnp.int32)).astype(jnp.float32)
@@ -167,7 +144,7 @@
 def solution(mesh):
     placed = (P("grow", "lat", None), P("grow", "lat", None), P(), P())
     return jax.shard_map(
-        shards,
+        work,
         mesh=mesh,
         in_specs=placed,
         out_specs=(

time: 128 us -> 132 us (1.031)
  waiting for transfers between devices: 38.7 us -> 57.6 us
  starting transfers between devices: 65.9 us -> 51.9 us
    ppermute x12 -> x10, waiting for transfers between devices: 38.1 us -> 57.5 us  [the longest x1 35.7 us: work(): lax.ppermute(state, 'grow', [(i, i - 1) for i in range(1, grow_count)])]
    ppermute x12 -> x10, starting transfers between devices: 54.5 us -> 39.4 us  [the longest x2 14.3 us: exchange(): lax.ppermute(jnp.where(even, high, low), axis, [(i, i ^ 1) for i in range...]
    another operation x2 -> x1, other arithmetic: 2.4 us -> 0.6 us  [work(): landed = jnp.stack([landed[:, :piece], landed[:, piece:]])]
    select_n x5 -> x8, other arithmetic: 1.17 us -> 2.8 us  [the longest x2 1.32 us: exchange(): outer = lax.ppermute(jnp.where(even, low, high), axis, others)]
  transfers between devices with their start and end apart: 13 -> 11, of which waited for: 4 -> 5; matrix products, arithmetic and copies ran while one was open for 4% -> 3% of each run, Pallas kernels for 0% -> 0%
where the time goes in v2:
time: 132 us; the launch traced here: 131 us
  waiting for transfers between devices  57.6 us (44%)
  starting transfers between devices  51.9 us (39%)
  other arithmetic  14.3 us (11%)
  local copies, waits for them, and re-layouts  5.99 us (5%)
    ppermute x1, waiting for transfers between devices, work(): lax.ppermute(state, 'grow', [(i, i - 1) for i in range(1, grow_count)])  35.7 us
    ppermute x2, waiting for transfers between devices, exchange(): outer = lax.ppermute(jnp.where(even, low, high), axis, others)  15.1 us
    ppermute x2, starting transfers between devices, exchange(): lax.ppermute(jnp.where(even, high, low), axis, [(i, i ^ 1) for i in range...  14.3 us
    all_to_all x1, starting transfers between devices, work(): landed = lax.all_to_all(slots, 'lat', 0, 0, tiled=True).sum(axis=0)  12.5 us
    ppermute x1, starting transfers between devices, work(): lax.ppermute(state, 'grow', [(i, i - 1) for i in range(1, grow_count)])  11.9 us
    ppermute x2, starting transfers between devices, exchange(): outer = lax.ppermute(jnp.where(even, low, high), axis, others)  9.35 us
    another operation x4, other arithmetic, advance(): return jnp.stack([p + time_step * rate, u + time_step * urate])  4.54 us
    ppermute x2, waiting for transfers between devices, exchange(): lax.ppermute(jnp.where(even, high, low), axis, [(i, i ^ 1) for i in range...  4.53 us
  transfers between devices with their start and end apart: 11, of which 5 were waited for; matrix products, arithmetic and copies ran while one was open for 3% of the time, Pallas kernels for 0%

profile of v2, /device:TPU:1, one launch (start us, length us, event | category | flops | bytes accessed | tf_op | source)
XLA Modules:
  0.0 131.0 jit_solution(1482549682028337654)
XLA Ops:
  0.7 1.0 broadcast_select_fusion.7
  1.7 12.4 %collective-permute-start.1 = (f32[2,2,4,1536]{3,2,1,0:T(4,128)S(1)}, f32[2,2,4,1536]{3,2,1,0:T(4,128)S(1)}, u32[]{:S(2)}, u32[]{:S(2)}) collective-permute-start(f32[2,2,4,1536]{3,2,1,0:T(4,128)S(1)} %bitcast.87), channel_id=1, source_target_pairs={{0,1},{1,0},{2,3},{3,2},{4,5},{5,4},{6,7},{7,6},{8,9},{9,8},{10,11... | collective-permute-start | bytes 294920 | tf_op jit(solution)/shard_map/ppermute | solution.py:68
  14.1 1.9 %collective-permute-start = (f32[2,2,4,1536]{3,2,1,0:T(4,128)S(1)}, f32[2,2,4,1536]{3,2,1,0:T(4,128)S(1)}, u32[]{:S(2)}, u32[]{:S(2)}) collective-permute-start(f32[2,2,4,1536]{3,2,1,0:T(4,128)S(1)} %get-tuple-element.13), channel_id=1, source_target_pairs={{0,5},{1,2},{2,1},{3,4},{4,3},{5,0},{6,11},{7,8},{8,7},{9,10},{10,... | collective-permute-start | bytes 294920 | tf_op jit(solution)/shard_map/ppermute | solution.py:70
  16.1 8.2 %collective-permute-done = f32[2,2,4,1536]{3,2,1,0:T(4,128)S(1)} collective-permute-done((f32[2,2,4,1536]{3,2,1,0:T(4,128)S(1)}, f32[2,2,4,1536]{3,2,1,0:T(4,128)S(1)}, u32[]{:S(2)}, u32[]{:S(2)}) %collective-permute-start) | collective-permute-done | bytes 98336 | tf_op jit(solution)/shard_map/ppermute | solution.py:70
  24.4 0.2 pad_maximum_fusion.1
  24.6 0.3 broadcast_select_fusion.3
  24.9 7.4 %collective-permute-start.2 = (f32[2,18,2,1536]{3,2,1,0:T(2,128)S(1)}, f32[2,18,2,1536]{3,2,1,0:T(2,128)S(1)}, u32[]{:S(2)}, u32[]{:S(2)}) collective-permute-start(f32[2,18,2,1536]{3,2,1,0:T(2,128)S(1)} %get-tuple-element.48), channel_id=1, source_target_pairs={{0,762},{6,12},{12,6},{18,24},{24,18},{30,36},{36,30},{42,48},{48,... | collective-permute-start | bytes 1327112 | tf_op jit(solution)/shard_map/ppermute | solution.py:70
  32.3 1.9 %collective-permute-start.3 = (f32[2,18,2,1536]{3,2,1,0:T(2,128)S(1)}, f32[2,18,2,1536]{3,2,1,0:T(2,128)S(1)}, u32[]{:S(2)}, u32[]{:S(2)}) collective-permute-start(f32[2,18,2,1536]{3,2,1,0:T(2,128)S(1)} %get-tuple-element.49), channel_id=1, source_target_pairs={{0,6},{6,0},{12,18},{18,12},{24,30},{30,24},{36,42},{42,36},{48,54... | collective-permute-start | bytes 1327112 | tf_op jit(solution)/shard_map/ppermute | solution.py:68
  34.3 1.3 dynamic_slice.6
  35.6 6.8 %collective-permute-done.2 = f32[2,18,2,1536]{3,2,1,0:T(2,128)S(1)} collective-permute-done((f32[2,18,2,1536]{3,2,1,0:T(2,128)S(1)}, f32[2,18,2,1536]{3,2,1,0:T(2,128)S(1)}, u32[]{:S(2)}, u32[]{:S(2)}) %collective-permute-start.2) | collective-permute-done | bytes 442400 | tf_op jit(solution)/shard_map/ppermute | solution.py:70
  42.5 4.5 %collective-permute-done.3 = f32[2,18,2,1536]{3,2,1,0:T(2,128)S(1)} collective-permute-done((f32[2,18,2,1536]{3,2,1,0:T(2,128)S(1)}, f32[2,18,2,1536]{3,2,1,0:T(2,128)S(1)}, u32[]{:S(2)}, u32[]{:S(2)}) %collective-permute-start.3) | collective-permute-done | bytes 442400 | tf_op jit(solution)/shard_map/ppermute | solution.py:68
  47.0 0.3 broadcast_select_fusion.1
  47.3 0.6 select_maximum_fusion
  47.9 0.1 subtract_multiply_fusion
  48.1 0.1 slice_bitcast_fusion.1
  48.3 0.3 fusion.67
  48.7 0.3 fusion.71
  49.1 0.3 fusion.69
  49.5 2.1 %add_bitcast_fusion.1 = (f32[1,18,6,1536]{3,2,1,0:T(8,128)S(1)}, f32[18,6,1536]{2,1,0:T(8,128)S(1)}) fusion(f32[20,8,1536]{2,1,0:T(8,128)S(1)} %get-tuple-element.16, f32[18]{0:T(128)S(1)} %multiply_add_fusion.2, f32[20,8,1536]{2,1,0:T(8,128)S(1)} %get-tuple-element.17, f32[18,6,1535]{2,1,0:T(8,128)S(1)} %get-tuple-element.23, ...), kind=kLoop, calls=%fused_computation.57 | loop fusion | flops 8792064 | bytes 6637128 | tf_op jit(solution)/shard_map/stack | solution.py:62
  51.6 2.1 %add_bitcast_fusion = f32[1,18,6,1536]{3,2,1,0:T(8,128)S(1)} fusion(f32[18,6,1535]{2,1,0:T(8,128)S(1)} %get-tuple-element.31, f32[18,6,1]{2,1,0:T(8,128)S(1)} %get-tuple-element.33, f32[18,6,1535]{2,1,0:T(8,128)S(1)} %get-tuple-element.27, f32[18,6,1]{2,1,0:T(8,128)S(1)} %get-tuple-element.29, f32[18,6,1]{2,1,0:T(8,128)S(1)} %get-tuple-element.32, ...), kind=kLoop, calls=%fused_computation.56 | loop fusion | flops 7464960 | bytes 11280384 | tf_op jit(solution)/shard_map/stack | solution.py:62
  53.7 0.1 fusion
  53.9 0.7 copy-done.2
  54.7 0.2 pad_maximum_fusion
  54.8 0.1 subtract_multiply_fusion.1
  55.0 0.1 slice_bitcast_fusion.3
  55.2 0.3 fusion.73
  55.6 0.3 fusion.77
  56.0 0.3 fusion.75
  56.3 1.7 %multiply_add_fusion.1 = (f32[16,4,1536]{2,1,0:T(4,128)S(1)}, f32[16,4,1536]{2,1,0:T(4,128)S(1)}) fusion(f32[18,6,1536]{2,1,0:T(8,128)S(1)} %get-tuple-element.18, f32[16]{0:T(128)S(1)} %slice.342, f32[18,6,1536]{2,1,0:T(8,128)S(1)} %get-tuple-element.19, f32[16,4,1535]{2,1,0:T(4,128)S(1)} %get-tuple-element.35, f32[16,4,1]{2,1,0:T(4,128)S(1)} %get-tuple-element.37, ...), kind=kLoop, calls=%fused_computation.108 | loop fusion | flops 5210112 | bytes 3933760 | tf_op jit(solution)/shard_map/add | solution.py:62
  58.0 1.9 %multiply_add_fusion = f32[16,4,1536]{2,1,0:T(4,128)S(1)} fusion(f32[16,4,1535]{2,1,0:T(4,128)S(1)} %get-tuple-element.43, f32[16,4,1]{2,1,0:T(4,128)S(1)} %get-tuple-element.45, f32[16,4,1535]{2,1,0:T(4,128)S(1)} %get-tuple-element.39, f32[16,4,1]{2,1,0:T(4,128)S(1)} %get-tuple-element.41, f32[16,4,1]{2,1,0:T(4,128)S(1)} %get-tuple-element.44, ...), kind=kLoop, calls=%fused_computation.107 | loop fusion | flops 4423680 | bytes 6684672 | tf_op jit(solution)/shard_map/add | solution.py:62
  59.9 0.3 maximum_reduce_fusion
  60.2 0.2 fusion.52
  60.6 1.3 collective-permute-start.5
  62.0 0.7 collective-permute-start.6
  62.7 0.7 collective-permute-start.7
  63.5 0.7 collective-permute-start.8
  64.2 0.7 collective-permute-start.9
  64.8 0.7 iota_compare_fusion.4
  65.5 2.3 %collective-permute-done.5 = f32[4,128]{1,0:T(4,128)S(1)} collective-permute-done((f32[4,128]{1,0:T(4,128)S(1)}, f32[4,128]{1,0:T(4,128)S(1)}, u32[]{:S(2)}, u32[]{:S(2)}) %collective-permute-start.5) | collective-permute-done | bytes 2080 | tf_op jit(solution)/shard_map/ppermute | solution.py:135
  67.9 0.9 broadcast_select_fusion.5
  68.8 12.5 %all-to-all-start = ((f32[128,4,128]{2,1,0:T(4,128)}), f32[128,4,128]{2,1,0:T(4,128)S(1)}, u32[]{:S(2)}, u32[]{:S(2)}) async-start(f32[128,4,128]{2,1,0:T(4,128)} %broadcast_select_fusion.5), calls=%async_computation | async-start | bytes 524288 | tf_op jit(solution)/shard_map/all_to_all | solution.py:139
  81.3 0.2 pad_maximum_fusion.4
  81.5 11.9 %collective-permute-start.4 = (f32[2,16,4,1536]{3,2,1,0:T(4,128)S(1)}, f32[2,16,4,1536]{3,2,1,0:T(4,128)S(1)}, u32[]{:S(2)}, u32[]{:S(2)}) collective-permute-start(f32[2,16,4,1536]{3,2,1,0:T(4,128)S(1)} %pad_maximum_fusion.4), channel_id=1, source_target_pairs={{1,0},{2,1},{3,2},{4,3},{5,4},{7,6},{8,7},{9,8},{10,9},{11,10},{13... | collective-permute-start | bytes 2359304 | tf_op jit(solution)/shard_map/ppermute | solution.py:122
  93.4 0.1 reduce_sum.19
  93.6 0.6 pad_maximum_fusion.10
  94.2 35.7 %collective-permute-done.4 = f32[2,16,4,1536]{3,2,1,0:T(4,128)S(1)} collective-permute-done((f32[2,16,4,1536]{3,2,1,0:T(4,128)S(1)}, f32[2,16,4,1536]{3,2,1,0:T(4,128)S(1)}, u32[]{:S(2)}, u32[]{:S(2)}) %collective-permute-start.4) | collective-permute-done | bytes 786464 | tf_op jit(solution)/shard_map/ppermute | solution.py:122
  129.9 0.2 broadcast_select_fusion.4
  130.1 0.9 slice_bitcast_fusion.4
  (41 shorter events, 1.5 us)
Async XLA Ops:
  0.6 23.7 %copy-start = (f32[16,4,1536]{2,1,0:T(4,128)S(1)}, f32[16,4,1536]{2,1,0:T(4,128)}, u32[]{:S(2)}) copy-start(f32[16,4,1536]{2,1,0:T(4,128)} %param.5) | copy-start | bytes 1179652
  0.6 23.7 %copy-start.1 = (f32[16,4,1536]{2,1,0:T(4,128)S(1)}, f32[16,4,1536]{2,1,0:T(4,128)}, u32[]{:S(2)}) copy-start(f32[16,4,1536]{2,1,0:T(4,128)} %param.4) | copy-start | bytes 1179652
  1.7 14.4 %collective-permute-start.1 = (f32[2,2,4,1536]{3,2,1,0:T(4,128)S(1)}, f32[2,2,4,1536]{3,2,1,0:T(4,128)S(1)}, u32[]{:S(2)}, u32[]{:S(2)}) collective-permute-start(f32[2,2,4,1536]{3,2,1,0:T(4,128)S(1)} %bitcast.87), channel_id=1, source_target_pairs={{0,1},{1,0},{2,3},{3,2},{4,5},{5,4},{6,7},{7,6},{8,9},{9,8},{10,11... | collective-permute-start | bytes 294920 | tf_op jit(solution)/shard_map/ppermute | solution.py:68
  14.1 10.2 %collective-permute-start = (f32[2,2,4,1536]{3,2,1,0:T(4,128)S(1)}, f32[2,2,4,1536]{3,2,1,0:T(4,128)S(1)}, u32[]{:S(2)}, u32[]{:S(2)}) collective-permute-start(f32[2,2,4,1536]{3,2,1,0:T(4,128)S(1)} %get-tuple-element.13), channel_id=1, source_target_pairs={{0,5},{1,2},{2,1},{3,4},{4,3},{5,0},{6,11},{7,8},{8,7},{9,10},{10,... | collective-permute-start | bytes 294920 | tf_op jit(solution)/shard_map/ppermute | solution.py:70
  24.3 11.3 %copy-start.4 = (s32[1536]{0:T(1024)S(1)}, s32[1536]{0:T(1024)}, u32[]{:S(2)}) copy-start(s32[1536]{0:T(1024)} %param.6) | copy-start | bytes 18436
  24.9 17.6 %collective-permute-start.2 = (f32[2,18,2,1536]{3,2,1,0:T(2,128)S(1)}, f32[2,18,2,1536]{3,2,1,0:T(2,128)S(1)}, u32[]{:S(2)}, u32[]{:S(2)}) collective-permute-start(f32[2,18,2,1536]{3,2,1,0:T(2,128)S(1)} %get-tuple-element.48), channel_id=1, source_target_pairs={{0,762},{6,12},{12,6},{18,24},{24,18},{30,36},{36,30},{42,48},{48,... | collective-permute-start | bytes 1327112 | tf_op jit(solution)/shard_map/ppermute | solution.py:70
  32.3 14.7 %collective-permute-start.3 = (f32[2,18,2,1536]{3,2,1,0:T(2,128)S(1)}, f32[2,18,2,1536]{3,2,1,0:T(2,128)S(1)}, u32[]{:S(2)}, u32[]{:S(2)}) collective-permute-start(f32[2,18,2,1536]{3,2,1,0:T(2,128)S(1)} %get-tuple-element.49), channel_id=1, source_target_pairs={{0,6},{6,0},{12,18},{18,12},{24,30},{30,24},{36,42},{42,36},{48,54... | collective-permute-start | bytes 1327112 | tf_op jit(solution)/shard_map/ppermute | solution.py:68
  53.7 0.9 copy-start.2
  53.7 0.9 copy-start.3
  59.9 70.0 %copy-start.5 = (f32[2]{0:T(128)S(1)}, f32[2]{0:T(128)}, u32[]{:S(2)}) copy-start(f32[2]{0:T(128)} %constant.49.clone.1) | copy-start | bytes 28
  60.6 7.1 %collective-permute-start.5 = (f32[4,128]{1,0:T(4,128)S(1)}, f32[4,128]{1,0:T(4,128)S(1)}, u32[]{:S(2)}, u32[]{:S(2)}) collective-permute-start(f32[4,128]{1,0:T(4,128)S(1)} %pad_maximum_fusion.11), channel_id=1, source_target_pairs={{0,1},{6,7},{12,13},{18,19},{24,25},{30,31},{36,37},{42,43},{48,49... | collective-permute-start | bytes 6152 | tf_op jit(solution)/shard_map/ppermute | solution.py:135
  62.0 5.8 %collective-permute-start.6 = (f32[4,128]{1,0:T(4,128)S(1)}, f32[4,128]{1,0:T(4,128)S(1)}, u32[]{:S(2)}, u32[]{:S(2)}) collective-permute-start(f32[4,128]{1,0:T(4,128)S(1)} %pad_maximum_fusion.12), channel_id=1, source_target_pairs={{0,2},{6,8},{12,14},{18,20},{24,26},{30,32},{36,38},{42,44},{48,50... | collective-permute-start | bytes 6152 | tf_op jit(solution)/shard_map/ppermute | solution.py:135
  62.7 5.0 %collective-permute-start.7 = (f32[4,128]{1,0:T(4,128)S(1)}, f32[4,128]{1,0:T(4,128)S(1)}, u32[]{:S(2)}, u32[]{:S(2)}) collective-permute-start(f32[4,128]{1,0:T(4,128)S(1)} %pad_maximum_fusion.13), channel_id=1, source_target_pairs={{0,3},{6,9},{12,15},{18,21},{24,27},{30,33},{36,39},{42,45},{48,51... | collective-permute-start | bytes 6152 | tf_op jit(solution)/shard_map/ppermute | solution.py:135
  63.5 4.3 %collective-permute-start.8 = (f32[4,128]{1,0:T(4,128)S(1)}, f32[4,128]{1,0:T(4,128)S(1)}, u32[]{:S(2)}, u32[]{:S(2)}) collective-permute-start(f32[4,128]{1,0:T(4,128)S(1)} %pad_maximum_fusion.14), channel_id=1, source_target_pairs={{0,4},{6,10},{12,16},{18,22},{24,28},{30,34},{36,40},{42,46},{48,5... | collective-permute-start | bytes 6152 | tf_op jit(solution)/shard_map/ppermute | solution.py:135
  64.2 3.6 %collective-permute-start.9 = (f32[4,128]{1,0:T(4,128)S(1)}, f32[4,128]{1,0:T(4,128)S(1)}, u32[]{:S(2)}, u32[]{:S(2)}) collective-permute-start(f32[4,128]{1,0:T(4,128)S(1)} %pad_maximum_fusion.15), channel_id=1, source_target_pairs={{0,5},{6,11},{12,17},{18,23},{24,29},{30,35},{36,41},{42,47},{48,5... | collective-permute-start | bytes 6152 | tf_op jit(solution)/shard_map/ppermute | solution.py:135
  68.8 24.6 %all-to-all-start = ((f32[128,4,128]{2,1,0:T(4,128)}), f32[128,4,128]{2,1,0:T(4,128)S(1)}, u32[]{:S(2)}, u32[]{:S(2)}) async-start(f32[128,4,128]{2,1,0:T(4,128)} %broadcast_select_fusion.5), calls=%async_computation | async-start | bytes 524288 | tf_op jit(solution)/shard_map/all_to_all | solution.py:139
  81.5 48.4 %collective-permute-start.4 = (f32[2,16,4,1536]{3,2,1,0:T(4,128)S(1)}, f32[2,16,4,1536]{3,2,1,0:T(4,128)S(1)}, u32[]{:S(2)}, u32[]{:S(2)}) collective-permute-start(f32[2,16,4,1536]{3,2,1,0:T(4,128)S(1)} %pad_maximum_fusion.4), channel_id=1, source_target_pairs={{1,0},{2,1},{3,2},{4,3},{5,4},{7,6},{8,7},{9,8},{10,9},{11,10},{13... | collective-permute-start | bytes 2359304 | tf_op jit(solution)/shard_map/ppermute | solution.py:122

commit v3 on v1

--- a/solution.py
+++ b/solution.py
@@ -1,9 +1,11 @@
 import jax
 import jax.numpy as jnp
 from jax import lax
+from jax.sharding import Mesh
 from jax.sharding import PartitionSpec as P
 
-SHIFT = 16
+
+LAT = ("x", "y", "z")
 
 
 time_step = 0.15
@@ -88,27 +90,26 @@
     return cells.reshape(2, planes // 4, width // 4)
 
 
-def shards(phase, solute, seed_grain, writer):
-    planes, rows, width = phase.shape
+def work(phase, solute, seed_grain, writer):
+    planes, _, width = phase.shape
     grow_count = lax.axis_size("grow")
     grow_at = lax.axis_index("grow")
-    lat_count = lax.axis_size("lat")
-    lat_at = lax.axis_index("lat")
+    lat_at = lax.axis_index(LAT)
     total = planes * grow_count
     grain = seed_grain > 0
     state = jnp.stack([phase, solute])
     lowest = grow_at == 0
     highest = grow_at == grow_count - 1
 
+    left = shift(state[:, :, -2:], LAT, 1)
+    right = shift(state[:, :, :2], LAT, -1)
     below = shift(state[:, -2:], "grow", 1)
     above = shift(state[:, :2], "grow", -1)
-    left = shift(state[:, :, -2:], "lat", 1)
-    right = shift(state[:, :, :2], "lat", -1)
     below = jnp.where(lowest, fields(1.0, solid_u, below), below)
     above = jnp.where(highest, fields(-1.0, liquid_u, above), above)
     edges = jnp.concatenate([below[:, 1:], above[:, :1]], axis=1)
-    edges_left = shift(edges[:, :, -1:], "lat", 1)
-    edges_right = shift(edges[:, :, :1], "lat", -1)
+    edges_left = shift(edges[:, :, -1:], LAT, 1)
+    edges_right = shift(edges[:, :, :1], LAT, -1)
     pad = ((0, 0), (0, 0), (1, 0), (0, 0))
     dap = ((0, 0), (0, 0), (0, 1), (0, 0))
     low = ((0, 0), (1, 0), (0, 0), (0, 0))
@@ -153,27 +154,39 @@
         )
         for r in range(grow_count)
     ]
-    mine = jnp.where(lowest, blocks[0], 0.0)
-    for r in range(1, grow_count):
-        mine = mine + lax.ppermute(blocks[r], "grow", [(0, r)])
+    x_count, y_count, z_count = (lax.axis_size(axis) for axis in LAT)
+    x_at, y_at, z_at = (lax.axis_index(axis) for axis in LAT)
+    mine = jnp.stack(blocks)
+    targets = lax.dynamic_index_in_dim(writer, lat_at, 1, keepdims=False)
+    to_y = jnp.arange(y_count)[:, None] == (targets // z_count % y_count)[None]
+    slots = jnp.where(to_y[:, :, None, None], mine[None], 0.0)
+    slots = slots.reshape((y_count * grow_count,) + mine.shape[1:])
+    held = lax.all_to_all(slots, ("y", "grow"), 0, 0, tiled=True)
+    held = held.reshape((y_count, grow_count) + mine.shape[1:])[:, 0]
     row_ids = lax.dynamic_index_in_dim(writer, grow_at, 0, keepdims=False)
-    target = lax.dynamic_index_in_dim(row_ids, lat_at, 0, keepdims=False)
-    slots = jnp.where((jnp.arange(lat_count) == target)[:, None, None], mine[None], 0.0)
-    landed = lax.all_to_all(slots, "lat", 0, 0, tiled=True).sum(axis=0)
+    row_ids = row_ids.reshape(x_count, y_count, z_count)
+    onward = lax.dynamic_index_in_dim(row_ids, x_at, 0, keepdims=False)
+    onward = lax.dynamic_index_in_dim(onward, z_at, 1, keepdims=False)
+    place = onward // (y_count * z_count) * z_count + onward % z_count
+    place = jnp.where(onward // z_count % y_count == y_at, place, -1)
+    chosen = jnp.arange(x_count * z_count)[:, None] == place[None]
+    slots = jnp.where(chosen[:, :, None, None], held[None], 0.0).sum(axis=1)
+    landed = lax.all_to_all(slots, ("x", "z"), 0, 0, tiled=True).sum(axis=0)
     landed = jnp.stack([landed[:, :piece], landed[:, piece:]])
     return (moved[0], moved[1], landed[None, None, :, :, None])
 
 
 def solution(mesh):
-    placed = (P("grow", "lat", None), P("grow", "lat", None), P(), P())
+    fine = Mesh(mesh.devices.reshape(4, 8, 4, 6), LAT + ("grow",))
+    placed = (P("grow", LAT, None), P("grow", LAT, None), P(), P())
     return jax.shard_map(
-        shards,
-        mesh=mesh,
+        work,
+        mesh=fine,
         in_specs=placed,
         out_specs=(
-            P("grow", "lat", None),
-            P("grow", "lat", None),
-            P("grow", "lat", None, None, None, None),
+            P("grow", LAT, None),
+            P("grow", LAT, None),
+            P("grow", LAT, None, None, None, None),
         ),
         check_vma=False,
     )

time: 128 us -> 118 us (0.922)
  blocking collectives: 0 us -> 33.1 us
  waiting for transfers between devices: 38.7 us -> 12.9 us
  starting transfers between devices: 65.9 us -> 50.3 us
    ppermute x6 -> x1, waiting for transfers between devices: 35.7 us -> 0.01 us  [work(): lax.ppermute(state, 'grow', [(i, i - 1) for i in range(1, grow_count)])]
    all_to_all x0 -> x1, blocking collectives: none -> 33.1 us  [work(): landed = lax.all_to_all(slots, ('x', 'z'), 0, 0, tiled=True).sum(axis=0)]
    ppermute x6 -> x1, starting transfers between devices: 14.9 us -> 2.25 us  [work(): lax.ppermute(state, 'grow', [(i, i - 1) for i in range(1, grow_count)])]
    all_to_all x1, waiting for transfers between devices: 0.54 us -> 10.1 us  [work(): held = lax.all_to_all(slots, ('y', 'grow'), 0, 0, tiled=True)]
    all_to_all x1, starting transfers between devices: 11.4 us -> 8.46 us  [work(): held = lax.all_to_all(slots, ('y', 'grow'), 0, 0, tiled=True)]
  transfers between devices with their start and end apart: 13 -> 8, of which waited for: 4 -> 2; matrix products, arithmetic and copies ran while one was open for 4% -> 3% of each run, Pallas kernels for 0% -> 0%
where the time goes in v3:
time: 118 us
  starting transfers between devices  50.3 us (43%)
  blocking collectives  33.1 us (28%)
  other arithmetic  14.7 us (12%)
  waiting for transfers between devices  12.9 us (11%)
  local copies, waits for them, and re-layouts  5.39 us (5%)
    ppermute x6, starting transfers between devices, shift(): lax.ppermute(block, axis, [(i, (i + step) % count) for i in range(count)])  39.6 us
    all_to_all x1, blocking collectives, work(): landed = lax.all_to_all(slots, ('x', 'z'), 0, 0, tiled=True).sum(axis=0)  33.1 us
    all_to_all x1, waiting for transfers between devices, work(): held = lax.all_to_all(slots, ('y', 'grow'), 0, 0, tiled=True)  10.1 us
    all_to_all x1, starting transfers between devices, work(): held = lax.all_to_all(slots, ('y', 'grow'), 0, 0, tiled=True)  8.46 us
    another operation x4, other arithmetic, advance(): return jnp.stack([p + time_step * rate, u + time_step * urate])  4.55 us
    add x2, other arithmetic, advance(): return jnp.stack([p + time_step * rate, u + time_step * urate])  3.57 us
    ppermute x6, waiting for transfers between devices, shift(): lax.ppermute(block, axis, [(i, (i + step) % count) for i in range(count)])  2.81 us
  transfers between devices with their start and end apart: 8, of which 2 were waited for; matrix products, arithmetic and copies ran while one was open for 3% of the time, Pallas kernels for 0%

profile of v3, /device:TPU:1, one launch (start us, length us, event | category | flops | bytes accessed | tf_op | source)
XLA Modules:
  0.0 117.8 jit_solution(12502403638209950537)
XLA Ops:
  0.7 1.0 pad_maximum_fusion.9
  1.7 12.4 %collective-permute-start.1 = (f32[2,2,4,1536]{3,2,1,0:T(4,128)S(1)}, f32[2,2,4,1536]{3,2,1,0:T(4,128)S(1)}, u32[]{:S(2)}, u32[]{:S(2)}) collective-permute-start(f32[2,2,4,1536]{3,2,1,0:T(4,128)S(1)} %get-tuple-element.45), channel_id=1, source_target_pairs={{0,5},{1,0},{2,1},{3,2},{4,3},{5,4},{6,11},{7,6},{8,7},{9,8},{10,9... | collective-permute-start | bytes 294920 | tf_op jit(solution)/shard_map/ppermute | solution.py:71
  14.1 1.9 %collective-permute-start = (f32[2,2,4,1536]{3,2,1,0:T(4,128)S(1)}, f32[2,2,4,1536]{3,2,1,0:T(4,128)S(1)}, u32[]{:S(2)}, u32[]{:S(2)}) collective-permute-start(f32[2,2,4,1536]{3,2,1,0:T(4,128)S(1)} %get-tuple-element.44), channel_id=1, source_target_pairs={{0,1},{1,2},{2,3},{3,4},{4,5},{5,0},{6,7},{7,8},{8,9},{9,10},{10,1... | collective-permute-start | bytes 294920 | tf_op jit(solution)/shard_map/ppermute | solution.py:71
  16.0 1.8 %fusion.38 = (f32[2,16,2,1536]{3,2,1,0:T(2,128)S(1)}, f32[2,16,2,1536]{3,2,1,0:T(2,128)S(1)}) fusion(f32[1,16,4,1536]{3,2,1,0:T(4,128)} %bitcast.108, f32[1,16,4,1536]{3,2,1,0:T(4,128)} %bitcast.105), kind=kLoop, calls=%fused_computation.79 | loop fusion | flops 196608 | bytes 1572864 | tf_op jit(solution)/shard_map/stack | solution.py:100
  17.8 3.6 %collective-permute-start.4 = (f32[2,16,2,1536]{3,2,1,0:T(2,128)S(1)}, f32[2,16,2,1536]{3,2,1,0:T(2,128)S(1)}, u32[]{:S(2)}, u32[]{:S(2)}) collective-permute-start(f32[2,16,2,1536]{3,2,1,0:T(2,128)S(1)} %get-tuple-element.42), channel_id=1, source_target_pairs={{0,6},{6,12},{12,18},{18,24},{24,30},{30,36},{36,42},{42,48},{48,5... | collective-permute-start | bytes 1179656 | tf_op jit(solution)/shard_map/ppermute | solution.py:71
  21.5 10.3 %collective-permute-start.5 = (f32[2,16,2,1536]{3,2,1,0:T(2,128)S(1)}, f32[2,16,2,1536]{3,2,1,0:T(2,128)S(1)}, u32[]{:S(2)}, u32[]{:S(2)}) collective-permute-start(f32[2,16,2,1536]{3,2,1,0:T(2,128)S(1)} %get-tuple-element.43), channel_id=1, source_target_pairs={{0,762},{6,0},{12,6},{18,12},{24,18},{30,24},{36,30},{42,36},{48,4... | collective-permute-start | bytes 1179656 | tf_op jit(solution)/shard_map/ppermute | solution.py:71
  31.9 0.2 dynamic-slice_reduce_fusion
  32.1 0.1 reshape.228
  32.3 0.2 dynamic-slice_reduce_fusion.1
  32.6 1.9 %collective-permute-start.2 = (f32[2,2,1,1536]{3,2,1,0:T(1,128)S(1)}, f32[2,2,1,1536]{3,2,1,0:T(1,128)S(1)}, u32[]{:S(2)}, u32[]{:S(2)}) collective-permute-start(f32[2,2,1,1536]{3,2,1,0:T(1,128)S(1)} %get-tuple-element.46), channel_id=1, source_target_pairs={{0,6},{6,12},{12,18},{18,24},{24,30},{30,36},{36,42},{42,48},{48,5... | collective-permute-start | bytes 73736 | tf_op jit(solution)/shard_map/ppermute | solution.py:71
  34.7 0.1 eq.82
  34.8 9.4 %collective-permute-start.3 = (f32[2,2,1,1536]{3,2,1,0:T(1,128)S(1)}, f32[2,2,1,1536]{3,2,1,0:T(1,128)S(1)}, u32[]{:S(2)}, u32[]{:S(2)}) collective-permute-start(f32[2,2,1,1536]{3,2,1,0:T(1,128)S(1)} %get-tuple-element.47), channel_id=1, source_target_pairs={{0,762},{6,0},{12,6},{18,12},{24,18},{30,24},{36,30},{42,36},{48,4... | collective-permute-start | bytes 73736 | tf_op jit(solution)/shard_map/ppermute | solution.py:71
  44.2 2.8 %collective-permute-done.2 = f32[2,2,1,1536]{3,2,1,0:T(1,128)S(1)} collective-permute-done((f32[2,2,1,1536]{3,2,1,0:T(1,128)S(1)}, f32[2,2,1,1536]{3,2,1,0:T(1,128)S(1)}, u32[]{:S(2)}, u32[]{:S(2)}) %collective-permute-start.2) | collective-permute-done | bytes 24608 | tf_op jit(solution)/shard_map/ppermute | solution.py:71
  47.1 0.7 fusion
  47.8 0.1 slice_bitcast_fusion.1
  47.9 0.1 fusion.74
  48.1 0.7 fusion.73
  48.7 0.1 subtract_multiply_fusion
  48.9 0.3 fusion.75
  49.2 0.1 fusion.76
  49.3 2.1 %add_bitcast_fusion.1 = (f32[1,18,6,1536]{3,2,1,0:T(8,128)S(1)}, f32[18,6,1536]{2,1,0:T(8,128)S(1)}) fusion(f32[20,8,1536]{2,1,0:T(8,128)S(1)} %get-tuple-element.10, f32[18]{0:T(128)S(1)} %multiply_add_fusion.2, f32[20,8,1536]{2,1,0:T(8,128)S(1)} %get-tuple-element.11, f32[18,6,1535]{2,1,0:T(8,128)S(1)} %get-tuple-element.17, ...), kind=kLoop, calls=%fused_computation.66 | loop fusion | flops 8792064 | bytes 6637128 | tf_op jit(solution)/shard_map/stack | solution.py:66
  51.4 2.1 %add_bitcast_fusion = f32[1,18,6,1536]{3,2,1,0:T(8,128)S(1)} fusion(f32[18,6,1535]{2,1,0:T(8,128)S(1)} %get-tuple-element.66, f32[18,6,1]{2,1,0:T(8,128)S(1)} %get-tuple-element.68, f32[18,6,1535]{2,1,0:T(8,128)S(1)} %get-tuple-element.21, f32[18,6,1]{2,1,0:T(8,128)S(1)} %get-tuple-element.23, f32[18,6,1]{2,1,0:T(8,128)S(1)} %get-tuple-element.69, ...), kind=kLoop, calls=%fused_computation.65 | loop fusion | flops 7464960 | bytes 11280384 | tf_op jit(solution)/shard_map/stack | solution.py:66
  53.6 0.1 fusion.6
  53.7 0.7 copy-done.5
  54.5 0.2 pad_maximum_fusion
  54.7 0.1 slice_bitcast_fusion.3
  54.8 0.3 fusion.79
  55.1 0.1 fusion.80
  55.2 0.3 fusion.83
  55.5 0.1 fusion.84
  55.6 0.1 subtract_multiply_fusion.1
  55.8 0.3 fusion.81
  56.1 0.1 fusion.82
  56.2 1.7 %multiply_add_fusion.1 = (f32[16,4,1536]{2,1,0:T(4,128)S(1)}, f32[16,4,1536]{2,1,0:T(4,128)S(1)}) fusion(f32[18,6,1536]{2,1,0:T(8,128)S(1)} %get-tuple-element.12, f32[16]{0:T(128)S(1)} %slice.361, f32[18,6,1536]{2,1,0:T(8,128)S(1)} %get-tuple-element.13, f32[16,4,1535]{2,1,0:T(4,128)S(1)} %get-tuple-element.29, f32[16,4,1]{2,1,0:T(4,128)S(1)} %get-tuple-element.31, ...), kind=kLoop, calls=%fused_computation.117 | loop fusion | flops 5210112 | bytes 3933760 | tf_op jit(solution)/shard_map/add | solution.py:66
  57.8 1.9 %multiply_add_fusion = f32[16,4,1536]{2,1,0:T(4,128)S(1)} fusion(f32[16,4,1535]{2,1,0:T(4,128)S(1)} %get-tuple-element.37, f32[16,4,1]{2,1,0:T(4,128)S(1)} %get-tuple-element.39, f32[16,4,1535]{2,1,0:T(4,128)S(1)} %get-tuple-element.33, f32[16,4,1]{2,1,0:T(4,128)S(1)} %get-tuple-element.35, f32[16,4,1]{2,1,0:T(4,128)S(1)} %get-tuple-element.38, ...), kind=kLoop, calls=%fused_computation.116 | loop fusion | flops 4423680 | bytes 6684672 | tf_op jit(solution)/shard_map/add | solution.py:66
  59.7 0.3 maximum_reduce_fusion
  60.0 0.2 fusion.59
  60.2 0.1 reshape.230
  60.9 0.8 bitcast_select_fusion
  61.6 8.5 %all-to-all-start = ((f32[48,4,128]{2,1,0:T(4,128)}), f32[48,4,128]{2,1,0:T(4,128)S(1)}, u32[]{:S(2)}, u32[]{:S(2)}) async-start(f32[48,4,128]{2,1,0:T(4,128)} %bitcast_select_fusion), calls=%async_computation | async-start | bytes 196608 | tf_op jit(solution)/shard_map/all_to_all | solution.py:164
  70.1 0.2 pad_maximum_fusion.3
  70.3 2.3 %collective-permute-start.6 = (f32[2,16,4,1536]{3,2,1,0:T(4,128)S(1)}, f32[2,16,4,1536]{3,2,1,0:T(4,128)S(1)}, u32[]{:S(2)}, u32[]{:S(2)}) collective-permute-start(f32[2,16,4,1536]{3,2,1,0:T(4,128)S(1)} %pad_maximum_fusion.3), channel_id=1, source_target_pairs={{1,0},{2,1},{3,2},{4,3},{5,4},{7,6},{8,7},{9,8},{10,9},{11,10},{13... | collective-permute-start | bytes 2359304 | tf_op jit(solution)/shard_map/ppermute | solution.py:146
  72.6 10.1 %all-to-all-done = f32[48,4,128]{2,1,0:T(4,128)S(1)} async-done(((f32[48,4,128]{2,1,0:T(4,128)}), f32[48,4,128]{2,1,0:T(4,128)S(1)}, u32[]{:S(2)}, u32[]{:S(2)}) %all-to-all-start) | async-done | bytes 98336 | tf_op jit(solution)/shard_map/all_to_all | solution.py:164
  82.7 0.2 select_reduce_fusion
  82.9 33.1 %all_to_all.10 = f32[16,4,128]{2,1,0:T(4,128)S(1)} all-to-all(f32[16,4,128]{2,1,0:T(4,128)S(1)} %select_reduce_fusion), channel_id=1, replica_groups=mesh['x'=4,'y'=8,'z'=4,'grow'=6] {'x','z'}, dimensions={0} | all-to-all | bytes 65536 | tf_op jit(solution)/shard_map/all_to_all | solution.py:174
  116.1 0.6 pad_maximum_fusion.12
  116.7 0.2 broadcast_select_fusion
  116.9 0.9 slice_bitcast_fusion.4
  (55 shorter events, 1.2 us)
Async XLA Ops:
  0.6 31.3 %copy-start = (s32[6,128]{1,0:T(8,128)S(1)}, s32[6,128]{1,0:T(8,128)}, u32[]{:S(2)}) copy-start(s32[6,128]{1,0:T(8,128)} %param.7) | copy-start | bytes 9220
  0.6 31.8 %copy-start.4 = (f32[2,2,4,1536]{3,2,1,0:T(4,128)S(1)}, f32[2,2,4,1536]{3,2,1,0:T(4,128)}, u32[]{:S(2)}) copy-start(f32[2,2,4,1536]{3,2,1,0:T(4,128)} %constant.164.clone.1) | copy-start | bytes 294916
  0.7 31.9 %copy-start.3 = (f32[2,2,4,1536]{3,2,1,0:T(4,128)S(1)}, f32[2,2,4,1536]{3,2,1,0:T(4,128)}, u32[]{:S(2)}) copy-start(f32[2,2,4,1536]{3,2,1,0:T(4,128)} %constant.163.clone.1) | copy-start | bytes 294916
  0.7 46.4 %copy-start.2 = (f32[16,4,1536]{2,1,0:T(4,128)S(1)}, f32[16,4,1536]{2,1,0:T(4,128)}, u32[]{:S(2)}) copy-start(f32[16,4,1536]{2,1,0:T(4,128)} %param.4) | copy-start | bytes 1179652
  0.7 46.4 %copy-start.1 = (f32[16,4,1536]{2,1,0:T(4,128)S(1)}, f32[16,4,1536]{2,1,0:T(4,128)}, u32[]{:S(2)}) copy-start(f32[16,4,1536]{2,1,0:T(4,128)} %param.5) | copy-start | bytes 1179652
  0.7 31.2 %copy-start.7 = (s32[1536]{0:T(1024)S(1)}, s32[1536]{0:T(1024)}, u32[]{:S(2)}) copy-start(s32[1536]{0:T(1024)} %param.6) | copy-start | bytes 18436
  1.7 30.8 %collective-permute-start.1 = (f32[2,2,4,1536]{3,2,1,0:T(4,128)S(1)}, f32[2,2,4,1536]{3,2,1,0:T(4,128)S(1)}, u32[]{:S(2)}, u32[]{:S(2)}) collective-permute-start(f32[2,2,4,1536]{3,2,1,0:T(4,128)S(1)} %get-tuple-element.45), channel_id=1, source_target_pairs={{0,5},{1,0},{2,1},{3,2},{4,3},{5,4},{6,11},{7,6},{8,7},{9,8},{10,9... | collective-permute-start | bytes 294920 | tf_op jit(solution)/shard_map/ppermute | solution.py:71
  14.1 18.4 %collective-permute-start = (f32[2,2,4,1536]{3,2,1,0:T(4,128)S(1)}, f32[2,2,4,1536]{3,2,1,0:T(4,128)S(1)}, u32[]{:S(2)}, u32[]{:S(2)}) collective-permute-start(f32[2,2,4,1536]{3,2,1,0:T(4,128)S(1)} %get-tuple-element.44), channel_id=1, source_target_pairs={{0,1},{1,2},{2,3},{3,4},{4,5},{5,0},{6,7},{7,8},{8,9},{9,10},{10,1... | collective-permute-start | bytes 294920 | tf_op jit(solution)/shard_map/ppermute | solution.py:71
  17.8 29.2 %collective-permute-start.4 = (f32[2,16,2,1536]{3,2,1,0:T(2,128)S(1)}, f32[2,16,2,1536]{3,2,1,0:T(2,128)S(1)}, u32[]{:S(2)}, u32[]{:S(2)}) collective-permute-start(f32[2,16,2,1536]{3,2,1,0:T(2,128)S(1)} %get-tuple-element.42), channel_id=1, source_target_pairs={{0,6},{6,12},{12,18},{18,24},{24,30},{30,36},{36,42},{42,48},{48,5... | collective-permute-start | bytes 1179656 | tf_op jit(solution)/shard_map/ppermute | solution.py:71
  21.5 25.6 %collective-permute-start.5 = (f32[2,16,2,1536]{3,2,1,0:T(2,128)S(1)}, f32[2,16,2,1536]{3,2,1,0:T(2,128)S(1)}, u32[]{:S(2)}, u32[]{:S(2)}) collective-permute-start(f32[2,16,2,1536]{3,2,1,0:T(2,128)S(1)} %get-tuple-element.43), channel_id=1, source_target_pairs={{0,762},{6,0},{12,6},{18,12},{24,18},{30,24},{36,30},{42,36},{48,4... | collective-permute-start | bytes 1179656 | tf_op jit(solution)/shard_map/ppermute | solution.py:71
  32.6 14.4 %collective-permute-start.2 = (f32[2,2,1,1536]{3,2,1,0:T(1,128)S(1)}, f32[2,2,1,1536]{3,2,1,0:T(1,128)S(1)}, u32[]{:S(2)}, u32[]{:S(2)}) collective-permute-start(f32[2,2,1,1536]{3,2,1,0:T(1,128)S(1)} %get-tuple-element.46), channel_id=1, source_target_pairs={{0,6},{6,12},{12,18},{18,24},{24,30},{30,36},{36,42},{42,48},{48,5... | collective-permute-start | bytes 73736 | tf_op jit(solution)/shard_map/ppermute | solution.py:71
  34.8 12.2 %collective-permute-start.3 = (f32[2,2,1,1536]{3,2,1,0:T(1,128)S(1)}, f32[2,2,1,1536]{3,2,1,0:T(1,128)S(1)}, u32[]{:S(2)}, u32[]{:S(2)}) collective-permute-start(f32[2,2,1,1536]{3,2,1,0:T(1,128)S(1)} %get-tuple-element.47), channel_id=1, source_target_pairs={{0,762},{6,0},{12,6},{18,12},{24,18},{30,24},{36,30},{42,36},{48,4... | collective-permute-start | bytes 73736 | tf_op jit(solution)/shard_map/ppermute | solution.py:71
  53.6 0.9 copy-start.5
  53.6 0.9 copy-start.6
  59.7 57.0 %copy-start.8 = (f32[2]{0:T(128)S(1)}, f32[2]{0:T(128)}, u32[]{:S(2)}) copy-start(f32[2]{0:T(128)} %constant.160.clone.1) | copy-start | bytes 28
  61.6 21.1 %all-to-all-start = ((f32[48,4,128]{2,1,0:T(4,128)}), f32[48,4,128]{2,1,0:T(4,128)S(1)}, u32[]{:S(2)}, u32[]{:S(2)}) async-start(f32[48,4,128]{2,1,0:T(4,128)} %bitcast_select_fusion), calls=%async_computation | async-start | bytes 196608 | tf_op jit(solution)/shard_map/all_to_all | solution.py:164
  70.3 46.4 %collective-permute-start.6 = (f32[2,16,4,1536]{3,2,1,0:T(4,128)S(1)}, f32[2,16,4,1536]{3,2,1,0:T(4,128)S(1)}, u32[]{:S(2)}, u32[]{:S(2)}) collective-permute-start(f32[2,16,4,1536]{3,2,1,0:T(4,128)S(1)} %pad_maximum_fusion.3), channel_id=1, source_target_pairs={{1,0},{2,1},{3,2},{4,3},{5,4},{7,6},{8,7},{9,8},{10,9},{11,10},{13... | collective-permute-start | bytes 2359304 | tf_op jit(solution)/shard_map/ppermute | solution.py:146

commit v4 on v3

v4 whole, which is shorter than its diff:
```python
import jax
import jax.numpy as jnp
from jax import lax
from jax.experimental import pallas as pl
from jax.experimental.pallas import tpu as pltpu
from jax.sharding import Mesh
from jax.sharding import PartitionSpec as P


LAT = ("x", "y", "z")
GRID = (4, 8, 4, 6)
LANES = 128

time_step = 0.15
aniso_strength = 0.15
coupling = 3.0
partition = 0.15
solid_u = -0.5
liquid_u = 0.0


def shift(block, axis, step):
    count = lax.axis_size(axis)
    return lax.ppermute(block, axis, [(i, (i + step) % count) for i in range(count)])


def clipped(p):
    return jnp.minimum(jnp.maximum(p, -1.0), 1.0)


def cell_step(p, u, near_p, near_u, theta, even_w, cross_w):
    pzp, pzm, pxp, pxm, pyp, pym = near_p
    gz = pzp - pzm
    gx = pxp - pxm
    gy = pyp - pym
    sz = gz * gz
    sx = gx * gx
    sy = gy * gy
    flat = sx + sy
    quartic = even_w * (flat * flat) + cross_w * (sx * sy) + sz * sz
    floored = jnp.maximum(flat + sz, 1.0)
    square = floored * floored
    base = 1.0 - 3.0 * aniso_strength
    ratio = square * pl.reciprocal(base * square + (4.0 * aniso_strength) * quartic, approx=False)
    laplace = ((pzp + pzm) + (pxp + pxm)) + ((pyp + pym) - 6.0 * p)
    hump = 1.0 - p * p
    drive = p * hump - (coupling * (u + theta)) * (hump * hump)
    rate = laplace + drive * (ratio * ratio)
    c = clipped(p)
    two = 2.0 - c
    flux = None
    for pn, un in zip(near_p, near_u, strict=True):
        face = (two - clipped(pn)) * (un - u)
        flux = face if flux is None else flux + face
    weight = (1.0 + partition) - (1.0 - partition) * c
    urate = (0.5 * flux + (1.0 + (1.0 - partition) * u) * rate) * pl.reciprocal(weight, approx=False)
    return p + time_step * rate, u + time_step * urate


def steps_kernel(
    at, phase, solute, left, right, below, above, edge_l, edge_r, weights, phase_to, solute_to, coarse_to,
    op, ou, dp, du, opr, our, dpr, dur, sp, su, spr, sur, tpr, tur, sums,
):
    planes, rows, width = phase.shape
    pairs = planes // 2
    last = pairs + 1
    chunks = width // LANES
    grow_at = at[0]
    lowest = grow_at == 0
    highest = grow_at == at[1] - 1
    tile = (2 * rows, LANES)
    sub = lax.broadcasted_iota(jnp.int32, tile, 0)
    lane = lax.broadcasted_iota(jnp.int32, tile, 1)
    early = sub < rows
    first_x = (sub & (rows - 1)) == 0
    last_x = (sub & (rows - 1)) == rows - 1
    first_y = lane == 0
    last_y = lane == LANES - 1
    total = (at[1] * planes).astype(jnp.float32)

    for field, (o, d, solid, liquid) in enumerate(((op, dp, 1.0, -1.0), (ou, du, solid_u, liquid_u))):
        o[0, 0:rows] = jnp.where(lowest, solid, below[field, 0])
        o[0, rows:] = jnp.where(lowest, solid, below[field, 1])
        o[last, 0:rows] = jnp.where(highest, liquid, above[field, 0])
        o[last, rows:] = jnp.where(highest, liquid, above[field, 1])
        d[0] = jnp.zeros((2 * rows, width), jnp.float32)
        d[last] = jnp.zeros((2 * rows, width), jnp.float32)
        d[0, rows : rows + 1] = jnp.where(lowest, solid, edge_r[field, 0])
        d[0, 2 * rows - 1 :] = jnp.where(lowest, solid, edge_l[field, 0])
        d[last, 0:1] = jnp.where(highest, liquid, edge_r[field, 1])
        d[last, rows - 1 : rows] = jnp.where(highest, liquid, edge_l[field, 1])

    def gather(k, carry):
        for field, (own, o, d) in enumerate(((phase, op, dp), (solute, ou, du))):
            o[k + 1, 0:rows] = own[2 * k]
            o[k + 1, rows:] = own[2 * k + 1]
            d[k + 1, 0:2] = right[field, 2 * k]
            d[k + 1, 2:4] = left[field, 2 * k]
            d[k + 1, 4:6] = right[field, 2 * k + 1]
            d[k + 1, 6:8] = left[field, 2 * k + 1]
        return carry

    lax.fori_loop(0, pairs, gather, 0)

    def turn(t, carry):
        for one, turned in ((op, opr), (ou, our), (dp, dpr), (du, dur)):
            for c in range(chunks):
                at_c = pl.ds(c * LANES, LANES)
                turned[t, :, at_c] = pltpu.roll(one[t, :, at_c], rows, 0)
        return carry

    lax.fori_loop(0, last + 1, turn, 0)

    def neighbours(one, turned, other, t, t_low, t_high, c):
        here = pl.ds(c * LANES, LANES)
        mid = one[t, :, here]
        ahead = one[t, :, pl.ds((c + 1) % chunks * LANES, LANES)]
        behind = one[t, :, pl.ds((c - 1) % chunks * LANES, LANES)]
        swapped = turned[t, :, here]
        beside = other[t, :, here]
        return mid, (
            jnp.where(early, swapped, turned[t_high, :, here]),
            jnp.where(early, turned[t_low, :, here], swapped),
            pltpu.roll(jnp.where(first_x, beside, mid), 2 * rows - 1, 0),
            pltpu.roll(jnp.where(last_x, beside, mid), 1, 0),
            pltpu.roll(jnp.where(first_y, ahead, mid), LANES - 1, 1),
            pltpu.roll(jnp.where(last_y, behind, mid), 1, 1),
        )

    def theta_of(t):
        level = (grow_at * planes + 2 * (t - 1) + jnp.where(early, 0, 1)).astype(jnp.float32)
        return (level + 0.5) / total - 0.5

    def tile_step(fields_p, fields_u, t, t_low, t_high, theta, c):
        p, near_p = neighbours(*fields_p, t, t_low, t_high, c)
        u, near_u = neighbours(*fields_u, t, t_low, t_high, c)
        here = pl.ds(c * LANES, LANES)
        return cell_step(p, u, near_p, near_u, theta, weights[0, :, here], weights[1, :, here])

    def own_once(t, carry):
        theta = theta_of(t)
        t_low = jnp.maximum(t - 1, 0)
        t_high = jnp.minimum(t + 1, last)
        solid = jnp.logical_and(lowest, t == 0)
        liquid = jnp.logical_and(highest, t == last)
        for c in range(chunks):
            here = pl.ds(c * LANES, LANES)
            p, u = tile_step((op, opr, dpr), (ou, our, dur), t, t_low, t_high, theta, c)
            p = jnp.where(solid, 1.0, jnp.where(liquid, -1.0, p))
            u = jnp.where(solid, solid_u, jnp.where(liquid, liquid_u, u))
            sp[t, :, here] = p
            su[t, :, here] = u
            spr[t, :, here] = pltpu.roll(p, rows, 0)
            sur[t, :, here] = pltpu.roll(u, rows, 0)
        return carry

    lax.fori_loop(0, last + 1, own_once, 0)

    def side_once(t, carry):
        theta = theta_of(t)
        for c in range(chunks):
            here = pl.ds(c * LANES, LANES)
            p, u = tile_step((dp, dpr, opr), (du, dur, our), t, t - 1, t + 1, theta, c)
            tpr[t, :, here] = pltpu.roll(p, rows, 0)
            tur[t, :, here] = pltpu.roll(u, rows, 0)
        return carry

    lax.fori_loop(1, last, side_once, 0)

    def own_twice(k, carry):
        t = k + 1
        theta = theta_of(t)
        for c in range(chunks):
            here = pl.ds(c * LANES, LANES)
            p, u = tile_step((sp, spr, tpr), (su, sur, tur), t, t - 1, t + 1, theta, c)
            sums[0, k, c : c + 1] = jnp.sum(p, axis=0, keepdims=True)
            sums[1, k, c : c + 1] = jnp.sum(u, axis=0, keepdims=True)
            p = jnp.where(lowest, -1.0, p)
            u = jnp.where(lowest, liquid_u, u)
            phase_to[2 * k, :, here] = p[:rows]
            phase_to[2 * k + 1, :, here] = p[rows:]
            solute_to[2 * k, :, here] = u[:rows]
            solute_to[2 * k + 1, :, here] = u[rows:]
        return carry

    lax.fori_loop(0, pairs, own_twice, 0)

    pieces = coarse_to.shape[0]
    per = chunks // pieces
    span = per * LANES
    pick = (
        lax.broadcasted_iota(jnp.int32, (LANES, LANES), 0) // 4
        - lax.broadcasted_iota(jnp.int32, (LANES, LANES), 1)
    )
    wide = LANES // 4
    total_cells = None
    for field in range(2):
        for h in range(per):
            start = field * (span // 4) + h * wide
            take = jnp.where(pick == -start, 1.0 / 64.0, 0.0).astype(jnp.float32)
            lines = []
            for r in range(pieces):
                for q in range(pairs // 2):
                    c = r * per + h
                    lines.append(sums[field, 2 * q, c : c + 1] + sums[field, 2 * q + 1, c : c + 1])
            got = jnp.dot(
                jnp.concatenate(lines, axis=0),
                take,
                precision=lax.Precision.HIGHEST,
                preferred_element_type=jnp.float32,
            )
            total_cells = got if total_cells is None else total_cells + got
    for r in range(pieces):
        coarse_to[r] = total_cells[r * (pairs // 2) : (r + 1) * (pairs // 2)]


def two_steps(at, phase, solute, left, right, below, above, edge_l, edge_r, weights, pieces, interpret=False):
    planes, rows, width = phase.shape
    pairs = planes // 2
    vmem = pl.BlockSpec(memory_space=pltpu.VMEM)
    scratch = pltpu.VMEM((pairs + 2, 2 * rows, width), jnp.float32)
    return pl.pallas_call(
        steps_kernel,
        out_shape=(
            jax.ShapeDtypeStruct(phase.shape, jnp.float32),
            jax.ShapeDtypeStruct(phase.shape, jnp.float32),
            jax.ShapeDtypeStruct((pieces, pairs // 2, LANES), jnp.float32),
        ),
        in_specs=[pl.BlockSpec(memory_space=pltpu.SMEM)] + [vmem] * 9,
        out_specs=(vmem, vmem, vmem),
        scratch_shapes=[scratch] * 14 + [pltpu.VMEM((2, pairs, width // LANES, LANES), jnp.float32)],
        interpret=interpret,
    )(at, phase, solute, left, right, below, above, edge_l, edge_r, weights)


def work(phase, solute, seed_grain, writer):
    _, rows, width = phase.shape
    grow_count = lax.axis_size("grow")
    grow_at = lax.axis_index("grow")
    lat_at = lax.axis_index(LAT)
    x_count, y_count, z_count = (lax.axis_size(axis) for axis in LAT)
    x_at, y_at, z_at = (lax.axis_index(axis) for axis in LAT)
    state = jnp.stack([phase, solute])

    below = shift(state[:, -2:], "grow", 1)
    above = shift(state[:, :2], "grow", -1)
    left = shift(state[:, :, -2:], LAT, 1)
    right = shift(state[:, :, :2], LAT, -1)
    edges = jnp.concatenate([below[:, 1:], above[:, :1]], axis=1)
    edge_l = shift(edges[:, :, -1:], LAT, 1)
    edge_r = shift(edges[:, :, :1], LAT, -1)

    turned = seed_grain > 0
    weights = jnp.stack([jnp.where(turned, 0.5, 1.0), jnp.where(turned, 2.0, -2.0)]).astype(jnp.float32)
    weights = jnp.broadcast_to(weights[:, None], (2, 2 * rows, width))
    at = jnp.stack([grow_at, jnp.int32(grow_count)]).astype(jnp.int32)
    phase_to, solute_to, blocks = two_steps(
        at, phase, solute, left, right, below, above, edge_l, edge_r, weights, grow_count
    )
    phase_out = shift(phase_to, "grow", -1)
    solute_out = shift(solute_to, "grow", -1)

    mine = jnp.where(grow_at == 0, blocks[0], 0.0)
    for r in range(1, grow_count):
        mine = mine + lax.ppermute(blocks[r], "grow", [(0, r)])
    row_ids = lax.dynamic_index_in_dim(writer, grow_at, 0, keepdims=False)
    target = lax.dynamic_index_in_dim(row_ids, lat_at, 0, keepdims=False)
    to_y = jnp.arange(y_count) == target // z_count % y_count
    slots = jnp.where(to_y[:, None, None], mine[None], 0.0)
    held = lax.all_to_all(slots, "y", 0, 0, tiled=True)
    row_ids = row_ids.reshape(x_count, y_count, z_count)
    onward = lax.dynamic_index_in_dim(row_ids, x_at, 0, keepdims=False)
    onward = lax.dynamic_index_in_dim(onward, z_at, 1, keepdims=False)
    place = onward // (y_count * z_count) * z_count + onward % z_count
    place = jnp.where(onward // z_count % y_count == y_at, place, -1)
    chosen = jnp.arange(x_count * z_count)[:, None] == place[None]
    slots = jnp.where(chosen[:, :, None, None], held[None], 0.0).sum(axis=1)
    landed = lax.all_to_all(slots, ("x", "z"), 0, 0, tiled=True).sum(axis=0)
    piece = width // 4 // grow_count
    landed = jnp.stack([landed[:, :piece], landed[:, piece:]])
    return (phase_out, solute_out, landed[None, None, :, :, None])


def solution(mesh):
    fine = Mesh(mesh.devices.reshape(GRID), LAT + ("grow",))
    placed = (P("grow", LAT, None), P("grow", LAT, None), P(), P())
    return jax.shard_map(
        work,
        mesh=fine,
        in_specs=placed,
        out_specs=(
            P("grow", LAT, None),
            P("grow", LAT, None),
            P("grow", LAT, None, None, None, None),
        ),
        check_vma=False,
    )
```

time: 118 us -> 139 us (1.18)
  the two profiles are of different devices: /device:TPU:1 before, /device:TPU:65 now
where the time goes in v4:
time: 139 us; the launch traced here: 138 us
  waiting for transfers between devices  63.8 us (46%)
  starting transfers between devices  50.2 us (36%)
  Pallas kernels  7.95 us (6%)
  local copies, waits for them, and re-layouts  7.58 us (5%)
  other arithmetic  5.32 us (4%)
  between operations  3.62 us (3%)
    ppermute x8, waiting for transfers between devices, shift(): lax.ppermute(block, axis, [(i, (i + step) % count) for i in range(count)])  51.3 us
    ppermute x8, starting transfers between devices, shift(): lax.ppermute(block, axis, [(i, (i + step) % count) for i in range(count)])  31.6 us
    all_to_all x1, starting transfers between devices, work(): landed = lax.all_to_all(slots, ('x', 'z'), 0, 0, tiled=True).sum(axis=0)  8.36 us
    pallas_call x1, Pallas kernels, two_steps(): pl.pallas_call(steps_kernel, out_shape=(jax.ShapeDtypeStruct(phase.shape,...  7.95 us
    all_to_all x1, waiting for transfers between devices, work(): held = lax.all_to_all(slots, 'y', 0, 0, tiled=True)  6.62 us
    all_to_all x1, starting transfers between devices, work(): held = lax.all_to_all(slots, 'y', 0, 0, tiled=True)  6.33 us
    ppermute x5, waiting for transfers between devices, work(): mine = mine + lax.ppermute(blocks[r], 'grow', [(0, r)])  5.9 us
    ppermute x5, starting transfers between devices, work(): mine = mine + lax.ppermute(blocks[r], 'grow', [(0, r)])  3.93 us
  transfers between devices with their start and end apart: 15, of which 5 were waited for; matrix products, arithmetic and copies ran while one was open for 3% of the time, Pallas kernels for 0%

profile of v4, /device:TPU:65, one launch (start us, length us, event | category | flops | bytes accessed | tf_op | source)
XLA Modules:
  0.0 138.5 jit_solution(4785193379783448762)
XLA Ops:
  0.6 0.0 copy-start
  0.6 0.0 copy-start.1
  0.7 1.8 %fusion.1 = (f32[2,16,2,1536]{3,2,1,0:T(2,128)S(1)}, f32[2,16,2,1536]{3,2,1,0:T(2,128)S(1)}) fusion(f32[1,16,4,1536]{3,2,1,0:T(4,128)} %bitcast.31, f32[1,16,4,1536]{3,2,1,0:T(4,128)} %bitcast.33), kind=kLoop, calls=%fused_computation.7 | loop fusion | flops 196608 | bytes 1572864 | tf_op jit(solution)/shard_map/stack | solution.py:243
  2.5 4.0 %collective-permute-start = (f32[2,16,2,1536]{3,2,1,0:T(2,128)S(1)}, f32[2,16,2,1536]{3,2,1,0:T(2,128)S(1)}, u32[]{:S(2)}, u32[]{:S(2)}) collective-permute-start(f32[2,16,2,1536]{3,2,1,0:T(2,128)S(1)} %get-tuple-element.20), channel_id=1, source_target_pairs={{0,6},{6,12},{12,18},{18,24},{24,30},{30,36},{36,42},{42,48},{48,5... | collective-permute-start | bytes 1179656 | tf_op jit(solution)/shard_map/ppermute | solution.py:24
  6.5 1.9 %collective-permute-start.1 = (f32[2,16,2,1536]{3,2,1,0:T(2,128)S(1)}, f32[2,16,2,1536]{3,2,1,0:T(2,128)S(1)}, u32[]{:S(2)}, u32[]{:S(2)}) collective-permute-start(f32[2,16,2,1536]{3,2,1,0:T(2,128)S(1)} %get-tuple-element.19), channel_id=1, source_target_pairs={{0,762},{6,0},{12,6},{18,12},{24,18},{30,24},{36,30},{42,36},{48,4... | collective-permute-start | bytes 1179656 | tf_op jit(solution)/shard_map/ppermute | solution.py:24
  8.5 11.5 %collective-permute-start.2 = (f32[2,2,4,1536]{3,2,1,0:T(4,128)S(1)}, f32[2,2,4,1536]{3,2,1,0:T(4,128)S(1)}, u32[]{:S(2)}, u32[]{:S(2)}) collective-permute-start(f32[2,2,4,1536]{3,2,1,0:T(4,128)S(1)} %get-tuple-element.18), channel_id=1, source_target_pairs={{0,1},{1,2},{2,3},{3,4},{4,5},{5,0},{6,7},{7,8},{8,9},{9,10},{10,1... | collective-permute-start | bytes 294920 | tf_op jit(solution)/shard_map/ppermute | solution.py:24
  20.0 1.9 %collective-permute-start.3 = (f32[2,2,4,1536]{3,2,1,0:T(4,128)S(1)}, f32[2,2,4,1536]{3,2,1,0:T(4,128)S(1)}, u32[]{:S(2)}, u32[]{:S(2)}) collective-permute-start(f32[2,2,4,1536]{3,2,1,0:T(4,128)S(1)} %get-tuple-element.17), channel_id=1, source_target_pairs={{0,5},{1,0},{2,1},{3,2},{4,3},{5,4},{6,11},{7,6},{8,7},{9,8},{10,9... | collective-permute-start | bytes 294920 | tf_op jit(solution)/shard_map/ppermute | solution.py:24
  21.9 0.0 copy-start.8
  21.9 0.7 copy-done.8
  22.7 0.7 dynamic-slice_reduce_fusion.1
  23.4 0.1 reshape.116
  23.5 0.2 dynamic-slice_reduce_fusion
  23.7 13.8 %collective-permute-done.3.above = f32[2,2,4,1536]{3,2,1,0:T(4,128)S(1)} collective-permute-done((f32[2,2,4,1536]{3,2,1,0:T(4,128)S(1)}, f32[2,2,4,1536]{3,2,1,0:T(4,128)S(1)}, u32[]{:S(2)}, u32[]{:S(2)}) %collective-permute-start.3) | collective-permute-done | bytes 98336 | tf_op jit(solution)/shard_map/ppermute | solution.py:24
  37.5 0.6 copy-done.5
  38.1 0.0 collective-permute-done.2.below
  38.2 0.8 slice-done
  39.0 1.9 %collective-permute-start.4 = (f32[2,2,1,1536]{3,2,1,0:T(1,128)S(1)}, f32[2,2,1,1536]{3,2,1,0:T(1,128)S(1)}, u32[]{:S(2)}, u32[]{:S(2)}) collective-permute-start(f32[2,2,1,1536]{3,2,1,0:T(1,128)S(1)} %get-tuple-element.22), channel_id=1, source_target_pairs={{0,6},{6,12},{12,18},{18,24},{24,30},{30,36},{36,42},{42,48},{48,5... | collective-permute-start | bytes 73736 | tf_op jit(solution)/shard_map/ppermute | solution.py:24
  40.9 4.3 %collective-permute-start.5 = (f32[2,2,1,1536]{3,2,1,0:T(1,128)S(1)}, f32[2,2,1,1536]{3,2,1,0:T(1,128)S(1)}, u32[]{:S(2)}, u32[]{:S(2)}) collective-permute-start(f32[2,2,1,1536]{3,2,1,0:T(1,128)S(1)} %get-tuple-element.21), channel_id=1, source_target_pairs={{0,762},{6,0},{12,6},{18,12},{24,18},{30,24},{36,30},{42,36},{48,4... | collective-permute-start | bytes 73736 | tf_op jit(solution)/shard_map/ppermute | solution.py:24
  45.3 0.6 pad_add_fusion.at
  45.9 1.3 dynamic_slice.16
  49.8 0.0 collective-permute-done.4.edge_l
  49.8 0.0 copy-start.2
  49.8 0.0 copy-start.3
  49.9 0.7 broadcast_in_dim.79.weights
  50.6 0.0 copy-done.2
  50.6 0.1 copy-done.3
  50.7 7.9 %shard_map.67 = (f32[16,4,1536]{2,1,0:T(4,128)}, f32[16,4,1536]{2,1,0:T(4,128)}, f32[6,4,128]{2,1,0:T(4,128)}) custom-call(s32[2]{0:T(128)} %pad_add_fusion.at, f32[16,4,1536]{2,1,0:T(4,128)} %phase.1, f32[16,4,1536]{2,1,0:T(4,128)} %solute.1, f32[2,16,2,1536]{3,2,1,0:T(2,128)} %copy-done.2, f32[2,16,2,1536]{3,2,1,0:T(2,128)} %copy-done.3, ...), custom_call_target="tpu_custom_call" | custom-call | tf_op jit(solution)/shard_map/pallas_call | solution.py:222
  58.7 0.7 slice_bitcast_fusion.6
  59.4 0.6 collective-permute-start.12
  60.0 0.7 collective-permute-start.11
  60.7 0.7 collective-permute-start.10
  61.4 0.7 collective-permute-start.9
  62.0 1.3 collective-permute-start.8
  63.4 5.9 %collective-permute-done.8 = f32[4,128]{1,0:T(4,128)S(1)} collective-permute-done((f32[4,128]{1,0:T(4,128)S(1)}, f32[4,128]{1,0:T(4,128)S(1)}, u32[]{:S(2)}, u32[]{:S(2)}) %collective-permute-start.8) | collective-permute-done | bytes 2080 | tf_op jit(solution)/shard_map/ppermute | solution.py:265
  69.3 0.7 fusion.6
  70.0 0.7 broadcast_select_fusion
  70.6 6.3 %all-to-all-start = ((f32[8,4,128]{2,1,0:T(4,128)}), f32[8,4,128]{2,1,0:T(4,128)S(1)}, u32[]{:S(2)}, u32[]{:S(2)}) async-start(f32[8,4,128]{2,1,0:T(4,128)} %broadcast_select_fusion), calls=%async_computation | async-start | bytes 32768 | tf_op jit(solution)/shard_map/all_to_all | solution.py:270
  77.0 6.6 %all-to-all-done = f32[8,4,128]{2,1,0:T(4,128)S(1)} async-done(((f32[8,4,128]{2,1,0:T(4,128)}), f32[8,4,128]{2,1,0:T(4,128)S(1)}, u32[]{:S(2)}, u32[]{:S(2)}) %all-to-all-start) | async-done | bytes 16416 | tf_op jit(solution)/shard_map/all_to_all | solution.py:270
  83.6 0.8 select_reduce_fusion
  84.4 8.4 %all-to-all-start.1 = ((f32[16,4,128]{2,1,0:T(4,128)}), f32[16,4,128]{2,1,0:T(4,128)S(1)}, u32[]{:S(2)}, u32[]{:S(2)}) async-start(f32[16,4,128]{2,1,0:T(4,128)} %select_reduce_fusion), calls=%async_computation.1 | async-start | bytes 65536 | tf_op jit(solution)/shard_map/all_to_all | solution.py:278
  92.7 4.1 %collective-permute-start.6 = (f32[16,4,1536]{2,1,0:T(4,128)}, f32[16,4,1536]{2,1,0:T(4,128)S(1)}, u32[]{:S(2)}, u32[]{:S(2)}) collective-permute-start(f32[16,4,1536]{2,1,0:T(4,128)} %get-tuple-element.6), channel_id=1, source_target_pairs={{0,5},{1,0},{2,1},{3,2},{4,3},{5,4},{6,11},{7,6},{8,7},{9,8},{10,9... | collective-permute-start | bytes 1179656 | tf_op jit(solution)/shard_map/ppermute | solution.py:24
  96.8 1.9 %collective-permute-start.7 = (f32[16,4,1536]{2,1,0:T(4,128)}, f32[16,4,1536]{2,1,0:T(4,128)S(1)}, u32[]{:S(2)}, u32[]{:S(2)}) collective-permute-start(f32[16,4,1536]{2,1,0:T(4,128)} %get-tuple-element.7), channel_id=1, source_target_pairs={{0,5},{1,0},{2,1},{3,2},{4,3},{5,4},{6,11},{7,6},{8,7},{9,8},{10,9... | collective-permute-start | bytes 1179656 | tf_op jit(solution)/shard_map/ppermute | solution.py:24
  98.8 0.1 slice_bitcast_fusion.1
  98.8 0.6 pad_maximum_fusion.4
  99.4 29.4 %collective-permute-done.6 = f32[16,4,1536]{2,1,0:T(4,128)S(1)} collective-permute-done((f32[16,4,1536]{2,1,0:T(4,128)}, f32[16,4,1536]{2,1,0:T(4,128)S(1)}, u32[]{:S(2)}, u32[]{:S(2)}) %collective-permute-start.6) | collective-permute-done | bytes 393248 | tf_op jit(solution)/shard_map/ppermute | solution.py:24
  128.8 8.2 %collective-permute-done.7 = f32[16,4,1536]{2,1,0:T(4,128)S(1)} collective-permute-done((f32[16,4,1536]{2,1,0:T(4,128)}, f32[16,4,1536]{2,1,0:T(4,128)S(1)}, u32[]{:S(2)}, u32[]{:S(2)}) %collective-permute-start.7) | collective-permute-done | bytes 393248 | tf_op jit(solution)/shard_map/ppermute | solution.py:24
  137.0 0.7 copy.17
  137.7 0.7 copy.18
  (31 shorter events, 0.2 us)
Async XLA Ops:
  0.6 7.8 %copy-start = (f32[16,4,1536]{2,1,0:T(4,128)S(1)}, f32[16,4,1536]{2,1,0:T(4,128)}, u32[]{:S(2)}) copy-start(f32[16,4,1536]{2,1,0:T(4,128)} %phase.1) | copy-start | bytes 1179652
  0.6 7.8 %copy-start.1 = (f32[16,4,1536]{2,1,0:T(4,128)S(1)}, f32[16,4,1536]{2,1,0:T(4,128)}, u32[]{:S(2)}) copy-start(f32[16,4,1536]{2,1,0:T(4,128)} %solute.1) | copy-start | bytes 1179652
  2.5 47.3 %collective-permute-start = (f32[2,16,2,1536]{3,2,1,0:T(2,128)S(1)}, f32[2,16,2,1536]{3,2,1,0:T(2,128)S(1)}, u32[]{:S(2)}, u32[]{:S(2)}) collective-permute-start(f32[2,16,2,1536]{3,2,1,0:T(2,128)S(1)} %get-tuple-element.20), channel_id=1, source_target_pairs={{0,6},{6,12},{12,18},{18,24},{24,30},{30,36},{36,42},{42,48},{48,5... | collective-permute-start | bytes 1179656 | tf_op jit(solution)/shard_map/ppermute | solution.py:24
  6.5 43.3 %collective-permute-start.1 = (f32[2,16,2,1536]{3,2,1,0:T(2,128)S(1)}, f32[2,16,2,1536]{3,2,1,0:T(2,128)S(1)}, u32[]{:S(2)}, u32[]{:S(2)}) collective-permute-start(f32[2,16,2,1536]{3,2,1,0:T(2,128)S(1)} %get-tuple-element.19), channel_id=1, source_target_pairs={{0,762},{6,0},{12,6},{18,12},{24,18},{30,24},{36,30},{42,36},{48,4... | collective-permute-start | bytes 1179656 | tf_op jit(solution)/shard_map/ppermute | solution.py:24
  8.5 29.6 %collective-permute-start.2 = (f32[2,2,4,1536]{3,2,1,0:T(4,128)S(1)}, f32[2,2,4,1536]{3,2,1,0:T(4,128)S(1)}, u32[]{:S(2)}, u32[]{:S(2)}) collective-permute-start(f32[2,2,4,1536]{3,2,1,0:T(4,128)S(1)} %get-tuple-element.18), channel_id=1, source_target_pairs={{0,1},{1,2},{2,3},{3,4},{4,5},{5,0},{6,7},{7,8},{8,9},{9,10},{10,1... | collective-permute-start | bytes 294920 | tf_op jit(solution)/shard_map/ppermute | solution.py:24
  20.0 17.5 %collective-permute-start.3 = (f32[2,2,4,1536]{3,2,1,0:T(4,128)S(1)}, f32[2,2,4,1536]{3,2,1,0:T(4,128)S(1)}, u32[]{:S(2)}, u32[]{:S(2)}) collective-permute-start(f32[2,2,4,1536]{3,2,1,0:T(4,128)S(1)} %get-tuple-element.17), channel_id=1, source_target_pairs={{0,5},{1,0},{2,1},{3,2},{4,3},{5,4},{6,11},{7,6},{8,7},{9,8},{10,9... | collective-permute-start | bytes 294920 | tf_op jit(solution)/shard_map/ppermute | solution.py:24
  21.9 0.7 copy-start.8
  37.5 0.6 copy-start.5
  38.1 0.9 copy-start.4
  38.1 0.8 slice-start
  39.0 10.7 %collective-permute-start.4 = (f32[2,2,1,1536]{3,2,1,0:T(1,128)S(1)}, f32[2,2,1,1536]{3,2,1,0:T(1,128)S(1)}, u32[]{:S(2)}, u32[]{:S(2)}) collective-permute-start(f32[2,2,1,1536]{3,2,1,0:T(1,128)S(1)} %get-tuple-element.22), channel_id=1, source_target_pairs={{0,6},{6,12},{12,18},{18,24},{24,30},{30,36},{36,42},{42,48},{48,5... | collective-permute-start | bytes 73736 | tf_op jit(solution)/shard_map/ppermute | solution.py:24
  40.9 8.8 %collective-permute-start.5 = (f32[2,2,1,1536]{3,2,1,0:T(1,128)S(1)}, f32[2,2,1,1536]{3,2,1,0:T(1,128)S(1)}, u32[]{:S(2)}, u32[]{:S(2)}) collective-permute-start(f32[2,2,1,1536]{3,2,1,0:T(1,128)S(1)} %get-tuple-element.21), channel_id=1, source_target_pairs={{0,762},{6,0},{12,6},{18,12},{24,18},{30,24},{36,30},{42,36},{48,4... | collective-permute-start | bytes 73736 | tf_op jit(solution)/shard_map/ppermute | solution.py:24
  49.8 0.8 copy-start.6
  49.8 0.8 copy-start.7
  49.8 0.8 copy-start.2
  49.8 0.9 copy-start.3
  59.4 4.0 %collective-permute-start.12 = (f32[4,128]{1,0:T(4,128)S(1)}, f32[4,128]{1,0:T(4,128)S(1)}, u32[]{:S(2)}, u32[]{:S(2)}) collective-permute-start(f32[4,128]{1,0:T(4,128)S(1)} %get-tuple-element.24), channel_id=1, source_target_pairs={{0,5},{6,11},{12,17},{18,23},{24,29},{30,35},{36,41},{42,47},{48,5... | collective-permute-start | bytes 6152 | tf_op jit(solution)/shard_map/ppermute | solution.py:265
  60.0 3.3 %collective-permute-start.11 = (f32[4,128]{1,0:T(4,128)S(1)}, f32[4,128]{1,0:T(4,128)S(1)}, u32[]{:S(2)}, u32[]{:S(2)}) collective-permute-start(f32[4,128]{1,0:T(4,128)S(1)} %get-tuple-element.25), channel_id=1, source_target_pairs={{0,4},{6,10},{12,16},{18,22},{24,28},{30,34},{36,40},{42,46},{48,5... | collective-permute-start | bytes 6152 | tf_op jit(solution)/shard_map/ppermute | solution.py:265
  60.7 2.7 %collective-permute-start.10 = (f32[4,128]{1,0:T(4,128)S(1)}, f32[4,128]{1,0:T(4,128)S(1)}, u32[]{:S(2)}, u32[]{:S(2)}) collective-permute-start(f32[4,128]{1,0:T(4,128)S(1)} %get-tuple-element.26), channel_id=1, source_target_pairs={{0,3},{6,9},{12,15},{18,21},{24,27},{30,33},{36,39},{42,45},{48,51... | collective-permute-start | bytes 6152 | tf_op jit(solution)/shard_map/ppermute | solution.py:265
  61.4 2.0 %collective-permute-start.9 = (f32[4,128]{1,0:T(4,128)S(1)}, f32[4,128]{1,0:T(4,128)S(1)}, u32[]{:S(2)}, u32[]{:S(2)}) collective-permute-start(f32[4,128]{1,0:T(4,128)S(1)} %get-tuple-element.27), channel_id=1, source_target_pairs={{0,2},{6,8},{12,14},{18,20},{24,26},{30,32},{36,38},{42,44},{48,50... | collective-permute-start | bytes 6152 | tf_op jit(solution)/shard_map/ppermute | solution.py:265
  62.0 7.2 %collective-permute-start.8 = (f32[4,128]{1,0:T(4,128)S(1)}, f32[4,128]{1,0:T(4,128)S(1)}, u32[]{:S(2)}, u32[]{:S(2)}) collective-permute-start(f32[4,128]{1,0:T(4,128)S(1)} %get-tuple-element.23), channel_id=1, source_target_pairs={{0,1},{6,7},{12,13},{18,19},{24,25},{30,31},{36,37},{42,43},{48,49... | collective-permute-start | bytes 6152 | tf_op jit(solution)/shard_map/ppermute | solution.py:265
  70.6 12.9 %all-to-all-start = ((f32[8,4,128]{2,1,0:T(4,128)}), f32[8,4,128]{2,1,0:T(4,128)S(1)}, u32[]{:S(2)}, u32[]{:S(2)}) async-start(f32[8,4,128]{2,1,0:T(4,128)} %broadcast_select_fusion), calls=%async_computation | async-start | bytes 32768 | tf_op jit(solution)/shard_map/all_to_all | solution.py:270
  84.4 14.3 %all-to-all-start.1 = ((f32[16,4,128]{2,1,0:T(4,128)}), f32[16,4,128]{2,1,0:T(4,128)S(1)}, u32[]{:S(2)}, u32[]{:S(2)}) async-start(f32[16,4,128]{2,1,0:T(4,128)} %select_reduce_fusion), calls=%async_computation.1 | async-start | bytes 65536 | tf_op jit(solution)/shard_map/all_to_all | solution.py:278
  92.7 36.1 %collective-permute-start.6 = (f32[16,4,1536]{2,1,0:T(4,128)}, f32[16,4,1536]{2,1,0:T(4,128)S(1)}, u32[]{:S(2)}, u32[]{:S(2)}) collective-permute-start(f32[16,4,1536]{2,1,0:T(4,128)} %get-tuple-element.6), channel_id=1, source_target_pairs={{0,5},{1,0},{2,1},{3,2},{4,3},{5,4},{6,11},{7,6},{8,7},{9,8},{10,9... | collective-permute-start | bytes 1179656 | tf_op jit(solution)/shard_map/ppermute | solution.py:24
  96.8 40.2 %collective-permute-start.7 = (f32[16,4,1536]{2,1,0:T(4,128)}, f32[16,4,1536]{2,1,0:T(4,128)S(1)}, u32[]{:S(2)}, u32[]{:S(2)}) collective-permute-start(f32[16,4,1536]{2,1,0:T(4,128)} %get-tuple-element.7), channel_id=1, source_target_pairs={{0,5},{1,0},{2,1},{3,2},{4,3},{5,4},{6,11},{7,6},{8,7},{9,8},{10,9... | collective-permute-start | bytes 1179656 | tf_op jit(solution)/shard_map/ppermute | solution.py:24

commit v5 on v4

--- a/solution.py
+++ b/solution.py
@@ -22,6 +22,10 @@
 def shift(block, axis, step):
     count = lax.axis_size(axis)
     return lax.ppermute(block, axis, [(i, (i + step) % count) for i in range(count)])
+
+
+def near(block):
+    return pltpu.with_memory_space_constraint(block, pltpu.VMEM)
 
 
 def clipped(p):
@@ -58,7 +62,7 @@
 
 
 def steps_kernel(
-    at, phase, solute, left, right, below, above, edge_l, edge_r, weights, phase_to, solute_to, coarse_to,
+    at, phase, solute, left, right, below, above, edge_l, edge_r, weights, state_to, coarse_to,
     op, ou, dp, du, opr, our, dpr, dur, sp, su, spr, sur, tpr, tur, sums,
 ):
     planes, rows, width = phase.shape
@@ -135,7 +139,7 @@
         p, near_p = neighbours(*fields_p, t, t_low, t_high, c)
         u, near_u = neighbours(*fields_u, t, t_low, t_high, c)
         here = pl.ds(c * LANES, LANES)
-        return cell_step(p, u, near_p, near_u, theta, weights[0, :, here], weights[1, :, here])
+        return cell_step(p, u, near_p, near_u, theta, weights[0:1, here], weights[1:2, here])
 
     def own_once(t, carry):
         theta = theta_of(t)
@@ -175,12 +179,10 @@
             p, u = tile_step((sp, spr, tpr), (su, sur, tur), t, t - 1, t + 1, theta, c)
             sums[0, k, c : c + 1] = jnp.sum(p, axis=0, keepdims=True)
             sums[1, k, c : c + 1] = jnp.sum(u, axis=0, keepdims=True)
-            p = jnp.where(lowest, -1.0, p)
-            u = jnp.where(lowest, liquid_u, u)
-            phase_to[2 * k, :, here] = p[:rows]
-            phase_to[2 * k + 1, :, here] = p[rows:]
-            solute_to[2 * k, :, here] = u[:rows]
-            solute_to[2 * k + 1, :, here] = u[rows:]
+            state_to[0, 2 * k, :, here] = p[:rows]
+            state_to[0, 2 * k + 1, :, here] = p[rows:]
+            state_to[1, 2 * k, :, here] = u[:rows]
+            state_to[1, 2 * k + 1, :, here] = u[rows:]
         return carry
 
     lax.fori_loop(0, pairs, own_twice, 0)
@@ -222,24 +224,22 @@
     return pl.pallas_call(
         steps_kernel,
         out_shape=(
-            jax.ShapeDtypeStruct(phase.shape, jnp.float32),
-            jax.ShapeDtypeStruct(phase.shape, jnp.float32),
+            jax.ShapeDtypeStruct((2,) + phase.shape, jnp.float32),
             jax.ShapeDtypeStruct((pieces, pairs // 2, LANES), jnp.float32),
         ),
         in_specs=[pl.BlockSpec(memory_space=pltpu.SMEM)] + [vmem] * 9,
-        out_specs=(vmem, vmem, vmem),
+        out_specs=(vmem, vmem),
         scratch_shapes=[scratch] * 14 + [pltpu.VMEM((2, pairs, width // LANES, LANES), jnp.float32)],
         interpret=interpret,
     )(at, phase, solute, left, right, below, above, edge_l, edge_r, weights)
 
 
 def work(phase, solute, seed_grain, writer):
-    _, rows, width = phase.shape
+    _, _, width = phase.shape
     grow_count = lax.axis_size("grow")
     grow_at = lax.axis_index("grow")
     lat_at = lax.axis_index(LAT)
-    x_count, y_count, z_count = (lax.axis_size(axis) for axis in LAT)
-    x_at, y_at, z_at = (lax.axis_index(axis) for axis in LAT)
+    lat_count = lax.axis_size(LAT)
     state = jnp.stack([phase, solute])
 
     below = shift(state[:, -2:], "grow", 1)
@@ -252,30 +252,23 @@
 
     turned = seed_grain > 0
     weights = jnp.stack([jnp.where(turned, 0.5, 1.0), jnp.where(turned, 2.0, -2.0)]).astype(jnp.float32)
-    weights = jnp.broadcast_to(weights[:, None], (2, 2 * rows, width))
     at = jnp.stack([grow_at, jnp.int32(grow_count)]).astype(jnp.int32)
-    phase_to, solute_to, blocks = two_steps(
-        at, phase, solute, left, right, below, above, edge_l, edge_r, weights, grow_count
-    )
-    phase_out = shift(phase_to, "grow", -1)
-    solute_out = shift(solute_to, "grow", -1)
-
-    mine = jnp.where(grow_at == 0, blocks[0], 0.0)
-    for r in range(1, grow_count):
-        mine = mine + lax.ppermute(blocks[r], "grow", [(0, r)])
+    halos = tuple(near(halo) for halo in (left, right, below, above, edge_l, edge_r))
+    state, blocks = two_steps(at, phase, solute, *halos, weights, grow_count)
+
+    odd = lax.ppermute(blocks[1::2], "grow", [(0, 1)])
+    rows_of = jnp.where(grow_at == 0, blocks[0::2], odd)
+    mine = jnp.where(grow_at < 2, rows_of[0], 0.0)
+    for step in range(1, grow_count // 2):
+        mine = mine + lax.ppermute(rows_of[step], "grow", [(0, 2 * step), (1, 2 * step + 1)])
+    arrived = lax.ppermute(state, "grow", [(i, i - 1) for i in range(1, grow_count)])
+    top = grow_at == grow_count - 1
+    phase_out = jnp.where(top, -1.0, arrived[0])
+    solute_out = jnp.where(top, liquid_u, arrived[1])
     row_ids = lax.dynamic_index_in_dim(writer, grow_at, 0, keepdims=False)
     target = lax.dynamic_index_in_dim(row_ids, lat_at, 0, keepdims=False)
-    to_y = jnp.arange(y_count) == target // z_count % y_count
-    slots = jnp.where(to_y[:, None, None], mine[None], 0.0)
-    held = lax.all_to_all(slots, "y", 0, 0, tiled=True)
-    row_ids = row_ids.reshape(x_count, y_count, z_count)
-    onward = lax.dynamic_index_in_dim(row_ids, x_at, 0, keepdims=False)
-    onward = lax.dynamic_index_in_dim(onward, z_at, 1, keepdims=False)
-    place = onward // (y_count * z_count) * z_count + onward % z_count
-    place = jnp.where(onward // z_count % y_count == y_at, place, -1)
-    chosen = jnp.arange(x_count * z_count)[:, None] == place[None]
-    slots = jnp.where(chosen[:, :, None, None], held[None], 0.0).sum(axis=1)
-    landed = lax.all_to_all(slots, ("x", "z"), 0, 0, tiled=True).sum(axis=0)
+    slots = jnp.where((jnp.arange(lat_count) == target)[:, None, None], mine[None], 0.0)
+    landed = lax.all_to_all(slots, LAT, 0, 0, tiled=True).sum(axis=0)
     piece = width // 4 // grow_count
     landed = jnp.stack([landed[:, :piece], landed[:, piece:]])
     return (phase_out, solute_out, landed[None, None, :, :, None])

time: 139 us -> 111 us (0.80)
  the two profiles are of different devices: /device:TPU:65 before, /device:TPU:1 now
where the time goes in v5:
time: 111 us; the launch traced here: 110 us
  starting transfers between devices  60.9 us (55%)
  waiting for transfers between devices  31.5 us (28%)
  Pallas kernels  7.61 us (7%)
  other arithmetic  5.97 us (5%)
  local copies, waits for them, and re-layouts  3.52 us (3%)
    ppermute x6, starting transfers between devices, shift(): lax.ppermute(block, axis, [(i, (i + step) % count) for i in range(count)])  39.6 us
    ppermute x1, waiting for transfers between devices, work(): lax.ppermute(state, 'grow', [(i, i - 1) for i in range(1, grow_count)])  16.1 us
    all_to_all x1, waiting for transfers between devices, work(): landed = lax.all_to_all(slots, LAT, 0, 0, tiled=True).sum(axis=0)  11.2 us
    all_to_all x1, starting transfers between devices, work(): landed = lax.all_to_all(slots, LAT, 0, 0, tiled=True).sum(axis=0)  8.56 us
    ppermute x2, starting transfers between devices, work(): lax.ppermute(rows_of[step], 'grow', [(0, 2 * step), (1, 2 * step + 1)])  7.8 us
    pallas_call x1, Pallas kernels, two_steps(): pl.pallas_call(steps_kernel, out_shape=(jax.ShapeDtypeStruct((2,) + phase...  7.61 us
    ppermute x6, waiting for transfers between devices, shift(): lax.ppermute(block, axis, [(i, (i + step) % count) for i in range(count)])  4.11 us
    ppermute x1, starting transfers between devices, work(): lax.ppermute(state, 'grow', [(i, i - 1) for i in range(1, grow_count)])  3.68 us
  transfers between devices with their start and end apart: 11, of which 3 were waited for; matrix products, arithmetic and copies ran while one was open for 5% of the time, Pallas kernels for 0%

profile of v5, /device:TPU:1, one launch (start us, length us, event | category | flops | bytes accessed | tf_op | source)
XLA Modules:
  0.0 110.5 jit_solution(15452110336262269147)
XLA Ops:
  0.6 0.0 copy-start.2
  0.6 0.0 copy-start.3
  0.7 1.0 pad_maximum_fusion
  1.6 12.0 %collective-permute-start.2 = (f32[2,2,4,1536]{3,2,1,0:T(4,128)S(1)}, f32[2,2,4,1536]{3,2,1,0:T(4,128)S(1)}, u32[]{:S(2)}, u32[]{:S(2)}) collective-permute-start(f32[2,2,4,1536]{3,2,1,0:T(4,128)S(1)} %get-tuple-element.18), channel_id=1, source_target_pairs={{0,1},{1,2},{2,3},{3,4},{4,5},{5,0},{6,7},{7,8},{8,9},{9,10},{10,1... | collective-permute-start | bytes 294920 | tf_op jit(solution)/shard_map/ppermute | solution.py:24
  13.7 2.3 %collective-permute-start.3 = (f32[2,2,4,1536]{3,2,1,0:T(4,128)S(1)}, f32[2,2,4,1536]{3,2,1,0:T(4,128)S(1)}, u32[]{:S(2)}, u32[]{:S(2)}) collective-permute-start(f32[2,2,4,1536]{3,2,1,0:T(4,128)S(1)} %get-tuple-element.17), channel_id=1, source_target_pairs={{0,5},{1,0},{2,1},{3,2},{4,3},{5,4},{6,11},{7,6},{8,7},{9,8},{10,9... | collective-permute-start | bytes 294920 | tf_op jit(solution)/shard_map/ppermute | solution.py:24
  16.0 0.0 copy-done.2
  16.0 0.0 copy-done.3
  16.0 0.0 copy-start.5
  16.0 0.3 fusion.1
  16.3 3.6 %collective-permute-start = (f32[2,16,2,1536]{3,2,1,0:T(2,128)S(1)}, f32[2,16,2,1536]{3,2,1,0:T(2,128)S(1)}, u32[]{:S(2)}, u32[]{:S(2)}) collective-permute-start(f32[2,16,2,1536]{3,2,1,0:T(2,128)S(1)} %get-tuple-element.20), channel_id=1, source_target_pairs={{0,6},{6,12},{12,18},{18,24},{24,30},{30,36},{36,42},{42,48},{48,5... | collective-permute-start | bytes 1179656 | tf_op jit(solution)/shard_map/ppermute | solution.py:24
  19.9 10.3 %collective-permute-start.1 = (f32[2,16,2,1536]{3,2,1,0:T(2,128)S(1)}, f32[2,16,2,1536]{3,2,1,0:T(2,128)S(1)}, u32[]{:S(2)}, u32[]{:S(2)}) collective-permute-start(f32[2,16,2,1536]{3,2,1,0:T(2,128)S(1)} %get-tuple-element.19), channel_id=1, source_target_pairs={{0,762},{6,0},{12,6},{18,12},{24,18},{30,24},{36,30},{42,36},{48,4... | collective-permute-start | bytes 1179656 | tf_op jit(solution)/shard_map/ppermute | solution.py:24
  30.3 0.0 copy-done.5
  30.4 0.6 pad_maximum_fusion.3.weights
  31.0 0.0 collective-permute-done.2.below
  31.0 0.0 copy-start
  31.0 0.6 copy-done
  31.6 0.0 collective-permute-done.3.above
  31.6 0.0 slice-start
  31.6 0.8 slice-done
  32.5 1.9 %collective-permute-start.4 = (f32[2,2,1,1536]{3,2,1,0:T(1,128)S(1)}, f32[2,2,1,1536]{3,2,1,0:T(1,128)S(1)}, u32[]{:S(2)}, u32[]{:S(2)}) collective-permute-start(f32[2,2,1,1536]{3,2,1,0:T(1,128)S(1)} %get-tuple-element.22), channel_id=1, source_target_pairs={{0,6},{6,12},{12,18},{18,24},{24,30},{30,36},{36,42},{42,48},{48,5... | collective-permute-start | bytes 73736 | tf_op jit(solution)/shard_map/ppermute | solution.py:24
  34.4 9.4 %collective-permute-start.5 = (f32[2,2,1,1536]{3,2,1,0:T(1,128)S(1)}, f32[2,2,1,1536]{3,2,1,0:T(1,128)S(1)}, u32[]{:S(2)}, u32[]{:S(2)}) collective-permute-start(f32[2,2,1,1536]{3,2,1,0:T(1,128)S(1)} %get-tuple-element.21), channel_id=1, source_target_pairs={{0,762},{6,0},{12,6},{18,12},{24,18},{30,24},{36,30},{42,36},{48,4... | collective-permute-start | bytes 73736 | tf_op jit(solution)/shard_map/ppermute | solution.py:24
  43.8 0.6 pad_add_fusion.at
  44.4 4.1 %collective-permute-done.4.edge_l = f32[2,2,1,1536]{3,2,1,0:T(1,128)S(1)} collective-permute-done((f32[2,2,1,1536]{3,2,1,0:T(1,128)S(1)}, f32[2,2,1,1536]{3,2,1,0:T(1,128)S(1)}, u32[]{:S(2)}, u32[]{:S(2)}) %collective-permute-start.4) | collective-permute-done | bytes 24608 | tf_op jit(solution)/shard_map/ppermute | solution.py:24
  48.5 0.0 collective-permute-done.5.edge_r
  48.5 0.0 collective-permute-done.left
  48.5 0.0 collective-permute-done.1.right
  48.5 0.0 copy-done.1
  48.5 7.6 %shard_map.67 = (f32[2,16,4,1536]{3,2,1,0:T(4,128)}, f32[6,4,128]{2,1,0:T(4,128)}) custom-call(s32[2]{0:T(128)} %pad_add_fusion.at, f32[16,4,1536]{2,1,0:T(4,128)} %phase.1, f32[16,4,1536]{2,1,0:T(4,128)} %solute.1, f32[2,16,2,1536]{3,2,1,0:T(2,128)S(1)} %collective-permute-done.left, f32[2,16,2,1536]{3,2,1,0:T(2,128)S(1)} %collective-permute-done.1.right, ...), custom_call_target="tpu_custom_call" | custom-call | tf_op jit(solution)/shard_map/pallas_call | solution.py:224
  56.1 0.7 slice.62
  56.8 1.3 %collective-permute-start.7 = (f32[3,4,128]{2,1,0:T(4,128)S(1)}, f32[3,4,128]{2,1,0:T(4,128)S(1)}, u32[]{:S(2)}, u32[]{:S(2)}) collective-permute-start(f32[3,4,128]{2,1,0:T(4,128)S(1)} %slice.62), channel_id=1, source_target_pairs={{0,1},{6,7},{12,13},{18,19},{24,25},{30,31},{36,37},{42,43},{48,49... | collective-permute-start | bytes 18440 | tf_op jit(solution)/shard_map/ppermute | solution.py:259
  58.1 0.0 copy-start.4
  58.2 1.3 %dynamic_slice.6 = s32[1,1]{1,0:T(1,128)} dynamic-slice(s32[6,128]{1,0:T(8,128)} %param.7, s32[]{:T(128)S(6)} %select_n.68, s32[]{:T(128)S(6)} %select_n.70), dynamic_slice_sizes={1,1} | dynamic-slice | bytes 12 | tf_op jit(solution)/shard_map/jit(dynamic_index_in_dim)/dynamic_slice | solution.py:269
  59.4 3.7 %collective-permute-start.6 = (f32[2,16,4,1536]{3,2,1,0:T(4,128)}, f32[2,16,4,1536]{3,2,1,0:T(4,128)S(1)}, u32[]{:S(2)}, u32[]{:S(2)}) collective-permute-start(f32[2,16,4,1536]{3,2,1,0:T(4,128)} %get-tuple-element.5), channel_id=1, source_target_pairs={{1,0},{2,1},{3,2},{4,3},{5,4},{7,6},{8,7},{9,8},{10,9},{11,10},{13... | collective-permute-start | bytes 2359304 | tf_op jit(solution)/shard_map/ppermute | solution.py:264
  63.1 0.0 collective-permute-done.7
  63.1 0.0 copy-done.4
  63.2 6.5 %collective-permute-start.8 = (f32[4,128]{1,0:T(4,128)S(1)}, f32[4,128]{1,0:T(4,128)S(1)}, u32[]{:S(2)}, u32[]{:S(2)}) collective-permute-start(f32[4,128]{1,0:T(4,128)S(1)} %get-tuple-element.23), channel_id=1, source_target_pairs={{0,2},{1,3},{6,8},{7,9},{12,14},{13,15},{18,20},{19,21},{24,26},{2... | collective-permute-start | bytes 6152 | tf_op jit(solution)/shard_map/ppermute | solution.py:263
  69.7 1.3 %collective-permute-start.9 = (f32[4,128]{1,0:T(4,128)S(1)}, f32[4,128]{1,0:T(4,128)S(1)}, u32[]{:S(2)}, u32[]{:S(2)}) collective-permute-start(f32[4,128]{1,0:T(4,128)S(1)} %get-tuple-element.24), channel_id=1, source_target_pairs={{0,4},{1,5},{6,10},{7,11},{12,16},{13,17},{18,22},{19,23},{24,28},... | collective-permute-start | bytes 6152 | tf_op jit(solution)/shard_map/ppermute | solution.py:263
  71.0 0.7 iota_compare_fusion
  71.6 0.0 collective-permute-done.8
  71.7 0.0 collective-permute-done.9
  71.7 0.9 broadcast_select_fusion
  72.6 8.6 %all-to-all-start = ((f32[128,4,128]{2,1,0:T(4,128)}), f32[128,4,128]{2,1,0:T(4,128)S(1)}, u32[]{:S(2)}, u32[]{:S(2)}) async-start(f32[128,4,128]{2,1,0:T(4,128)} %broadcast_select_fusion), calls=%async_computation | async-start | bytes 524288 | tf_op jit(solution)/shard_map/all_to_all | solution.py:271
  81.2 16.1 %collective-permute-done.6 = f32[2,16,4,1536]{3,2,1,0:T(4,128)S(1)} collective-permute-done((f32[2,16,4,1536]{3,2,1,0:T(4,128)}, f32[2,16,4,1536]{3,2,1,0:T(4,128)S(1)}, u32[]{:S(2)}, u32[]{:S(2)}) %collective-permute-start.6) | collective-permute-done | bytes 786464 | tf_op jit(solution)/shard_map/ppermute | solution.py:264
  97.3 1.1 fusion.2
  98.4 11.2 %all-to-all-done = f32[128,4,128]{2,1,0:T(4,128)S(1)} async-done(((f32[128,4,128]{2,1,0:T(4,128)}), f32[128,4,128]{2,1,0:T(4,128)S(1)}, u32[]{:S(2)}, u32[]{:S(2)}) %all-to-all-start) | async-done | bytes 262176 | tf_op jit(solution)/shard_map/all_to_all | solution.py:271
  109.6 0.1 reduce_sum.9
  109.8 0.1 slice_bitcast_fusion.3
  109.9 0.6 pad_maximum_fusion.4
  (10 shorter events, 0.1 us)
Async XLA Ops:
  0.6 15.3 %copy-start.2 = (f32[16,4,1536]{2,1,0:T(4,128)S(1)}, f32[16,4,1536]{2,1,0:T(4,128)}, u32[]{:S(2)}) copy-start(f32[16,4,1536]{2,1,0:T(4,128)} %phase.1) | copy-start | bytes 1179652
  0.6 15.3 %copy-start.3 = (f32[16,4,1536]{2,1,0:T(4,128)S(1)}, f32[16,4,1536]{2,1,0:T(4,128)}, u32[]{:S(2)}) copy-start(f32[16,4,1536]{2,1,0:T(4,128)} %solute.1) | copy-start | bytes 1179652
  1.6 29.3 %collective-permute-start.2 = (f32[2,2,4,1536]{3,2,1,0:T(4,128)S(1)}, f32[2,2,4,1536]{3,2,1,0:T(4,128)S(1)}, u32[]{:S(2)}, u32[]{:S(2)}) collective-permute-start(f32[2,2,4,1536]{3,2,1,0:T(4,128)S(1)} %get-tuple-element.18), channel_id=1, source_target_pairs={{0,1},{1,2},{2,3},{3,4},{4,5},{5,0},{6,7},{7,8},{8,9},{9,10},{10,1... | collective-permute-start | bytes 294920 | tf_op jit(solution)/shard_map/ppermute | solution.py:24
  13.7 18.0 %collective-permute-start.3 = (f32[2,2,4,1536]{3,2,1,0:T(4,128)S(1)}, f32[2,2,4,1536]{3,2,1,0:T(4,128)S(1)}, u32[]{:S(2)}, u32[]{:S(2)}) collective-permute-start(f32[2,2,4,1536]{3,2,1,0:T(4,128)S(1)} %get-tuple-element.17), channel_id=1, source_target_pairs={{0,5},{1,0},{2,1},{3,2},{4,3},{5,4},{6,11},{7,6},{8,7},{9,8},{10,9... | collective-permute-start | bytes 294920 | tf_op jit(solution)/shard_map/ppermute | solution.py:24
  16.0 14.3 %copy-start.5 = (s32[1536]{0:T(1024)S(1)}, s32[1536]{0:T(1024)}, u32[]{:S(2)}) copy-start(s32[1536]{0:T(1024)} %param.6) | copy-start | bytes 18436
  16.3 32.2 %collective-permute-start = (f32[2,16,2,1536]{3,2,1,0:T(2,128)S(1)}, f32[2,16,2,1536]{3,2,1,0:T(2,128)S(1)}, u32[]{:S(2)}, u32[]{:S(2)}) collective-permute-start(f32[2,16,2,1536]{3,2,1,0:T(2,128)S(1)} %get-tuple-element.20), channel_id=1, source_target_pairs={{0,6},{6,12},{12,18},{18,24},{24,30},{30,36},{36,42},{42,48},{48,5... | collective-permute-start | bytes 1179656 | tf_op jit(solution)/shard_map/ppermute | solution.py:24
  19.9 28.6 %collective-permute-start.1 = (f32[2,16,2,1536]{3,2,1,0:T(2,128)S(1)}, f32[2,16,2,1536]{3,2,1,0:T(2,128)S(1)}, u32[]{:S(2)}, u32[]{:S(2)}) collective-permute-start(f32[2,16,2,1536]{3,2,1,0:T(2,128)S(1)} %get-tuple-element.19), channel_id=1, source_target_pairs={{0,762},{6,0},{12,6},{18,12},{24,18},{30,24},{36,30},{42,36},{48,4... | collective-permute-start | bytes 1179656 | tf_op jit(solution)/shard_map/ppermute | solution.py:24
  31.0 0.6 copy-start
  31.6 0.8 slice-start
  32.4 16.1 %copy-start.1 = (f32[2,2,4,1536]{3,2,1,0:T(4,128)S(1)}, f32[2,2,4,1536]{3,2,1,0:T(4,128)}, u32[]{:S(2)}) copy-start(f32[2,2,4,1536]{3,2,1,0:T(4,128)} %copy-done) | copy-start | bytes 294916
  32.5 16.0 %collective-permute-start.4 = (f32[2,2,1,1536]{3,2,1,0:T(1,128)S(1)}, f32[2,2,1,1536]{3,2,1,0:T(1,128)S(1)}, u32[]{:S(2)}, u32[]{:S(2)}) collective-permute-start(f32[2,2,1,1536]{3,2,1,0:T(1,128)S(1)} %get-tuple-element.22), channel_id=1, source_target_pairs={{0,6},{6,12},{12,18},{18,24},{24,30},{30,36},{36,42},{42,48},{48,5... | collective-permute-start | bytes 73736 | tf_op jit(solution)/shard_map/ppermute | solution.py:24
  34.4 14.1 %collective-permute-start.5 = (f32[2,2,1,1536]{3,2,1,0:T(1,128)S(1)}, f32[2,2,1,1536]{3,2,1,0:T(1,128)S(1)}, u32[]{:S(2)}, u32[]{:S(2)}) collective-permute-start(f32[2,2,1,1536]{3,2,1,0:T(1,128)S(1)} %get-tuple-element.21), channel_id=1, source_target_pairs={{0,762},{6,0},{12,6},{18,12},{24,18},{30,24},{36,30},{42,36},{48,4... | collective-permute-start | bytes 73736 | tf_op jit(solution)/shard_map/ppermute | solution.py:24
  56.8 6.3 %collective-permute-start.7 = (f32[3,4,128]{2,1,0:T(4,128)S(1)}, f32[3,4,128]{2,1,0:T(4,128)S(1)}, u32[]{:S(2)}, u32[]{:S(2)}) collective-permute-start(f32[3,4,128]{2,1,0:T(4,128)S(1)} %slice.62), channel_id=1, source_target_pairs={{0,1},{6,7},{12,13},{18,19},{24,25},{30,31},{36,37},{42,43},{48,49... | collective-permute-start | bytes 18440 | tf_op jit(solution)/shard_map/ppermute | solution.py:259
  58.1 5.0 %copy-start.4 = (f32[6,4,128]{2,1,0:T(4,128)S(1)}, f32[6,4,128]{2,1,0:T(4,128)}, u32[]{:S(2)}) copy-start(f32[6,4,128]{2,1,0:T(4,128)} %get-tuple-element.6) | copy-start | bytes 36868
  59.4 37.9 %collective-permute-start.6 = (f32[2,16,4,1536]{3,2,1,0:T(4,128)}, f32[2,16,4,1536]{3,2,1,0:T(4,128)S(1)}, u32[]{:S(2)}, u32[]{:S(2)}) collective-permute-start(f32[2,16,4,1536]{3,2,1,0:T(4,128)} %get-tuple-element.5), channel_id=1, source_target_pairs={{1,0},{2,1},{3,2},{4,3},{5,4},{7,6},{8,7},{9,8},{10,9},{11,10},{13... | collective-permute-start | bytes 2359304 | tf_op jit(solution)/shard_map/ppermute | solution.py:264
  63.2 8.5 %collective-permute-start.8 = (f32[4,128]{1,0:T(4,128)S(1)}, f32[4,128]{1,0:T(4,128)S(1)}, u32[]{:S(2)}, u32[]{:S(2)}) collective-permute-start(f32[4,128]{1,0:T(4,128)S(1)} %get-tuple-element.23), channel_id=1, source_target_pairs={{0,2},{1,3},{6,8},{7,9},{12,14},{13,15},{18,20},{19,21},{24,26},{2... | collective-permute-start | bytes 6152 | tf_op jit(solution)/shard_map/ppermute | solution.py:263
  69.7 2.0 %collective-permute-start.9 = (f32[4,128]{1,0:T(4,128)S(1)}, f32[4,128]{1,0:T(4,128)S(1)}, u32[]{:S(2)}, u32[]{:S(2)}) collective-permute-start(f32[4,128]{1,0:T(4,128)S(1)} %get-tuple-element.24), channel_id=1, source_target_pairs={{0,4},{1,5},{6,10},{7,11},{12,16},{13,17},{18,22},{19,23},{24,28},... | collective-permute-start | bytes 6152 | tf_op jit(solution)/shard_map/ppermute | solution.py:263
  72.6 37.0 %all-to-all-start = ((f32[128,4,128]{2,1,0:T(4,128)}), f32[128,4,128]{2,1,0:T(4,128)S(1)}, u32[]{:S(2)}, u32[]{:S(2)}) async-start(f32[128,4,128]{2,1,0:T(4,128)} %broadcast_select_fusion), calls=%async_computation | async-start | bytes 524288 | tf_op jit(solution)/shard_map/all_to_all | solution.py:271

commit v6 on v5

--- a/solution.py
+++ b/solution.py
@@ -239,7 +239,8 @@
     grow_count = lax.axis_size("grow")
     grow_at = lax.axis_index("grow")
     lat_at = lax.axis_index(LAT)
-    lat_count = lax.axis_size(LAT)
+    x_count, y_count, z_count = (lax.axis_size(axis) for axis in LAT)
+    x_at, y_at, z_at = (lax.axis_index(axis) for axis in LAT)
     state = jnp.stack([phase, solute])
 
     below = shift(state[:, -2:], "grow", 1)
@@ -256,19 +257,26 @@
     halos = tuple(near(halo) for halo in (left, right, below, above, edge_l, edge_r))
     state, blocks = two_steps(at, phase, solute, *halos, weights, grow_count)
 
-    odd = lax.ppermute(blocks[1::2], "grow", [(0, 1)])
-    rows_of = jnp.where(grow_at == 0, blocks[0::2], odd)
-    mine = jnp.where(grow_at < 2, rows_of[0], 0.0)
-    for step in range(1, grow_count // 2):
-        mine = mine + lax.ppermute(rows_of[step], "grow", [(0, 2 * step), (1, 2 * step + 1)])
     arrived = lax.ppermute(state, "grow", [(i, i - 1) for i in range(1, grow_count)])
     top = grow_at == grow_count - 1
     phase_out = jnp.where(top, -1.0, arrived[0])
     solute_out = jnp.where(top, liquid_u, arrived[1])
-    row_ids = lax.dynamic_index_in_dim(writer, grow_at, 0, keepdims=False)
-    target = lax.dynamic_index_in_dim(row_ids, lat_at, 0, keepdims=False)
-    slots = jnp.where((jnp.arange(lat_count) == target)[:, None, None], mine[None], 0.0)
-    landed = lax.all_to_all(slots, LAT, 0, 0, tiled=True).sum(axis=0)
+
+    targets = lax.dynamic_index_in_dim(writer, lat_at, 1, keepdims=False)
+    to_y = jnp.arange(y_count)[:, None] == (targets // z_count % y_count)[None]
+    slots = jnp.where(to_y[:, :, None, None], blocks[None], 0.0)
+    held = lax.all_to_all(slots, "y", 0, 0, tiled=True)
+    onward = writer.reshape(grow_count, x_count, y_count, z_count)
+    onward = lax.dynamic_index_in_dim(onward, x_at, 1, keepdims=False)
+    onward = lax.dynamic_index_in_dim(onward, z_at, 2, keepdims=False)
+    place = onward // (y_count * z_count) * z_count + onward % z_count
+    place = jnp.where(onward // z_count % y_count == y_at, place, -1)
+    chosen = jnp.arange(x_count * z_count)[:, None, None] == place.T[None]
+    slots = jnp.where(chosen[..., None, None], held[None], 0.0).sum(axis=1)
+    landed = lax.all_to_all(
+        slots.reshape((-1,) + slots.shape[2:]), ("x", "z", "grow"), 0, 0, tiled=True
+    )
+    landed = landed.reshape(slots.shape)[:, 0].sum(axis=0)
     piece = width // 4 // grow_count
     landed = jnp.stack([landed[:, :piece], landed[:, piece:]])
     return (phase_out, solute_out, landed[None, None, :, :, None])

time: 111 us -> 134 us (1.21)
  waiting for transfers between devices: 31.5 us -> 59.3 us
  starting transfers between devices: 60.9 us -> 57.6 us
  local copies, waits for them, and re-layouts: 3.52 us -> 0.7 us
  other arithmetic: 5.97 us -> 7.79 us
    ppermute x1, waiting for transfers between devices: 16.1 us -> 29.2 us  [work(): lax.ppermute(state, 'grow', [(i, i - 1) for i in range(1, grow_count)])]
    all_to_all x1 -> x2, waiting for transfers between devices: 11.2 us -> 20.9 us  [the longest x1 13.3 us: work(): lax.all_to_all(slots.reshape((-1,) + slots.shape[2:]), ('x', 'z', 'grow')...]
    ppermute x3 -> x0, starting transfers between devices: 9.08 us -> none  [the longest x2 7.8 us: work(): lax.ppermute(rows_of[step], 'grow', [(0, 2 * step), (1, 2 * step + 1)])]
    all_to_all x1 -> x2, starting transfers between devices: 8.56 us -> 15.1 us  [the longest x1 11.8 us: work(): lax.all_to_all(slots.reshape((-1,) + slots.shape[2:]), ('x', 'z', 'grow')...]
    ppermute x6, waiting for transfers between devices: 4.11 us -> 9.17 us  [shift(): lax.ppermute(block, axis, [(i, (i + step) % count) for i in range(count)])]
  transfers between devices with their start and end apart: 11 -> 9, of which waited for: 3 -> 5; matrix products, arithmetic and copies ran while one was open for 5% -> 2% of each run, Pallas kernels for 0% -> 0%
where the time goes in v6:
time: 134 us
  waiting for transfers between devices  59.3 us (44%)
  starting transfers between devices  57.6 us (43%)
  other arithmetic  7.79 us (6%)
  Pallas kernels  7.61 us (6%)
    ppermute x6, starting transfers between devices, shift(): lax.ppermute(block, axis, [(i, (i + step) % count) for i in range(count)])  39.9 us
    ppermute x1, waiting for transfers between devices, work(): lax.ppermute(state, 'grow', [(i, i - 1) for i in range(1, grow_count)])  29.2 us
    all_to_all x1, waiting for transfers between devices, work(): lax.all_to_all(slots.reshape((-1,) + slots.shape[2:]), ('x', 'z', 'grow')...  13.3 us
    all_to_all x1, starting transfers between devices, work(): lax.all_to_all(slots.reshape((-1,) + slots.shape[2:]), ('x', 'z', 'grow')...  11.8 us
    ppermute x6, waiting for transfers between devices, shift(): lax.ppermute(block, axis, [(i, (i + step) % count) for i in range(count)])  9.17 us
    pallas_call x1, Pallas kernels, two_steps(): pl.pallas_call(steps_kernel, out_shape=(jax.ShapeDtypeStruct((2,) + phase...  7.61 us
    all_to_all x1, waiting for transfers between devices, work(): held = lax.all_to_all(slots, 'y', 0, 0, tiled=True)  7.57 us
    all_to_all x1, starting transfers between devices, work(): held = lax.all_to_all(slots, 'y', 0, 0, tiled=True)  3.36 us
  transfers between devices with their start and end apart: 9, of which 5 were waited for; matrix products, arithmetic and copies ran while one was open for 2% of the time, Pallas kernels for 0%

profile of v6, /device:TPU:1, one launch (start us, length us, event | category | flops | bytes accessed | tf_op | source)
XLA Modules:
  0.0 133.8 jit_solution(16402073358470590876)
XLA Ops:
  0.6 0.0 copy-start
  0.6 0.0 copy-start.1
  0.7 1.9 %fusion.1 = (f32[2,16,2,1536]{3,2,1,0:T(2,128)S(1)}, f32[2,16,2,1536]{3,2,1,0:T(2,128)S(1)}) fusion(f32[1,16,4,1536]{3,2,1,0:T(4,128)} %bitcast.18, f32[1,16,4,1536]{3,2,1,0:T(4,128)} %bitcast.20), kind=kLoop, calls=%fused_computation.8 | loop fusion | flops 196608 | bytes 1572864 | tf_op jit(solution)/shard_map/stack | solution.py:244
  2.5 0.0 copy-start.3
  2.5 0.0 copy-start.2
  2.5 4.8 %collective-permute-start = (f32[2,16,2,1536]{3,2,1,0:T(2,128)S(1)}, f32[2,16,2,1536]{3,2,1,0:T(2,128)S(1)}, u32[]{:S(2)}, u32[]{:S(2)}) collective-permute-start(f32[2,16,2,1536]{3,2,1,0:T(2,128)S(1)} %get-tuple-element.23), channel_id=1, source_target_pairs={{0,6},{6,12},{12,18},{18,24},{24,30},{30,36},{36,42},{42,48},{48,5... | collective-permute-start | bytes 1179656 | tf_op jit(solution)/shard_map/ppermute | solution.py:24
  7.4 10.6 %collective-permute-start.1 = (f32[2,16,2,1536]{3,2,1,0:T(2,128)S(1)}, f32[2,16,2,1536]{3,2,1,0:T(2,128)S(1)}, u32[]{:S(2)}, u32[]{:S(2)}) collective-permute-start(f32[2,16,2,1536]{3,2,1,0:T(2,128)S(1)} %get-tuple-element.22), channel_id=1, source_target_pairs={{0,762},{6,0},{12,6},{18,12},{24,18},{30,24},{36,30},{42,36},{48,4... | collective-permute-start | bytes 1179656 | tf_op jit(solution)/shard_map/ppermute | solution.py:24
  18.0 0.0 copy-done
  18.0 0.0 copy-done.1
  18.1 11.2 %collective-permute-start.2 = (f32[2,2,4,1536]{3,2,1,0:T(4,128)S(1)}, f32[2,2,4,1536]{3,2,1,0:T(4,128)S(1)}, u32[]{:S(2)}, u32[]{:S(2)}) collective-permute-start(f32[2,2,4,1536]{3,2,1,0:T(4,128)S(1)} %get-tuple-element.21), channel_id=1, source_target_pairs={{0,1},{1,2},{2,3},{3,4},{4,5},{5,0},{6,7},{7,8},{8,9},{9,10},{10,1... | collective-permute-start | bytes 294920 | tf_op jit(solution)/shard_map/ppermute | solution.py:24
  29.3 1.9 %collective-permute-start.3 = (f32[2,2,4,1536]{3,2,1,0:T(4,128)S(1)}, f32[2,2,4,1536]{3,2,1,0:T(4,128)S(1)}, u32[]{:S(2)}, u32[]{:S(2)}) collective-permute-start(f32[2,2,4,1536]{3,2,1,0:T(4,128)S(1)} %get-tuple-element.20), channel_id=1, source_target_pairs={{0,5},{1,0},{2,1},{3,2},{4,3},{5,4},{6,11},{7,6},{8,7},{9,8},{10,9... | collective-permute-start | bytes 294920 | tf_op jit(solution)/shard_map/ppermute | solution.py:24
  31.2 0.0 copy-done.3
  31.3 0.0 copy-done.2
  31.3 0.1 reshape.88
  31.4 0.2 dynamic-slice_reduce_fusion.1
  31.6 0.2 dynamic-slice_reduce_fusion
  31.9 0.6 pad_maximum_fusion.3.weights
  32.5 8.9 %collective-permute-done.3.above = f32[2,2,4,1536]{3,2,1,0:T(4,128)S(1)} collective-permute-done((f32[2,2,4,1536]{3,2,1,0:T(4,128)S(1)}, f32[2,2,4,1536]{3,2,1,0:T(4,128)S(1)}, u32[]{:S(2)}, u32[]{:S(2)}) %collective-permute-start.3) | collective-permute-done | bytes 98336 | tf_op jit(solution)/shard_map/ppermute | solution.py:24
  41.4 0.0 collective-permute-done.2.below
  41.5 1.9 %collective-permute-start.4 = (f32[2,2,1,1536]{3,2,1,0:T(1,128)S(1)}, f32[2,2,1,1536]{3,2,1,0:T(1,128)S(1)}, u32[]{:S(2)}, u32[]{:S(2)}) collective-permute-start(f32[2,2,1,1536]{3,2,1,0:T(1,128)S(1)} %get-tuple-element.25), channel_id=1, source_target_pairs={{0,6},{6,12},{12,18},{18,24},{24,30},{30,36},{36,42},{42,48},{48,5... | collective-permute-start | bytes 73736 | tf_op jit(solution)/shard_map/ppermute | solution.py:24
  43.4 9.4 %collective-permute-start.5 = (f32[2,2,1,1536]{3,2,1,0:T(1,128)S(1)}, f32[2,2,1,1536]{3,2,1,0:T(1,128)S(1)}, u32[]{:S(2)}, u32[]{:S(2)}) collective-permute-start(f32[2,2,1,1536]{3,2,1,0:T(1,128)S(1)} %get-tuple-element.24), channel_id=1, source_target_pairs={{0,762},{6,0},{12,6},{18,12},{24,18},{30,24},{36,30},{42,36},{48,4... | collective-permute-start | bytes 73736 | tf_op jit(solution)/shard_map/ppermute | solution.py:24
  52.8 0.7 pad_add_fusion.at
  53.5 0.0 collective-permute-done.4.edge_l
  53.5 0.3 collective-permute-done.5.edge_r
  53.7 0.0 collective-permute-done.left
  53.7 0.0 collective-permute-done.1.right
  53.7 7.6 %shard_map.67 = (f32[2,16,4,1536]{3,2,1,0:T(4,128)}, f32[6,4,128]{2,1,0:T(4,128)}) custom-call(s32[2]{0:T(128)} %pad_add_fusion.at, f32[16,4,1536]{2,1,0:T(4,128)} %phase.1, f32[16,4,1536]{2,1,0:T(4,128)} %solute.1, f32[2,16,2,1536]{3,2,1,0:T(2,128)S(1)} %collective-permute-done.left, f32[2,16,2,1536]{3,2,1,0:T(2,128)S(1)} %collective-permute-done.1.right, ...), custom_call_target="tpu_custom_call" | custom-call | tf_op jit(solution)/shard_map/pallas_call | solution.py:224
  61.4 0.0 copy-start.4
  61.4 1.5 %broadcast_select_fusion = f32[8,6,4,128]{3,2,1,0:T(4,128)} fusion(f32[6,4,128]{2,1,0:T(4,128)} %get-tuple-element.6, pred[8,6]{1,0:T(8,128)(4,1)S(1)} %iota_compare_fusion.1), kind=kLoop, calls=%fused_computation.16 | loop fusion | flops 24576 | bytes 110640 | tf_op jit(solution)/shard_map/jit(_where)/select_n | solution.py:267
  62.9 3.4 %all-to-all-start = ((f32[8,6,4,128]{3,2,1,0:T(4,128)}), f32[8,6,4,128]{3,2,1,0:T(4,128)S(1)}, u32[]{:S(2)}, u32[]{:S(2)}) async-start(f32[8,6,4,128]{3,2,1,0:T(4,128)} %broadcast_select_fusion), calls=%async_computation | async-start | bytes 196608 | tf_op jit(solution)/shard_map/all_to_all | solution.py:268
  66.3 7.6 %all-to-all-done = f32[8,6,4,128]{3,2,1,0:T(4,128)S(1)} async-done(((f32[8,6,4,128]{3,2,1,0:T(4,128)}), f32[8,6,4,128]{3,2,1,0:T(4,128)S(1)}, u32[]{:S(2)}, u32[]{:S(2)}) %all-to-all-start) | async-done | bytes 98336 | tf_op jit(solution)/shard_map/all_to_all | solution.py:268
  73.9 1.3 select_reduce_fusion
  75.2 11.8 %all-to-all-start.1 = ((f32[96,4,128]{2,1,0:T(4,128)}), f32[96,4,128]{2,1,0:T(4,128)S(1)}, u32[]{:S(2)}, u32[]{:S(2)}) async-start(f32[96,4,128]{2,1,0:T(4,128)} %bitcast.6), calls=%async_computation.1 | async-start | bytes 393216 | tf_op jit(solution)/shard_map/all_to_all | solution.py:276
  86.9 0.0 copy-done.4
  86.9 2.6 %collective-permute-start.6 = (f32[2,16,4,1536]{3,2,1,0:T(4,128)S(1)}, f32[2,16,4,1536]{3,2,1,0:T(4,128)S(1)}, u32[]{:S(2)}, u32[]{:S(2)}) collective-permute-start(f32[2,16,4,1536]{3,2,1,0:T(4,128)S(1)} %copy-done.4), channel_id=1, source_target_pairs={{1,0},{2,1},{3,2},{4,3},{5,4},{7,6},{8,7},{9,8},{10,9},{11,10},{13... | collective-permute-start | bytes 2359304 | tf_op jit(solution)/shard_map/ppermute | solution.py:260
  89.5 13.3 %all-to-all-done.1 = f32[96,4,128]{2,1,0:T(4,128)S(1)} async-done(((f32[96,4,128]{2,1,0:T(4,128)}), f32[96,4,128]{2,1,0:T(4,128)S(1)}, u32[]{:S(2)}, u32[]{:S(2)}) %all-to-all-start.1) | async-done | bytes 196640 | tf_op jit(solution)/shard_map/all_to_all | solution.py:276
  102.9 0.1 slice_bitcast_fusion.1
  103.0 0.6 pad_maximum_fusion.4
  103.6 29.2 %collective-permute-done.6 = f32[2,16,4,1536]{3,2,1,0:T(4,128)S(1)} collective-permute-done((f32[2,16,4,1536]{3,2,1,0:T(4,128)S(1)}, f32[2,16,4,1536]{3,2,1,0:T(4,128)S(1)}, u32[]{:S(2)}, u32[]{:S(2)}) %collective-permute-start.6) | collective-permute-done | bytes 786464 | tf_op jit(solution)/shard_map/ppermute | solution.py:260
  132.8 1.1 fusion.2
  (14 shorter events, 0.2 us)
Async XLA Ops:
  0.6 17.4 %copy-start = (f32[16,4,1536]{2,1,0:T(4,128)S(1)}, f32[16,4,1536]{2,1,0:T(4,128)}, u32[]{:S(2)}) copy-start(f32[16,4,1536]{2,1,0:T(4,128)} %phase.1) | copy-start | bytes 1179652
  0.6 17.4 %copy-start.1 = (f32[16,4,1536]{2,1,0:T(4,128)S(1)}, f32[16,4,1536]{2,1,0:T(4,128)}, u32[]{:S(2)}) copy-start(f32[16,4,1536]{2,1,0:T(4,128)} %solute.1) | copy-start | bytes 1179652
  2.5 28.7 %copy-start.3 = (s32[1536]{0:T(1024)S(1)}, s32[1536]{0:T(1024)}, u32[]{:S(2)}) copy-start(s32[1536]{0:T(1024)} %param.6) | copy-start | bytes 18436
  2.5 28.8 %copy-start.2 = (s32[6,128]{1,0:T(8,128)S(1)}, s32[6,128]{1,0:T(8,128)}, u32[]{:S(2)}) copy-start(s32[6,128]{1,0:T(8,128)} %param.7) | copy-start | bytes 9220
  2.5 51.2 %collective-permute-start = (f32[2,16,2,1536]{3,2,1,0:T(2,128)S(1)}, f32[2,16,2,1536]{3,2,1,0:T(2,128)S(1)}, u32[]{:S(2)}, u32[]{:S(2)}) collective-permute-start(f32[2,16,2,1536]{3,2,1,0:T(2,128)S(1)} %get-tuple-element.23), channel_id=1, source_target_pairs={{0,6},{6,12},{12,18},{18,24},{24,30},{30,36},{36,42},{42,48},{48,5... | collective-permute-start | bytes 1179656 | tf_op jit(solution)/shard_map/ppermute | solution.py:24
  7.4 46.4 %collective-permute-start.1 = (f32[2,16,2,1536]{3,2,1,0:T(2,128)S(1)}, f32[2,16,2,1536]{3,2,1,0:T(2,128)S(1)}, u32[]{:S(2)}, u32[]{:S(2)}) collective-permute-start(f32[2,16,2,1536]{3,2,1,0:T(2,128)S(1)} %get-tuple-element.22), channel_id=1, source_target_pairs={{0,762},{6,0},{12,6},{18,12},{24,18},{30,24},{36,30},{42,36},{48,4... | collective-permute-start | bytes 1179656 | tf_op jit(solution)/shard_map/ppermute | solution.py:24
  18.1 23.4 %collective-permute-start.2 = (f32[2,2,4,1536]{3,2,1,0:T(4,128)S(1)}, f32[2,2,4,1536]{3,2,1,0:T(4,128)S(1)}, u32[]{:S(2)}, u32[]{:S(2)}) collective-permute-start(f32[2,2,4,1536]{3,2,1,0:T(4,128)S(1)} %get-tuple-element.21), channel_id=1, source_target_pairs={{0,1},{1,2},{2,3},{3,4},{4,5},{5,0},{6,7},{7,8},{8,9},{9,10},{10,1... | collective-permute-start | bytes 294920 | tf_op jit(solution)/shard_map/ppermute | solution.py:24
  29.3 12.2 %collective-permute-start.3 = (f32[2,2,4,1536]{3,2,1,0:T(4,128)S(1)}, f32[2,2,4,1536]{3,2,1,0:T(4,128)S(1)}, u32[]{:S(2)}, u32[]{:S(2)}) collective-permute-start(f32[2,2,4,1536]{3,2,1,0:T(4,128)S(1)} %get-tuple-element.20), channel_id=1, source_target_pairs={{0,5},{1,0},{2,1},{3,2},{4,3},{5,4},{6,11},{7,6},{8,7},{9,8},{10,9... | collective-permute-start | bytes 294920 | tf_op jit(solution)/shard_map/ppermute | solution.py:24
  41.5 12.0 %collective-permute-start.4 = (f32[2,2,1,1536]{3,2,1,0:T(1,128)S(1)}, f32[2,2,1,1536]{3,2,1,0:T(1,128)S(1)}, u32[]{:S(2)}, u32[]{:S(2)}) collective-permute-start(f32[2,2,1,1536]{3,2,1,0:T(1,128)S(1)} %get-tuple-element.25), channel_id=1, source_target_pairs={{0,6},{6,12},{12,18},{18,24},{24,30},{30,36},{36,42},{42,48},{48,5... | collective-permute-start | bytes 73736 | tf_op jit(solution)/shard_map/ppermute | solution.py:24
  43.4 10.3 %collective-permute-start.5 = (f32[2,2,1,1536]{3,2,1,0:T(1,128)S(1)}, f32[2,2,1,1536]{3,2,1,0:T(1,128)S(1)}, u32[]{:S(2)}, u32[]{:S(2)}) collective-permute-start(f32[2,2,1,1536]{3,2,1,0:T(1,128)S(1)} %get-tuple-element.24), channel_id=1, source_target_pairs={{0,762},{6,0},{12,6},{18,12},{24,18},{30,24},{36,30},{42,36},{48,4... | collective-permute-start | bytes 73736 | tf_op jit(solution)/shard_map/ppermute | solution.py:24
  61.4 25.6 %copy-start.4 = (f32[2,16,4,1536]{3,2,1,0:T(4,128)S(1)}, f32[2,16,4,1536]{3,2,1,0:T(4,128)}, u32[]{:S(2)}) copy-start(f32[2,16,4,1536]{3,2,1,0:T(4,128)} %get-tuple-element.5) | copy-start | bytes 2359300
  62.9 11.0 %all-to-all-start = ((f32[8,6,4,128]{3,2,1,0:T(4,128)}), f32[8,6,4,128]{3,2,1,0:T(4,128)S(1)}, u32[]{:S(2)}, u32[]{:S(2)}) async-start(f32[8,6,4,128]{3,2,1,0:T(4,128)} %broadcast_select_fusion), calls=%async_computation | async-start | bytes 196608 | tf_op jit(solution)/shard_map/all_to_all | solution.py:268
  75.2 27.7 %all-to-all-start.1 = ((f32[96,4,128]{2,1,0:T(4,128)}), f32[96,4,128]{2,1,0:T(4,128)S(1)}, u32[]{:S(2)}, u32[]{:S(2)}) async-start(f32[96,4,128]{2,1,0:T(4,128)} %bitcast.6), calls=%async_computation.1 | async-start | bytes 393216 | tf_op jit(solution)/shard_map/all_to_all | solution.py:276
  86.9 45.8 %collective-permute-start.6 = (f32[2,16,4,1536]{3,2,1,0:T(4,128)S(1)}, f32[2,16,4,1536]{3,2,1,0:T(4,128)S(1)}, u32[]{:S(2)}, u32[]{:S(2)}) collective-permute-start(f32[2,16,4,1536]{3,2,1,0:T(4,128)S(1)} %copy-done.4), channel_id=1, source_target_pairs={{1,0},{2,1},{3,2},{4,3},{5,4},{7,6},{8,7},{9,8},{10,9},{11,10},{13... | collective-permute-start | bytes 2359304 | tf_op jit(solution)/shard_map/ppermute | solution.py:260

commit v7 on v5

--- a/solution.py
+++ b/solution.py
@@ -22,6 +22,12 @@
 def shift(block, axis, step):
     count = lax.axis_size(axis)
     return lax.ppermute(block, axis, [(i, (i + step) % count) for i in range(count)])
+
+
+def fields(phase, solute, like):
+    return jnp.stack(
+        [jnp.full(like.shape[1:], phase, jnp.float32), jnp.full(like.shape[1:], solute, jnp.float32)]
+    )
 
 
 def near(block):
@@ -89,10 +95,10 @@
         o[last, rows:] = jnp.where(highest, liquid, above[field, 1])
         d[0] = jnp.zeros((2 * rows, width), jnp.float32)
         d[last] = jnp.zeros((2 * rows, width), jnp.float32)
-        d[0, rows : rows + 1] = jnp.where(lowest, solid, edge_r[field, 0])
-        d[0, 2 * rows - 1 :] = jnp.where(lowest, solid, edge_l[field, 0])
-        d[last, 0:1] = jnp.where(highest, liquid, edge_r[field, 1])
-        d[last, rows - 1 : rows] = jnp.where(highest, liquid, edge_l[field, 1])
+        d[0, rows : rows + 1] = edge_r[field, 0]
+        d[0, 2 * rows - 1 :] = edge_l[field, 0]
+        d[last, 0:1] = edge_r[field, 1]
+        d[last, rows - 1 : rows] = edge_l[field, 1]
 
     def gather(k, carry):
         for field, (own, o, d) in enumerate(((phase, op, dp), (solute, ou, du))):
@@ -239,14 +245,23 @@
     grow_count = lax.axis_size("grow")
     grow_at = lax.axis_index("grow")
     lat_at = lax.axis_index(LAT)
-    lat_count = lax.axis_size(LAT)
+    x_count, y_count, z_count = (lax.axis_size(axis) for axis in LAT)
+    x_at, y_at, z_at = (lax.axis_index(axis) for axis in LAT)
     state = jnp.stack([phase, solute])
 
     below = shift(state[:, -2:], "grow", 1)
     above = shift(state[:, :2], "grow", -1)
     left = shift(state[:, :, -2:], LAT, 1)
     right = shift(state[:, :, :2], LAT, -1)
-    edges = jnp.concatenate([below[:, 1:], above[:, :1]], axis=1)
+    lowest = grow_at == 0
+    highest = grow_at == grow_count - 1
+    edges = jnp.concatenate(
+        [
+            jnp.where(lowest, fields(1.0, solid_u, below[:, 1:]), below[:, 1:]),
+            jnp.where(highest, fields(-1.0, liquid_u, above[:, :1]), above[:, :1]),
+        ],
+        axis=1,
+    )
     edge_l = shift(edges[:, :, -1:], LAT, 1)
     edge_r = shift(edges[:, :, :1], LAT, -1)
 
@@ -267,8 +282,17 @@
     solute_out = jnp.where(top, liquid_u, arrived[1])
     row_ids = lax.dynamic_index_in_dim(writer, grow_at, 0, keepdims=False)
     target = lax.dynamic_index_in_dim(row_ids, lat_at, 0, keepdims=False)
-    slots = jnp.where((jnp.arange(lat_count) == target)[:, None, None], mine[None], 0.0)
-    landed = lax.all_to_all(slots, LAT, 0, 0, tiled=True).sum(axis=0)
+    to_y = jnp.arange(y_count) == target // z_count % y_count
+    slots = jnp.where(to_y[:, None, None], mine[None], 0.0)
+    held = lax.all_to_all(slots, "y", 0, 0, tiled=True)
+    onward = row_ids.reshape(x_count, y_count, z_count)
+    onward = lax.dynamic_index_in_dim(onward, x_at, 0, keepdims=False)
+    onward = lax.dynamic_index_in_dim(onward, z_at, 1, keepdims=False)
+    place = onward // (y_count * z_count) * z_count + onward % z_count
+    place = jnp.where(onward // z_count % y_count == y_at, place, -1)
+    chosen = jnp.arange(x_count * z_count)[:, None] == place[None]
+    slots = jnp.where(chosen[:, :, None, None], held[None], 0.0).sum(axis=1)
+    landed = lax.all_to_all(slots, ("x", "z"), 0, 0, tiled=True).sum(axis=0)
     piece = width // 4 // grow_count
     landed = jnp.stack([landed[:, :piece], landed[:, piece:]])
     return (phase_out, solute_out, landed[None, None, :, :, None])

time: 111 us -> 116 us (1.045)
  blocking collectives: 0 us -> 26.6 us
  waiting for transfers between devices: 31.5 us -> 16.1 us
  starting transfers between devices: 60.9 us -> 51.8 us
  between operations: 0.92 us -> 3.61 us
    all_to_all x0 -> x1, blocking collectives: none -> 26.6 us  [work(): landed = lax.all_to_all(slots, ('x', 'z'), 0, 0, tiled=True).sum(axis=0)]
    ppermute x1, waiting for transfers between devices: 16.1 us -> 0.01 us  [work(): lax.ppermute(state, 'grow', [(i, i - 1) for i in range(1, grow_count)])]
    ppermute x6, waiting for transfers between devices: 4.11 us -> 9.4 us  [shift(): lax.ppermute(block, axis, [(i, (i + step) % count) for i in range(count)])]
    all_to_all x1, starting transfers between devices: 8.56 us -> 3.34 us  [work(): held = lax.all_to_all(slots, 'y', 0, 0, tiled=True)]
    all_to_all x1, waiting for transfers between devices: 11.2 us -> 6.67 us  [work(): held = lax.all_to_all(slots, 'y', 0, 0, tiled=True)]
    ppermute x2, starting transfers between devices: 7.8 us -> 5.14 us  [work(): lax.ppermute(rows_of[step], 'grow', [(0, 2 * step), (1, 2 * step + 1)])]
    ppermute x1, starting transfers between devices: 3.68 us -> 2.04 us  [work(): lax.ppermute(state, 'grow', [(i, i - 1) for i in range(1, grow_count)])]
  transfers between devices with their start and end apart: 11 -> 11, of which waited for: 3 -> 2; matrix products, arithmetic and copies ran while one was open for 5% -> 5% of each run, Pallas kernels for 0% -> 0%
where the time goes in v7:
time: 116 us; the launch traced here: 115 us
  starting transfers between devices  51.8 us (45%)
  blocking collectives  26.6 us (23%)
  waiting for transfers between devices  16.1 us (14%)
  Pallas kernels  7.61 us (7%)
  other arithmetic  5.85 us (5%)
  local copies, waits for them, and re-layouts  3.75 us (3%)
  between operations  3.61 us (3%)
    ppermute x6, starting transfers between devices, shift(): lax.ppermute(block, axis, [(i, (i + step) % count) for i in range(count)])  40 us
    all_to_all x1, blocking collectives, work(): landed = lax.all_to_all(slots, ('x', 'z'), 0, 0, tiled=True).sum(axis=0)  26.6 us
    ppermute x6, waiting for transfers between devices, shift(): lax.ppermute(block, axis, [(i, (i + step) % count) for i in range(count)])  9.4 us
    pallas_call x1, Pallas kernels, two_steps(): pl.pallas_call(steps_kernel, out_shape=(jax.ShapeDtypeStruct((2,) + phase...  7.61 us
    all_to_all x1, waiting for transfers between devices, work(): held = lax.all_to_all(slots, 'y', 0, 0, tiled=True)  6.67 us
    ppermute x2, starting transfers between devices, work(): lax.ppermute(rows_of[step], 'grow', [(0, 2 * step), (1, 2 * step + 1)])  5.14 us
    all_to_all x1, starting transfers between devices, work(): held = lax.all_to_all(slots, 'y', 0, 0, tiled=True)  3.34 us
  transfers between devices with their start and end apart: 11, of which 2 were waited for; matrix products, arithmetic and copies ran while one was open for 5% of the time, Pallas kernels for 0%

profile of v7, /device:TPU:1, one launch (start us, length us, event | category | flops | bytes accessed | tf_op | source)
XLA Modules:
  0.0 115.3 jit_solution(17065878744381436)
XLA Ops:
  0.6 0.0 copy-start
  0.6 0.0 copy-start.1
  0.7 1.9 %fusion.1 = (f32[2,16,2,1536]{3,2,1,0:T(2,128)S(1)}, f32[2,16,2,1536]{3,2,1,0:T(2,128)S(1)}) fusion(f32[1,16,4,1536]{3,2,1,0:T(4,128)} %bitcast.25, f32[1,16,4,1536]{3,2,1,0:T(4,128)} %bitcast.27), kind=kLoop, calls=%fused_computation.7 | loop fusion | flops 196608 | bytes 1572864 | tf_op jit(solution)/shard_map/stack | solution.py:250
  2.5 4.8 %collective-permute-start = (f32[2,16,2,1536]{3,2,1,0:T(2,128)S(1)}, f32[2,16,2,1536]{3,2,1,0:T(2,128)S(1)}, u32[]{:S(2)}, u32[]{:S(2)}) collective-permute-start(f32[2,16,2,1536]{3,2,1,0:T(2,128)S(1)} %get-tuple-element.20), channel_id=1, source_target_pairs={{0,6},{6,12},{12,18},{18,24},{24,30},{30,36},{36,42},{42,48},{48,5... | collective-permute-start | bytes 1179656 | tf_op jit(solution)/shard_map/ppermute | solution.py:24
  7.3 10.6 %collective-permute-start.1 = (f32[2,16,2,1536]{3,2,1,0:T(2,128)S(1)}, f32[2,16,2,1536]{3,2,1,0:T(2,128)S(1)}, u32[]{:S(2)}, u32[]{:S(2)}) collective-permute-start(f32[2,16,2,1536]{3,2,1,0:T(2,128)S(1)} %get-tuple-element.19), channel_id=1, source_target_pairs={{0,762},{6,0},{12,6},{18,12},{24,18},{30,24},{36,30},{42,36},{48,4... | collective-permute-start | bytes 1179656 | tf_op jit(solution)/shard_map/ppermute | solution.py:24
  18.0 0.0 copy-done
  18.0 0.0 copy-done.1
  18.0 0.0 copy-start.5
  18.1 0.0 copy-start.3
  18.1 11.3 %collective-permute-start.2 = (f32[2,2,4,1536]{3,2,1,0:T(4,128)S(1)}, f32[2,2,4,1536]{3,2,1,0:T(4,128)S(1)}, u32[]{:S(2)}, u32[]{:S(2)}) collective-permute-start(f32[2,2,4,1536]{3,2,1,0:T(4,128)S(1)} %get-tuple-element.18), channel_id=1, source_target_pairs={{0,1},{1,2},{2,3},{3,4},{4,5},{5,0},{6,7},{7,8},{8,9},{9,10},{10,1... | collective-permute-start | bytes 294920 | tf_op jit(solution)/shard_map/ppermute | solution.py:24
  29.4 1.9 %collective-permute-start.3 = (f32[2,2,4,1536]{3,2,1,0:T(4,128)S(1)}, f32[2,2,4,1536]{3,2,1,0:T(4,128)S(1)}, u32[]{:S(2)}, u32[]{:S(2)}) collective-permute-start(f32[2,2,4,1536]{3,2,1,0:T(4,128)S(1)} %get-tuple-element.17), channel_id=1, source_target_pairs={{0,5},{1,0},{2,1},{3,2},{4,3},{5,4},{6,11},{7,6},{8,7},{9,8},{10,9... | collective-permute-start | bytes 294920 | tf_op jit(solution)/shard_map/ppermute | solution.py:24
  31.3 0.0 copy-done.5
  31.4 0.6 pad_maximum_fusion.3.weights
  32.0 9.4 %collective-permute-done.3.above = f32[2,2,4,1536]{3,2,1,0:T(4,128)S(1)} collective-permute-done((f32[2,2,4,1536]{3,2,1,0:T(4,128)S(1)}, f32[2,2,4,1536]{3,2,1,0:T(4,128)S(1)}, u32[]{:S(2)}, u32[]{:S(2)}) %collective-permute-start.3) | collective-permute-done | bytes 98336 | tf_op jit(solution)/shard_map/ppermute | solution.py:24
  41.4 0.0 copy-done.3
  41.4 0.0 collective-permute-done.2.below
  41.4 0.0 copy-done.2
  41.5 1.9 %collective-permute-start.4 = (f32[2,2,1,1536]{3,2,1,0:T(1,128)S(1)}, f32[2,2,1,1536]{3,2,1,0:T(1,128)S(1)}, u32[]{:S(2)}, u32[]{:S(2)}) collective-permute-start(f32[2,2,1,1536]{3,2,1,0:T(1,128)S(1)} %get-tuple-element.22), channel_id=1, source_target_pairs={{0,6},{6,12},{12,18},{18,24},{24,30},{30,36},{36,42},{42,48},{48,5... | collective-permute-start | bytes 73736 | tf_op jit(solution)/shard_map/ppermute | solution.py:24
  43.4 9.4 %collective-permute-start.5 = (f32[2,2,1,1536]{3,2,1,0:T(1,128)S(1)}, f32[2,2,1,1536]{3,2,1,0:T(1,128)S(1)}, u32[]{:S(2)}, u32[]{:S(2)}) collective-permute-start(f32[2,2,1,1536]{3,2,1,0:T(1,128)S(1)} %get-tuple-element.21), channel_id=1, source_target_pairs={{0,762},{6,0},{12,6},{18,12},{24,18},{30,24},{36,30},{42,36},{48,4... | collective-permute-start | bytes 73736 | tf_op jit(solution)/shard_map/ppermute | solution.py:24
  52.8 0.7 pad_add_fusion.at
  53.5 0.7 dynamic-slice_reduce_fusion.1
  54.2 0.1 reshape.121
  54.3 0.2 dynamic-slice_reduce_fusion
  54.5 0.0 collective-permute-done.4.edge_l
  54.5 0.0 collective-permute-done.5.edge_r
  54.5 0.0 collective-permute-done.left
  54.5 0.0 collective-permute-done.1.right
  54.5 7.6 %shard_map.67 = (f32[2,16,4,1536]{3,2,1,0:T(4,128)}, f32[6,4,128]{2,1,0:T(4,128)}) custom-call(s32[2]{0:T(128)} %pad_add_fusion.at, f32[16,4,1536]{2,1,0:T(4,128)} %phase.1, f32[16,4,1536]{2,1,0:T(4,128)} %solute.1, f32[2,16,2,1536]{3,2,1,0:T(2,128)S(1)} %collective-permute-done.left, f32[2,16,2,1536]{3,2,1,0:T(2,128)S(1)} %collective-permute-done.1.right, ...), custom_call_target="tpu_custom_call" | custom-call | tf_op jit(solution)/shard_map/pallas_call | solution.py:230
  62.2 0.7 slice.62
  62.8 1.3 %collective-permute-start.7 = (f32[3,4,128]{2,1,0:T(4,128)S(1)}, f32[3,4,128]{2,1,0:T(4,128)S(1)}, u32[]{:S(2)}, u32[]{:S(2)}) collective-permute-start(f32[3,4,128]{2,1,0:T(4,128)S(1)} %slice.62), channel_id=1, source_target_pairs={{0,1},{6,7},{12,13},{18,19},{24,25},{30,31},{36,37},{42,43},{48,49... | collective-permute-start | bytes 18440 | tf_op jit(solution)/shard_map/ppermute | solution.py:274
  64.2 1.3 %dynamic_slice.16 = s32[1,1]{1,0:T(1,128)} dynamic-slice(s32[6,128]{1,0:T(8,128)} %param.7, s32[]{:T(128)S(6)} %select_n.164, s32[]{:T(128)S(6)} %select_n.166), dynamic_slice_sizes={1,1} | dynamic-slice | bytes 12 | tf_op jit(solution)/shard_map/jit(dynamic_index_in_dim)/dynamic_slice | solution.py:284
  68.1 0.0 copy-start.4
  68.1 0.0 collective-permute-done.7
  68.1 0.7 copy-done.4
  68.8 2.3 %collective-permute-start.9 = (f32[4,128]{1,0:T(4,128)S(1)}, f32[4,128]{1,0:T(4,128)S(1)}, u32[]{:S(2)}, u32[]{:S(2)}) collective-permute-start(f32[4,128]{1,0:T(4,128)S(1)} %get-tuple-element.24), channel_id=1, source_target_pairs={{0,4},{1,5},{6,10},{7,11},{12,16},{13,17},{18,22},{19,23},{24,28},... | collective-permute-start | bytes 6152 | tf_op jit(solution)/shard_map/ppermute | solution.py:278
  71.0 2.9 %collective-permute-start.8 = (f32[4,128]{1,0:T(4,128)S(1)}, f32[4,128]{1,0:T(4,128)S(1)}, u32[]{:S(2)}, u32[]{:S(2)}) collective-permute-start(f32[4,128]{1,0:T(4,128)S(1)} %get-tuple-element.23), channel_id=1, source_target_pairs={{0,2},{1,3},{6,8},{7,9},{12,14},{13,15},{18,20},{19,21},{24,26},{2... | collective-permute-start | bytes 6152 | tf_op jit(solution)/shard_map/ppermute | solution.py:278
  73.9 2.0 %collective-permute-start.6 = (f32[2,16,4,1536]{3,2,1,0:T(4,128)}, f32[2,16,4,1536]{3,2,1,0:T(4,128)S(1)}, u32[]{:S(2)}, u32[]{:S(2)}) collective-permute-start(f32[2,16,4,1536]{3,2,1,0:T(4,128)} %get-tuple-element.5), channel_id=1, source_target_pairs={{1,0},{2,1},{3,2},{4,3},{5,4},{7,6},{8,7},{9,8},{10,9},{11,10},{13... | collective-permute-start | bytes 2359304 | tf_op jit(solution)/shard_map/ppermute | solution.py:279
  76.0 0.0 collective-permute-done.9
  76.0 0.0 collective-permute-done.8
  76.0 0.7 broadcast_select_fusion
  76.7 3.3 %all-to-all-start = ((f32[8,4,128]{2,1,0:T(4,128)}), f32[8,4,128]{2,1,0:T(4,128)S(1)}, u32[]{:S(2)}, u32[]{:S(2)}) async-start(f32[8,4,128]{2,1,0:T(4,128)} %broadcast_select_fusion), calls=%async_computation | async-start | bytes 32768 | tf_op jit(solution)/shard_map/all_to_all | solution.py:287
  80.1 6.7 %all-to-all-done = f32[8,4,128]{2,1,0:T(4,128)S(1)} async-done(((f32[8,4,128]{2,1,0:T(4,128)}), f32[8,4,128]{2,1,0:T(4,128)S(1)}, u32[]{:S(2)}, u32[]{:S(2)}) %all-to-all-start) | async-done | bytes 16416 | tf_op jit(solution)/shard_map/all_to_all | solution.py:287
  86.7 0.2 select_reduce_fusion
  86.9 26.6 %all_to_all.10 = f32[16,4,128]{2,1,0:T(4,128)S(1)} all-to-all(f32[16,4,128]{2,1,0:T(4,128)S(1)} %select_reduce_fusion), channel_id=1, replica_groups=mesh['x'=4,'y'=8,'z'=4,'grow'=6] {'x','z'}, dimensions={0} | all-to-all | bytes 65536 | tf_op jit(solution)/shard_map/all_to_all | solution.py:295
  113.5 0.1 slice_bitcast_fusion.3
  113.6 0.6 pad_maximum_fusion.4
  114.2 0.0 collective-permute-done.6
  114.2 1.1 fusion.2
  (17 shorter events, 0.2 us)
Async XLA Ops:
  0.6 17.4 %copy-start = (f32[16,4,1536]{2,1,0:T(4,128)S(1)}, f32[16,4,1536]{2,1,0:T(4,128)}, u32[]{:S(2)}) copy-start(f32[16,4,1536]{2,1,0:T(4,128)} %phase.1) | copy-start | bytes 1179652
  0.6 17.4 %copy-start.1 = (f32[16,4,1536]{2,1,0:T(4,128)S(1)}, f32[16,4,1536]{2,1,0:T(4,128)}, u32[]{:S(2)}) copy-start(f32[16,4,1536]{2,1,0:T(4,128)} %solute.1) | copy-start | bytes 1179652
  2.5 52.0 %collective-permute-start = (f32[2,16,2,1536]{3,2,1,0:T(2,128)S(1)}, f32[2,16,2,1536]{3,2,1,0:T(2,128)S(1)}, u32[]{:S(2)}, u32[]{:S(2)}) collective-permute-start(f32[2,16,2,1536]{3,2,1,0:T(2,128)S(1)} %get-tuple-element.20), channel_id=1, source_target_pairs={{0,6},{6,12},{12,18},{18,24},{24,30},{30,36},{36,42},{42,48},{48,5... | collective-permute-start | bytes 1179656 | tf_op jit(solution)/shard_map/ppermute | solution.py:24
  7.3 47.2 %collective-permute-start.1 = (f32[2,16,2,1536]{3,2,1,0:T(2,128)S(1)}, f32[2,16,2,1536]{3,2,1,0:T(2,128)S(1)}, u32[]{:S(2)}, u32[]{:S(2)}) collective-permute-start(f32[2,16,2,1536]{3,2,1,0:T(2,128)S(1)} %get-tuple-element.19), channel_id=1, source_target_pairs={{0,762},{6,0},{12,6},{18,12},{24,18},{30,24},{36,30},{42,36},{48,4... | collective-permute-start | bytes 1179656 | tf_op jit(solution)/shard_map/ppermute | solution.py:24
  18.0 13.3 %copy-start.5 = (s32[1536]{0:T(1024)S(1)}, s32[1536]{0:T(1024)}, u32[]{:S(2)}) copy-start(s32[1536]{0:T(1024)} %param.6) | copy-start | bytes 18436
  18.1 23.3 %copy-start.3 = (f32[2,1,4,1536]{3,2,1,0:T(4,128)S(1)}, f32[2,1,4,1536]{3,2,1,0:T(4,128)}, u32[]{:S(2)}) copy-start(f32[2,1,4,1536]{3,2,1,0:T(4,128)} %constant.128.clone.1) | copy-start | bytes 147460
  18.1 23.3 %collective-permute-start.2 = (f32[2,2,4,1536]{3,2,1,0:T(4,128)S(1)}, f32[2,2,4,1536]{3,2,1,0:T(4,128)S(1)}, u32[]{:S(2)}, u32[]{:S(2)}) collective-permute-start(f32[2,2,4,1536]{3,2,1,0:T(4,128)S(1)} %get-tuple-element.18), channel_id=1, source_target_pairs={{0,1},{1,2},{2,3},{3,4},{4,5},{5,0},{6,7},{7,8},{8,9},{9,10},{10,1... | collective-permute-start | bytes 294920 | tf_op jit(solution)/shard_map/ppermute | solution.py:24
  29.4 12.0 %collective-permute-start.3 = (f32[2,2,4,1536]{3,2,1,0:T(4,128)S(1)}, f32[2,2,4,1536]{3,2,1,0:T(4,128)S(1)}, u32[]{:S(2)}, u32[]{:S(2)}) collective-permute-start(f32[2,2,4,1536]{3,2,1,0:T(4,128)S(1)} %get-tuple-element.17), channel_id=1, source_target_pairs={{0,5},{1,0},{2,1},{3,2},{4,3},{5,4},{6,11},{7,6},{8,7},{9,8},{10,9... | collective-permute-start | bytes 294920 | tf_op jit(solution)/shard_map/ppermute | solution.py:24
  32.0 9.4 %copy-start.2 = (f32[2,1,4,1536]{3,2,1,0:T(4,128)S(1)}, f32[2,1,4,1536]{3,2,1,0:T(4,128)}, u32[]{:S(2)}) copy-start(f32[2,1,4,1536]{3,2,1,0:T(4,128)} %constant.127.clone.1) | copy-start | bytes 147460
  41.5 13.0 %collective-permute-start.4 = (f32[2,2,1,1536]{3,2,1,0:T(1,128)S(1)}, f32[2,2,1,1536]{3,2,1,0:T(1,128)S(1)}, u32[]{:S(2)}, u32[]{:S(2)}) collective-permute-start(f32[2,2,1,1536]{3,2,1,0:T(1,128)S(1)} %get-tuple-element.22), channel_id=1, source_target_pairs={{0,6},{6,12},{12,18},{18,24},{24,30},{30,36},{36,42},{42,48},{48,5... | collective-permute-start | bytes 73736 | tf_op jit(solution)/shard_map/ppermute | solution.py:24
  43.4 11.1 %collective-permute-start.5 = (f32[2,2,1,1536]{3,2,1,0:T(1,128)S(1)}, f32[2,2,1,1536]{3,2,1,0:T(1,128)S(1)}, u32[]{:S(2)}, u32[]{:S(2)}) collective-permute-start(f32[2,2,1,1536]{3,2,1,0:T(1,128)S(1)} %get-tuple-element.21), channel_id=1, source_target_pairs={{0,762},{6,0},{12,6},{18,12},{24,18},{30,24},{36,30},{42,36},{48,4... | collective-permute-start | bytes 73736 | tf_op jit(solution)/shard_map/ppermute | solution.py:24
  62.8 5.2 %collective-permute-start.7 = (f32[3,4,128]{2,1,0:T(4,128)S(1)}, f32[3,4,128]{2,1,0:T(4,128)S(1)}, u32[]{:S(2)}, u32[]{:S(2)}) collective-permute-start(f32[3,4,128]{2,1,0:T(4,128)S(1)} %slice.62), channel_id=1, source_target_pairs={{0,1},{6,7},{12,13},{18,19},{24,25},{30,31},{36,37},{42,43},{48,49... | collective-permute-start | bytes 18440 | tf_op jit(solution)/shard_map/ppermute | solution.py:274
  68.1 0.7 copy-start.4
  68.8 7.2 %collective-permute-start.9 = (f32[4,128]{1,0:T(4,128)S(1)}, f32[4,128]{1,0:T(4,128)S(1)}, u32[]{:S(2)}, u32[]{:S(2)}) collective-permute-start(f32[4,128]{1,0:T(4,128)S(1)} %get-tuple-element.24), channel_id=1, source_target_pairs={{0,4},{1,5},{6,10},{7,11},{12,16},{13,17},{18,22},{19,23},{24,28},... | collective-permute-start | bytes 6152 | tf_op jit(solution)/shard_map/ppermute | solution.py:278
  71.0 5.0 %collective-permute-start.8 = (f32[4,128]{1,0:T(4,128)S(1)}, f32[4,128]{1,0:T(4,128)S(1)}, u32[]{:S(2)}, u32[]{:S(2)}) collective-permute-start(f32[4,128]{1,0:T(4,128)S(1)} %get-tuple-element.23), channel_id=1, source_target_pairs={{0,2},{1,3},{6,8},{7,9},{12,14},{13,15},{18,20},{19,21},{24,26},{2... | collective-permute-start | bytes 6152 | tf_op jit(solution)/shard_map/ppermute | solution.py:278
  73.9 40.2 %collective-permute-start.6 = (f32[2,16,4,1536]{3,2,1,0:T(4,128)}, f32[2,16,4,1536]{3,2,1,0:T(4,128)S(1)}, u32[]{:S(2)}, u32[]{:S(2)}) collective-permute-start(f32[2,16,4,1536]{3,2,1,0:T(4,128)} %get-tuple-element.5), channel_id=1, source_target_pairs={{1,0},{2,1},{3,2},{4,3},{5,4},{7,6},{8,7},{9,8},{10,9},{11,10},{13... | collective-permute-start | bytes 2359304 | tf_op jit(solution)/shard_map/ppermute | solution.py:279
  76.7 10.0 %all-to-all-start = ((f32[8,4,128]{2,1,0:T(4,128)}), f32[8,4,128]{2,1,0:T(4,128)S(1)}, u32[]{:S(2)}, u32[]{:S(2)}) async-start(f32[8,4,128]{2,1,0:T(4,128)} %broadcast_select_fusion), calls=%async_computation | async-start | bytes 32768 | tf_op jit(solution)/shard_map/all_to_all | solution.py:287

commit v8 on v7

--- a/solution.py
+++ b/solution.py
@@ -68,7 +68,7 @@
 
 
 def steps_kernel(
-    at, phase, solute, left, right, below, above, edge_l, edge_r, weights, state_to, coarse_to,
+    at, phase, solute, left, right, below, above, edge_l, edge_r, weights, state_to, slots_to,
     op, ou, dp, du, opr, our, dpr, dur, sp, su, spr, sur, tpr, tur, sums,
 ):
     planes, rows, width = phase.shape
@@ -193,7 +193,8 @@
 
     lax.fori_loop(0, pairs, own_twice, 0)
 
-    pieces = coarse_to.shape[0]
+    y_count = slots_to.shape[0]
+    pieces = slots_to.shape[1] * slots_to.shape[2]
     per = chunks // pieces
     span = per * LANES
     pick = (
@@ -219,10 +220,12 @@
             )
             total_cells = got if total_cells is None else total_cells + got
     for r in range(pieces):
-        coarse_to[r] = total_cells[r * (pairs // 2) : (r + 1) * (pairs // 2)]
-
-
-def two_steps(at, phase, solute, left, right, below, above, edge_l, edge_r, weights, pieces, interpret=False):
+        block = total_cells[r * (pairs // 2) : (r + 1) * (pairs // 2)]
+        for y in range(y_count):
+            slots_to[y, r % 2, r // 2] = jnp.where(at[2 + r] == y, block, 0.0)
+
+
+def two_steps(at, phase, solute, left, right, below, above, edge_l, edge_r, weights, pieces, y_count, interpret=False):
     planes, rows, width = phase.shape
     pairs = planes // 2
     vmem = pl.BlockSpec(memory_space=pltpu.VMEM)
@@ -231,7 +234,7 @@
         steps_kernel,
         out_shape=(
             jax.ShapeDtypeStruct((2,) + phase.shape, jnp.float32),
-            jax.ShapeDtypeStruct((pieces, pairs // 2, LANES), jnp.float32),
+            jax.ShapeDtypeStruct((y_count, 2, pieces // 2, pairs // 2, LANES), jnp.float32),
         ),
         in_specs=[pl.BlockSpec(memory_space=pltpu.SMEM)] + [vmem] * 9,
         out_specs=(vmem, vmem),
@@ -267,24 +270,24 @@
 
     turned = seed_grain > 0
     weights = jnp.stack([jnp.where(turned, 0.5, 1.0), jnp.where(turned, 2.0, -2.0)]).astype(jnp.float32)
-    at = jnp.stack([grow_at, jnp.int32(grow_count)]).astype(jnp.int32)
+    targets = lax.dynamic_index_in_dim(writer, lat_at, 1, keepdims=False)
+    at = jnp.concatenate([jnp.stack([grow_at, jnp.int32(grow_count)]), targets // z_count % y_count])
     halos = tuple(near(halo) for halo in (left, right, below, above, edge_l, edge_r))
-    state, blocks = two_steps(at, phase, solute, *halos, weights, grow_count)
-
-    odd = lax.ppermute(blocks[1::2], "grow", [(0, 1)])
-    rows_of = jnp.where(grow_at == 0, blocks[0::2], odd)
-    mine = jnp.where(grow_at < 2, rows_of[0], 0.0)
-    for step in range(1, grow_count // 2):
-        mine = mine + lax.ppermute(rows_of[step], "grow", [(0, 2 * step), (1, 2 * step + 1)])
+    state, slots = two_steps(at, phase, solute, *halos, weights, grow_count, y_count)
+
     arrived = lax.ppermute(state, "grow", [(i, i - 1) for i in range(1, grow_count)])
     top = grow_at == grow_count - 1
     phase_out = jnp.where(top, -1.0, arrived[0])
     solute_out = jnp.where(top, liquid_u, arrived[1])
+
+    held = lax.all_to_all(slots, "y", 0, 0, tiled=True)
+    odd = lax.ppermute(held[:, 1], "grow", [(0, 1)])
+    rows_of = jnp.where(grow_at == 0, held[:, 0], odd)
+    mine = jnp.where(grow_at < 2, rows_of[:, 0], 0.0)
+    for step in range(1, grow_count // 2):
+        mine = mine + lax.ppermute(rows_of[:, step], "grow", [(0, 2 * step), (1, 2 * step + 1)])
+    held = mine
     row_ids = lax.dynamic_index_in_dim(writer, grow_at, 0, keepdims=False)
-    target = lax.dynamic_index_in_dim(row_ids, lat_at, 0, keepdims=False)
-    to_y = jnp.arange(y_count) == target // z_count % y_count
-    slots = jnp.where(to_y[:, None, None], mine[None], 0.0)
-    held = lax.all_to_all(slots, "y", 0, 0, tiled=True)
     onward = row_ids.reshape(x_count, y_count, z_count)
     onward = lax.dynamic_index_in_dim(onward, x_at, 0, keepdims=False)
     onward = lax.dynamic_index_in_dim(onward, z_at, 1, keepdims=False)

time: 116 us -> 112 us (0.966)
  the two profiles are of different devices: /device:TPU:1 before, /device:TPU:8 now
where the time goes in v8:
time: 112 us; the launch traced here: 111 us
  starting transfers between devices  51.3 us (46%)
  blocking collectives  32.8 us (29%)
  waiting for transfers between devices  12.3 us (11%)
  Pallas kernels  7.87 us (7%)
  other arithmetic  4.58 us (4%)
  local copies, waits for them, and re-layouts  1.32 us (1%)
    ppermute x6, starting transfers between devices, shift(): lax.ppermute(block, axis, [(i, (i + step) % count) for i in range(count)])  33 us
    all_to_all x1, blocking collectives, work(): landed = lax.all_to_all(slots, ('x', 'z'), 0, 0, tiled=True).sum(axis=0)  32.8 us
    all_to_all x1, starting transfers between devices, work(): held = lax.all_to_all(slots, 'y', 0, 0, tiled=True)  8.71 us
    pallas_call x1, Pallas kernels, two_steps(): pl.pallas_call(steps_kernel, out_shape=(jax.ShapeDtypeStruct((2,) + phase...  7.87 us
    ppermute x2, starting transfers between devices, work(): lax.ppermute(rows_of[:, step], 'grow', [(0, 2 * step), (1, 2 * step + 1)])  7.05 us
    all_to_all x1, waiting for transfers between devices, work(): held = lax.all_to_all(slots, 'y', 0, 0, tiled=True)  6.97 us
    ppermute x6, waiting for transfers between devices, shift(): lax.ppermute(block, axis, [(i, (i + step) % count) for i in range(count)])  3.91 us
  transfers between devices with their start and end apart: 11, of which 5 were waited for; matrix products, arithmetic and copies ran while one was open for 3% of the time, Pallas kernels for 0%

profile of v8, /device:TPU:8, one launch (start us, length us, event | category | flops | bytes accessed | tf_op | source)
XLA Modules:
  0.0 111.2 jit_solution(4225655108660335429)
XLA Ops:
  0.6 0.0 copy-start
  0.6 0.0 copy-start.1
  0.7 0.0 copy-start.2
  0.7 1.0 pad_maximum_fusion
  1.7 14.0 %collective-permute-start.3 = (f32[2,2,4,1536]{3,2,1,0:T(4,128)S(1)}, f32[2,2,4,1536]{3,2,1,0:T(4,128)S(1)}, u32[]{:S(2)}, u32[]{:S(2)}) collective-permute-start(f32[2,2,4,1536]{3,2,1,0:T(4,128)S(1)} %get-tuple-element.14), channel_id=1, source_target_pairs={{0,5},{1,0},{2,1},{3,2},{4,3},{5,4},{6,11},{7,6},{8,7},{9,8},{10,9... | collective-permute-start | bytes 294920 | tf_op jit(solution)/shard_map/ppermute | solution.py:24
  15.7 1.9 %collective-permute-start.2 = (f32[2,2,4,1536]{3,2,1,0:T(4,128)S(1)}, f32[2,2,4,1536]{3,2,1,0:T(4,128)S(1)}, u32[]{:S(2)}, u32[]{:S(2)}) collective-permute-start(f32[2,2,4,1536]{3,2,1,0:T(4,128)S(1)} %get-tuple-element.15), channel_id=1, source_target_pairs={{0,1},{1,2},{2,3},{3,4},{4,5},{5,0},{6,7},{7,8},{8,9},{9,10},{10,1... | collective-permute-start | bytes 294920 | tf_op jit(solution)/shard_map/ppermute | solution.py:24
  17.6 0.0 copy-done.1
  17.6 0.0 copy-done.2
  17.6 0.3 fusion.1
  17.9 3.4 %collective-permute-start = (f32[2,16,2,1536]{3,2,1,0:T(2,128)S(1)}, f32[2,16,2,1536]{3,2,1,0:T(2,128)S(1)}, u32[]{:S(2)}, u32[]{:S(2)}) collective-permute-start(f32[2,16,2,1536]{3,2,1,0:T(2,128)S(1)} %get-tuple-element.17), channel_id=1, source_target_pairs={{0,6},{6,12},{12,18},{18,24},{24,30},{30,36},{36,42},{42,48},{48,5... | collective-permute-start | bytes 1179656 | tf_op jit(solution)/shard_map/ppermute | solution.py:24
  21.3 5.2 %collective-permute-start.1 = (f32[2,16,2,1536]{3,2,1,0:T(2,128)S(1)}, f32[2,16,2,1536]{3,2,1,0:T(2,128)S(1)}, u32[]{:S(2)}, u32[]{:S(2)}) collective-permute-start(f32[2,16,2,1536]{3,2,1,0:T(2,128)S(1)} %get-tuple-element.16), channel_id=1, source_target_pairs={{0,762},{6,0},{12,6},{18,12},{24,18},{30,24},{36,30},{42,36},{48,4... | collective-permute-start | bytes 1179656 | tf_op jit(solution)/shard_map/ppermute | solution.py:24
  26.5 0.0 copy-start.5
  26.5 0.7 copy-done.5
  27.2 0.0 copy-start.4
  27.2 0.0 copy-done
  27.2 0.2 dynamic-slice_reduce_fusion.1
  27.4 0.6 pad_maximum_fusion.3.weights
  28.1 0.0 copy-start.3
  28.1 0.0 collective-permute-done.3.above
  28.1 0.0 copy-done.4
  28.1 1.3 %collective-permute-done.2.below = f32[2,2,4,1536]{3,2,1,0:T(4,128)S(1)} collective-permute-done((f32[2,2,4,1536]{3,2,1,0:T(4,128)S(1)}, f32[2,2,4,1536]{3,2,1,0:T(4,128)S(1)}, u32[]{:S(2)}, u32[]{:S(2)}) %collective-permute-start.2) | collective-permute-done | bytes 98336 | tf_op jit(solution)/shard_map/ppermute | solution.py:24
  29.5 0.0 copy-done.3
  29.5 3.5 %collective-permute-start.4 = (f32[2,2,1,1536]{3,2,1,0:T(1,128)S(1)}, f32[2,2,1,1536]{3,2,1,0:T(1,128)S(1)}, u32[]{:S(2)}, u32[]{:S(2)}) collective-permute-start(f32[2,2,1,1536]{3,2,1,0:T(1,128)S(1)} %get-tuple-element.19), channel_id=1, source_target_pairs={{0,6},{6,12},{12,18},{18,24},{24,30},{30,36},{36,42},{42,48},{48,5... | collective-permute-start | bytes 73736 | tf_op jit(solution)/shard_map/ppermute | solution.py:24
  33.0 5.1 %collective-permute-start.5 = (f32[2,2,1,1536]{3,2,1,0:T(1,128)S(1)}, f32[2,2,1,1536]{3,2,1,0:T(1,128)S(1)}, u32[]{:S(2)}, u32[]{:S(2)}) collective-permute-start(f32[2,2,1,1536]{3,2,1,0:T(1,128)S(1)} %get-tuple-element.18), channel_id=1, source_target_pairs={{0,762},{6,0},{12,6},{18,12},{24,18},{30,24},{36,30},{42,36},{48,4... | collective-permute-start | bytes 73736 | tf_op jit(solution)/shard_map/ppermute | solution.py:24
  38.1 0.7 pad_add_fusion.at
  38.7 2.3 %collective-permute-done.4.edge_l = f32[2,2,1,1536]{3,2,1,0:T(1,128)S(1)} collective-permute-done((f32[2,2,1,1536]{3,2,1,0:T(1,128)S(1)}, f32[2,2,1,1536]{3,2,1,0:T(1,128)S(1)}, u32[]{:S(2)}, u32[]{:S(2)}) %collective-permute-start.4) | collective-permute-done | bytes 24608 | tf_op jit(solution)/shard_map/ppermute | solution.py:24
  41.1 0.2 collective-permute-done.5.edge_r
  41.3 0.0 collective-permute-done.left
  41.3 0.0 collective-permute-done.1.right
  41.3 7.9 %shard_map.67 = (f32[2,16,4,1536]{3,2,1,0:T(4,128)}, f32[8,2,3,4,128]{4,3,2,1,0:T(4,128)}) custom-call(s32[8]{0:T(128)} %pad_add_fusion.at, f32[16,4,1536]{2,1,0:T(4,128)} %phase.1, f32[16,4,1536]{2,1,0:T(4,128)} %solute.1, f32[2,16,2,1536]{3,2,1,0:T(2,128)S(1)} %collective-permute-done.left, f32[2,16,2,1536]{3,2,1,0:T(2,128)S(1)} %collective-permute-done.1.right, ...), custom_call_target="tpu_custom_call" | custom-call | tf_op jit(solution)/shard_map/pallas_call | solution.py:233
  49.2 8.7 %all-to-all-start = ((f32[8,2,3,4,128]{4,3,2,1,0:T(4,128)}), f32[8,2,3,4,128]{4,3,2,1,0:T(4,128)S(1)}, u32[]{:S(2)}, u32[]{:S(2)}) async-start(f32[8,2,3,4,128]{4,3,2,1,0:T(4,128)} %get-tuple-element.6), calls=%async_computation | async-start | bytes 196608 | tf_op jit(solution)/shard_map/all_to_all | solution.py:283
  57.9 0.1 reshape.114
  58.0 0.2 dynamic-slice_reduce_fusion
  58.2 7.0 %all-to-all-done = f32[8,2,3,4,128]{4,3,2,1,0:T(4,128)S(1)} async-done(((f32[8,2,3,4,128]{4,3,2,1,0:T(4,128)}), f32[8,2,3,4,128]{4,3,2,1,0:T(4,128)S(1)}, u32[]{:S(2)}, u32[]{:S(2)}) %all-to-all-start) | async-done | bytes 98336 | tf_op jit(solution)/shard_map/all_to_all | solution.py:283
  65.2 1.3 %collective-permute-start.7 = (f32[8,3,4,128]{3,2,1,0:T(4,128)S(1)}, f32[8,3,4,128]{3,2,1,0:T(4,128)S(1)}, u32[]{:S(2)}, u32[]{:S(2)}) collective-permute-start(f32[8,3,4,128]{3,2,1,0:T(4,128)S(1)} %slice_bitcast_fusion), channel_id=1, source_target_pairs={{0,1},{6,7},{12,13},{18,19},{24,25},{30,31},{36,37},{42,43},{48,49... | collective-permute-start | bytes 147464 | tf_op jit(solution)/shard_map/ppermute | solution.py:284
  66.5 1.3 %collective-permute-start.6 = (f32[2,16,4,1536]{3,2,1,0:T(4,128)}, f32[2,16,4,1536]{3,2,1,0:T(4,128)S(1)}, u32[]{:S(2)}, u32[]{:S(2)}) collective-permute-start(f32[2,16,4,1536]{3,2,1,0:T(4,128)} %get-tuple-element.5), channel_id=1, source_target_pairs={{1,0},{2,1},{3,2},{4,3},{5,4},{7,6},{8,7},{9,8},{10,9},{11,10},{13... | collective-permute-start | bytes 2359304 | tf_op jit(solution)/shard_map/ppermute | solution.py:278
  67.8 0.0 collective-permute-done.7
  67.9 5.5 %collective-permute-start.8 = (f32[8,4,128]{2,1,0:T(4,128)S(1)}, f32[8,4,128]{2,1,0:T(4,128)S(1)}, u32[]{:S(2)}, u32[]{:S(2)}) collective-permute-start(f32[8,4,128]{2,1,0:T(4,128)S(1)} %get-tuple-element.20), channel_id=1, source_target_pairs={{0,2},{1,3},{6,8},{7,9},{12,14},{13,15},{18,20},{19,21},{24,26},{2... | collective-permute-start | bytes 49160 | tf_op jit(solution)/shard_map/ppermute | solution.py:288
  73.3 1.6 %collective-permute-start.9 = (f32[8,4,128]{2,1,0:T(4,128)S(1)}, f32[8,4,128]{2,1,0:T(4,128)S(1)}, u32[]{:S(2)}, u32[]{:S(2)}) collective-permute-start(f32[8,4,128]{2,1,0:T(4,128)S(1)} %get-tuple-element.21), channel_id=1, source_target_pairs={{0,4},{1,5},{6,10},{7,11},{12,16},{13,17},{18,22},{19,23},{24,28},... | collective-permute-start | bytes 49160 | tf_op jit(solution)/shard_map/ppermute | solution.py:288
  75.0 0.0 collective-permute-done.8
  75.0 1.4 %collective-permute-done.9 = f32[8,4,128]{2,1,0:T(4,128)S(1)} collective-permute-done((f32[8,4,128]{2,1,0:T(4,128)S(1)}, f32[8,4,128]{2,1,0:T(4,128)S(1)}, u32[]{:S(2)}, u32[]{:S(2)}) %collective-permute-start.9) | collective-permute-done | bytes 16416 | tf_op jit(solution)/shard_map/ppermute | solution.py:288
  76.4 0.2 select_reduce_fusion
  76.5 32.8 %all_to_all.10 = f32[16,4,128]{2,1,0:T(4,128)S(1)} all-to-all(f32[16,4,128]{2,1,0:T(4,128)S(1)} %select_reduce_fusion), channel_id=1, replica_groups=mesh['x'=4,'y'=8,'z'=4,'grow'=6] {'x','z'}, dimensions={0} | all-to-all | bytes 65536 | tf_op jit(solution)/shard_map/all_to_all | solution.py:298
  109.4 0.1 slice_bitcast_fusion.6
  109.5 0.6 pad_maximum_fusion.4
  110.1 0.0 collective-permute-done.6
  110.1 1.1 fusion.2
  (17 shorter events, 0.2 us)
Async XLA Ops:
  0.6 26.6 %copy-start = (s32[6,128]{1,0:T(8,128)S(1)}, s32[6,128]{1,0:T(8,128)}, u32[]{:S(2)}) copy-start(s32[6,128]{1,0:T(8,128)} %param.7) | copy-start | bytes 9220
  0.6 16.9 %copy-start.1 = (f32[16,4,1536]{2,1,0:T(4,128)S(1)}, f32[16,4,1536]{2,1,0:T(4,128)}, u32[]{:S(2)}) copy-start(f32[16,4,1536]{2,1,0:T(4,128)} %phase.1) | copy-start | bytes 1179652
  0.7 16.9 %copy-start.2 = (f32[16,4,1536]{2,1,0:T(4,128)S(1)}, f32[16,4,1536]{2,1,0:T(4,128)}, u32[]{:S(2)}) copy-start(f32[16,4,1536]{2,1,0:T(4,128)} %solute.1) | copy-start | bytes 1179652
  1.7 26.4 %collective-permute-start.3 = (f32[2,2,4,1536]{3,2,1,0:T(4,128)S(1)}, f32[2,2,4,1536]{3,2,1,0:T(4,128)S(1)}, u32[]{:S(2)}, u32[]{:S(2)}) collective-permute-start(f32[2,2,4,1536]{3,2,1,0:T(4,128)S(1)} %get-tuple-element.14), channel_id=1, source_target_pairs={{0,5},{1,0},{2,1},{3,2},{4,3},{5,4},{6,11},{7,6},{8,7},{9,8},{10,9... | collective-permute-start | bytes 294920 | tf_op jit(solution)/shard_map/ppermute | solution.py:24
  15.7 13.8 %collective-permute-start.2 = (f32[2,2,4,1536]{3,2,1,0:T(4,128)S(1)}, f32[2,2,4,1536]{3,2,1,0:T(4,128)S(1)}, u32[]{:S(2)}, u32[]{:S(2)}) collective-permute-start(f32[2,2,4,1536]{3,2,1,0:T(4,128)S(1)} %get-tuple-element.15), channel_id=1, source_target_pairs={{0,1},{1,2},{2,3},{3,4},{4,5},{5,0},{6,7},{7,8},{8,9},{9,10},{10,1... | collective-permute-start | bytes 294920 | tf_op jit(solution)/shard_map/ppermute | solution.py:24
  17.9 23.4 %collective-permute-start = (f32[2,16,2,1536]{3,2,1,0:T(2,128)S(1)}, f32[2,16,2,1536]{3,2,1,0:T(2,128)S(1)}, u32[]{:S(2)}, u32[]{:S(2)}) collective-permute-start(f32[2,16,2,1536]{3,2,1,0:T(2,128)S(1)} %get-tuple-element.17), channel_id=1, source_target_pairs={{0,6},{6,12},{12,18},{18,24},{24,30},{30,36},{36,42},{42,48},{48,5... | collective-permute-start | bytes 1179656 | tf_op jit(solution)/shard_map/ppermute | solution.py:24
  21.3 20.0 %collective-permute-start.1 = (f32[2,16,2,1536]{3,2,1,0:T(2,128)S(1)}, f32[2,16,2,1536]{3,2,1,0:T(2,128)S(1)}, u32[]{:S(2)}, u32[]{:S(2)}) collective-permute-start(f32[2,16,2,1536]{3,2,1,0:T(2,128)S(1)} %get-tuple-element.16), channel_id=1, source_target_pairs={{0,762},{6,0},{12,6},{18,12},{24,18},{30,24},{36,30},{42,36},{48,4... | collective-permute-start | bytes 1179656 | tf_op jit(solution)/shard_map/ppermute | solution.py:24
  26.5 0.7 copy-start.5
  27.2 0.9 copy-start.4
  28.1 1.4 %copy-start.3 = (f32[2,1,4,1536]{3,2,1,0:T(4,128)S(1)}, f32[2,1,4,1536]{3,2,1,0:T(4,128)}, u32[]{:S(2)}) copy-start(f32[2,1,4,1536]{3,2,1,0:T(4,128)} %constant.131.clone.1) | copy-start | bytes 147460
  29.5 11.6 %collective-permute-start.4 = (f32[2,2,1,1536]{3,2,1,0:T(1,128)S(1)}, f32[2,2,1,1536]{3,2,1,0:T(1,128)S(1)}, u32[]{:S(2)}, u32[]{:S(2)}) collective-permute-start(f32[2,2,1,1536]{3,2,1,0:T(1,128)S(1)} %get-tuple-element.19), channel_id=1, source_target_pairs={{0,6},{6,12},{12,18},{18,24},{24,30},{30,36},{36,42},{42,48},{48,5... | collective-permute-start | bytes 73736 | tf_op jit(solution)/shard_map/ppermute | solution.py:24
  33.0 8.3 %collective-permute-start.5 = (f32[2,2,1,1536]{3,2,1,0:T(1,128)S(1)}, f32[2,2,1,1536]{3,2,1,0:T(1,128)S(1)}, u32[]{:S(2)}, u32[]{:S(2)}) collective-permute-start(f32[2,2,1,1536]{3,2,1,0:T(1,128)S(1)} %get-tuple-element.18), channel_id=1, source_target_pairs={{0,762},{6,0},{12,6},{18,12},{24,18},{30,24},{36,30},{42,36},{48,4... | collective-permute-start | bytes 73736 | tf_op jit(solution)/shard_map/ppermute | solution.py:24
  49.2 16.0 %all-to-all-start = ((f32[8,2,3,4,128]{4,3,2,1,0:T(4,128)}), f32[8,2,3,4,128]{4,3,2,1,0:T(4,128)S(1)}, u32[]{:S(2)}, u32[]{:S(2)}) async-start(f32[8,2,3,4,128]{4,3,2,1,0:T(4,128)} %get-tuple-element.6), calls=%async_computation | async-start | bytes 196608 | tf_op jit(solution)/shard_map/all_to_all | solution.py:283
  65.2 2.6 %collective-permute-start.7 = (f32[8,3,4,128]{3,2,1,0:T(4,128)S(1)}, f32[8,3,4,128]{3,2,1,0:T(4,128)S(1)}, u32[]{:S(2)}, u32[]{:S(2)}) collective-permute-start(f32[8,3,4,128]{3,2,1,0:T(4,128)S(1)} %slice_bitcast_fusion), channel_id=1, source_target_pairs={{0,1},{6,7},{12,13},{18,19},{24,25},{30,31},{36,37},{42,43},{48,49... | collective-permute-start | bytes 147464 | tf_op jit(solution)/shard_map/ppermute | solution.py:284
  66.5 43.6 %collective-permute-start.6 = (f32[2,16,4,1536]{3,2,1,0:T(4,128)}, f32[2,16,4,1536]{3,2,1,0:T(4,128)S(1)}, u32[]{:S(2)}, u32[]{:S(2)}) collective-permute-start(f32[2,16,4,1536]{3,2,1,0:T(4,128)} %get-tuple-element.5), channel_id=1, source_target_pairs={{1,0},{2,1},{3,2},{4,3},{5,4},{7,6},{8,7},{9,8},{10,9},{11,10},{13... | collective-permute-start | bytes 2359304 | tf_op jit(solution)/shard_map/ppermute | solution.py:278
  67.9 7.1 %collective-permute-start.8 = (f32[8,4,128]{2,1,0:T(4,128)S(1)}, f32[8,4,128]{2,1,0:T(4,128)S(1)}, u32[]{:S(2)}, u32[]{:S(2)}) collective-permute-start(f32[8,4,128]{2,1,0:T(4,128)S(1)} %get-tuple-element.20), channel_id=1, source_target_pairs={{0,2},{1,3},{6,8},{7,9},{12,14},{13,15},{18,20},{19,21},{24,26},{2... | collective-permute-start | bytes 49160 | tf_op jit(solution)/shard_map/ppermute | solution.py:288
  73.3 3.0 %collective-permute-start.9 = (f32[8,4,128]{2,1,0:T(4,128)S(1)}, f32[8,4,128]{2,1,0:T(4,128)S(1)}, u32[]{:S(2)}, u32[]{:S(2)}) collective-permute-start(f32[8,4,128]{2,1,0:T(4,128)S(1)} %get-tuple-element.21), channel_id=1, source_target_pairs={{0,4},{1,5},{6,10},{7,11},{12,16},{13,17},{18,22},{19,23},{24,28},... | collective-permute-start | bytes 49160 | tf_op jit(solution)/shard_map/ppermute | solution.py:288

commit v9 on v8

--- a/solution.py
+++ b/solution.py
@@ -10,6 +10,7 @@
 LAT = ("x", "y", "z")
 GRID = (4, 8, 4, 6)
 LANES = 128
+RELAYED = 384
 
 time_step = 0.15
 aniso_strength = 0.15
@@ -68,13 +69,14 @@
 
 
 def steps_kernel(
-    at, phase, solute, left, right, below, above, edge_l, edge_r, weights, state_to, slots_to,
+    at, phase, solute, left, right, below, above, edge_l, edge_r, weights, direct_to, relay_to, slots_to,
     op, ou, dp, du, opr, our, dpr, dur, sp, su, spr, sur, tpr, tur, sums,
 ):
     planes, rows, width = phase.shape
     pairs = planes // 2
     last = pairs + 1
     chunks = width // LANES
+    direct_chunks = direct_to.shape[-1] // LANES
     grow_at = at[0]
     lowest = grow_at == 0
     highest = grow_at == at[1] - 1
@@ -185,10 +187,13 @@
             p, u = tile_step((sp, spr, tpr), (su, sur, tur), t, t - 1, t + 1, theta, c)
             sums[0, k, c : c + 1] = jnp.sum(p, axis=0, keepdims=True)
             sums[1, k, c : c + 1] = jnp.sum(u, axis=0, keepdims=True)
-            state_to[0, 2 * k, :, here] = p[:rows]
-            state_to[0, 2 * k + 1, :, here] = p[rows:]
-            state_to[1, 2 * k, :, here] = u[:rows]
-            state_to[1, 2 * k + 1, :, here] = u[rows:]
+            straight = c < direct_chunks
+            state_to = direct_to if straight else relay_to
+            there = pl.ds((c if straight else c - direct_chunks) * LANES, LANES)
+            state_to[0, 2 * k, :, there] = p[:rows]
+            state_to[0, 2 * k + 1, :, there] = p[rows:]
+            state_to[1, 2 * k, :, there] = u[:rows]
+            state_to[1, 2 * k + 1, :, there] = u[rows:]
         return carry
 
     lax.fori_loop(0, pairs, own_twice, 0)
@@ -233,11 +238,12 @@
     return pl.pallas_call(
         steps_kernel,
         out_shape=(
-            jax.ShapeDtypeStruct((2,) + phase.shape, jnp.float32),
+            jax.ShapeDtypeStruct((2, planes, rows, width - RELAYED), jnp.float32),
+            jax.ShapeDtypeStruct((2, planes, rows, RELAYED), jnp.float32),
             jax.ShapeDtypeStruct((y_count, 2, pieces // 2, pairs // 2, LANES), jnp.float32),
         ),
         in_specs=[pl.BlockSpec(memory_space=pltpu.SMEM)] + [vmem] * 9,
-        out_specs=(vmem, vmem),
+        out_specs=(vmem, vmem, vmem),
         scratch_shapes=[scratch] * 14 + [pltpu.VMEM((2, pairs, width // LANES, LANES), jnp.float32)],
         interpret=interpret,
     )(at, phase, solute, left, right, below, above, edge_l, edge_r, weights)
@@ -273,9 +279,16 @@
     targets = lax.dynamic_index_in_dim(writer, lat_at, 1, keepdims=False)
     at = jnp.concatenate([jnp.stack([grow_at, jnp.int32(grow_count)]), targets // z_count % y_count])
     halos = tuple(near(halo) for halo in (left, right, below, above, edge_l, edge_r))
-    state, slots = two_steps(at, phase, solute, *halos, weights, grow_count, y_count)
-
-    arrived = lax.ppermute(state, "grow", [(i, i - 1) for i in range(1, grow_count)])
+    direct, relayed, slots = two_steps(at, phase, solute, *halos, weights, grow_count, y_count)
+
+    inside = [(i, i - 1) for i in range(1, grow_count, 2)]
+    down = range(2, grow_count, 2)
+    first_hop = [(i, (i + 3) % grow_count) for i in down]
+    second_hop = [((i + 3) % grow_count, i - 1) for i in down]
+    direct = lax.ppermute(direct, "grow", [(i, i - 1) for i in range(1, grow_count)])
+    relayed = lax.ppermute(relayed, "grow", inside + first_hop)
+    onto = lax.ppermute(relayed, "grow", second_hop)
+    arrived = jnp.concatenate([direct, jnp.where(grow_at % 2 == 0, relayed, onto)], axis=-1)
     top = grow_at == grow_count - 1
     phase_out = jnp.where(top, -1.0, arrived[0])
     solute_out = jnp.where(top, liquid_u, arrived[1])

time: 112 us -> 120 us (1.071)
  the two profiles are of different devices: /device:TPU:8 before, /device:TPU:1 now
where the time goes in v9:
time: 120 us; the launch traced here: 119 us
  starting transfers between devices  61.9 us (52%)
  waiting for transfers between devices  41.3 us (34%)
  Pallas kernels  7.87 us (7%)
  other arithmetic  5.15 us (4%)
  local copies, waits for them, and re-layouts  2.05 us (2%)
    ppermute x6, starting transfers between devices, shift(): lax.ppermute(block, axis, [(i, (i + step) % count) for i in range(count)])  39.6 us
    ppermute x1, waiting for transfers between devices, work(): lax.ppermute(direct, 'grow', [(i, i - 1) for i in range(1, grow_count)])  17.1 us
    all_to_all x1, starting transfers between devices, work(): landed = lax.all_to_all(slots, ('x', 'z'), 0, 0, tiled=True).sum(axis=0)  7.9 us
    pallas_call x1, Pallas kernels, two_steps(): pl.pallas_call(steps_kernel, out_shape=(jax.ShapeDtypeStruct((2, planes,...  7.87 us
    ppermute x1, waiting for transfers between devices, work(): onto = lax.ppermute(relayed, 'grow', second_hop)  7.78 us
    all_to_all x1, waiting for transfers between devices, work(): held = lax.all_to_all(slots, 'y', 0, 0, tiled=True)  7.36 us
    ppermute x1, waiting for transfers between devices, work(): relayed = lax.ppermute(relayed, 'grow', inside + first_hop)  4.55 us
    all_to_all x1, starting transfers between devices, work(): held = lax.all_to_all(slots, 'y', 0, 0, tiled=True)  3.76 us
  transfers between devices with their start and end apart: 14, of which 6 were waited for; matrix products, arithmetic and copies ran while one was open for 3% of the time, Pallas kernels for 0%

profile of v9, /device:TPU:1, one launch (start us, length us, event | category | flops | bytes accessed | tf_op | source)
XLA Modules:
  0.0 119.4 jit_solution(3219799207099769291)
XLA Ops:
  0.6 0.0 copy-start
  0.6 0.0 copy-start.1
  0.7 0.0 copy-start.2
  0.7 1.0 pad_maximum_fusion.1
  1.7 12.4 %collective-permute-start.3 = (f32[2,2,4,1536]{3,2,1,0:T(4,128)S(1)}, f32[2,2,4,1536]{3,2,1,0:T(4,128)S(1)}, u32[]{:S(2)}, u32[]{:S(2)}) collective-permute-start(f32[2,2,4,1536]{3,2,1,0:T(4,128)S(1)} %get-tuple-element.16), channel_id=1, source_target_pairs={{0,5},{1,0},{2,1},{3,2},{4,3},{5,4},{6,11},{7,6},{8,7},{9,8},{10,9... | collective-permute-start | bytes 294920 | tf_op jit(solution)/shard_map/ppermute | solution.py:25
  14.1 1.9 %collective-permute-start.2 = (f32[2,2,4,1536]{3,2,1,0:T(4,128)S(1)}, f32[2,2,4,1536]{3,2,1,0:T(4,128)S(1)}, u32[]{:S(2)}, u32[]{:S(2)}) collective-permute-start(f32[2,2,4,1536]{3,2,1,0:T(4,128)S(1)} %get-tuple-element.17), channel_id=1, source_target_pairs={{0,1},{1,2},{2,3},{3,4},{4,5},{5,0},{6,7},{7,8},{8,9},{9,10},{10,1... | collective-permute-start | bytes 294920 | tf_op jit(solution)/shard_map/ppermute | solution.py:25
  16.0 0.0 copy-done.1
  16.0 0.3 fusion.4
  16.3 3.6 %collective-permute-start = (f32[2,16,2,1536]{3,2,1,0:T(2,128)S(1)}, f32[2,16,2,1536]{3,2,1,0:T(2,128)S(1)}, u32[]{:S(2)}, u32[]{:S(2)}) collective-permute-start(f32[2,16,2,1536]{3,2,1,0:T(2,128)S(1)} %get-tuple-element.19), channel_id=1, source_target_pairs={{0,6},{6,12},{12,18},{18,24},{24,30},{30,36},{36,42},{42,48},{48,5... | collective-permute-start | bytes 1179656 | tf_op jit(solution)/shard_map/ppermute | solution.py:25
  20.0 10.3 %collective-permute-start.1 = (f32[2,16,2,1536]{3,2,1,0:T(2,128)S(1)}, f32[2,16,2,1536]{3,2,1,0:T(2,128)S(1)}, u32[]{:S(2)}, u32[]{:S(2)}) collective-permute-start(f32[2,16,2,1536]{3,2,1,0:T(2,128)S(1)} %get-tuple-element.18), channel_id=1, source_target_pairs={{0,762},{6,0},{12,6},{18,12},{24,18},{30,24},{36,30},{42,36},{48,4... | collective-permute-start | bytes 1179656 | tf_op jit(solution)/shard_map/ppermute | solution.py:25
  30.3 0.0 copy-start.5
  30.3 0.7 copy-done.5
  31.1 0.2 dynamic-slice_reduce_fusion.1
  31.3 0.6 pad_maximum_fusion.4.weights
  31.9 0.0 copy-start.3
  31.9 0.0 collective-permute-done.3.above
  32.0 0.0 collective-permute-done.2.below
  32.0 0.7 copy-done.3
  32.8 1.9 %collective-permute-start.4 = (f32[2,2,1,1536]{3,2,1,0:T(1,128)S(1)}, f32[2,2,1,1536]{3,2,1,0:T(1,128)S(1)}, u32[]{:S(2)}, u32[]{:S(2)}) collective-permute-start(f32[2,2,1,1536]{3,2,1,0:T(1,128)S(1)} %get-tuple-element.21), channel_id=1, source_target_pairs={{0,6},{6,12},{12,18},{18,24},{24,30},{30,36},{36,42},{42,48},{48,5... | collective-permute-start | bytes 73736 | tf_op jit(solution)/shard_map/ppermute | solution.py:25
  34.7 9.4 %collective-permute-start.5 = (f32[2,2,1,1536]{3,2,1,0:T(1,128)S(1)}, f32[2,2,1,1536]{3,2,1,0:T(1,128)S(1)}, u32[]{:S(2)}, u32[]{:S(2)}) collective-permute-start(f32[2,2,1,1536]{3,2,1,0:T(1,128)S(1)} %get-tuple-element.20), channel_id=1, source_target_pairs={{0,762},{6,0},{12,6},{18,12},{24,18},{30,24},{36,30},{42,36},{48,4... | collective-permute-start | bytes 73736 | tf_op jit(solution)/shard_map/ppermute | solution.py:25
  44.1 0.6 pad_add_fusion.at
  44.7 0.8 collective-permute-done.4.edge_l
  45.5 0.0 collective-permute-done.5.edge_r
  45.5 0.0 collective-permute-done.left
  45.5 0.0 collective-permute-done.1.right
  45.5 7.9 %shard_map.67 = (f32[2,16,4,1152]{3,2,1,0:T(4,128)}, f32[2,16,4,384]{3,2,1,0:T(4,128)}, f32[8,2,3,4,128]{4,3,2,1,0:T(4,128)}) custom-call(s32[8]{0:T(128)} %pad_add_fusion.at, f32[16,4,1536]{2,1,0:T(4,128)} %phase.1, f32[16,4,1536]{2,1,0:T(4,128)} %solute.1, f32[2,16,2,1536]{3,2,1,0:T(2,128)S(1)} %collective-permute-done.left, ...), custom_call_target="tpu_custom_call" | custom-call | tf_op jit(solution)/shard_map/pallas_call | solution.py:238
  53.4 3.8 %all-to-all-start = ((f32[8,2,3,4,128]{4,3,2,1,0:T(4,128)}), f32[8,2,3,4,128]{4,3,2,1,0:T(4,128)S(1)}, u32[]{:S(2)}, u32[]{:S(2)}) async-start(f32[8,2,3,4,128]{4,3,2,1,0:T(4,128)} %get-tuple-element.8), calls=%async_computation | async-start | bytes 196608 | tf_op jit(solution)/shard_map/all_to_all | solution.py:296
  57.2 0.1 reshape.114
  57.3 0.2 dynamic-slice_reduce_fusion
  57.5 7.4 %all-to-all-done = f32[8,2,3,4,128]{4,3,2,1,0:T(4,128)S(1)} async-done(((f32[8,2,3,4,128]{4,3,2,1,0:T(4,128)}), f32[8,2,3,4,128]{4,3,2,1,0:T(4,128)S(1)}, u32[]{:S(2)}, u32[]{:S(2)}) %all-to-all-start) | async-done | bytes 98336 | tf_op jit(solution)/shard_map/all_to_all | solution.py:296
  64.8 1.3 %collective-permute-start.9 = (f32[8,3,4,128]{3,2,1,0:T(4,128)S(1)}, f32[8,3,4,128]{3,2,1,0:T(4,128)S(1)}, u32[]{:S(2)}, u32[]{:S(2)}) collective-permute-start(f32[8,3,4,128]{3,2,1,0:T(4,128)S(1)} %slice_bitcast_fusion), channel_id=1, source_target_pairs={{0,1},{6,7},{12,13},{18,19},{24,25},{30,31},{36,37},{42,43},{48,49... | collective-permute-start | bytes 147464 | tf_op jit(solution)/shard_map/ppermute | solution.py:297
  66.1 3.7 %collective-permute-done.9 = f32[8,3,4,128]{3,2,1,0:T(4,128)S(1)} collective-permute-done((f32[8,3,4,128]{3,2,1,0:T(4,128)S(1)}, f32[8,3,4,128]{3,2,1,0:T(4,128)S(1)}, u32[]{:S(2)}, u32[]{:S(2)}) %collective-permute-start.9) | collective-permute-done | bytes 49184 | tf_op jit(solution)/shard_map/ppermute | solution.py:297
  69.9 1.7 %collective-permute-start.10 = (f32[8,4,128]{2,1,0:T(4,128)S(1)}, f32[8,4,128]{2,1,0:T(4,128)S(1)}, u32[]{:S(2)}, u32[]{:S(2)}) collective-permute-start(f32[8,4,128]{2,1,0:T(4,128)S(1)} %get-tuple-element.22), channel_id=1, source_target_pairs={{0,2},{1,3},{6,8},{7,9},{12,14},{13,15},{18,20},{19,21},{24,26},{2... | collective-permute-start | bytes 49160 | tf_op jit(solution)/shard_map/ppermute | solution.py:301
  71.6 1.9 %collective-permute-start.11 = (f32[8,4,128]{2,1,0:T(4,128)S(1)}, f32[8,4,128]{2,1,0:T(4,128)S(1)}, u32[]{:S(2)}, u32[]{:S(2)}) collective-permute-start(f32[8,4,128]{2,1,0:T(4,128)S(1)} %get-tuple-element.23), channel_id=1, source_target_pairs={{0,4},{1,5},{6,10},{7,11},{12,16},{13,17},{18,22},{19,23},{24,28},... | collective-permute-start | bytes 49160 | tf_op jit(solution)/shard_map/ppermute | solution.py:301
  73.5 1.9 %collective-permute-start.7 = (f32[2,16,4,384]{3,2,1,0:T(4,128)}, f32[2,16,4,384]{3,2,1,0:T(4,128)S(1)}, u32[]{:S(2)}, u32[]{:S(2)}) collective-permute-start(f32[2,16,4,384]{3,2,1,0:T(4,128)} %get-tuple-element.7), channel_id=1, source_target_pairs={{1,0},{3,2},{5,4},{2,5},{4,1},{7,6},{9,8},{11,10},{8,11},{10,7},{1... | collective-permute-start | bytes 589832 | tf_op jit(solution)/shard_map/ppermute | solution.py:289
  75.5 0.0 collective-permute-done.10
  75.5 0.0 collective-permute-done.11
  75.5 0.8 select_reduce_fusion
  76.3 7.9 %all-to-all-start.1 = ((f32[16,4,128]{2,1,0:T(4,128)}), f32[16,4,128]{2,1,0:T(4,128)S(1)}, u32[]{:S(2)}, u32[]{:S(2)}) async-start(f32[16,4,128]{2,1,0:T(4,128)} %select_reduce_fusion), calls=%async_computation.1 | async-start | bytes 65536 | tf_op jit(solution)/shard_map/all_to_all | solution.py:311
  84.2 1.9 %collective-permute-start.6 = (f32[2,16,4,1152]{3,2,1,0:T(4,128)S(1)}, f32[2,16,4,1152]{3,2,1,0:T(4,128)S(1)}, u32[]{:S(2)}, u32[]{:S(2)}) collective-permute-start(f32[2,16,4,1152]{3,2,1,0:T(4,128)S(1)} %copy-done.6), channel_id=1, source_target_pairs={{1,0},{2,1},{3,2},{4,3},{5,4},{7,6},{8,7},{9,8},{10,9},{11,10},{13... | collective-permute-start | bytes 1769480 | tf_op jit(solution)/shard_map/ppermute | solution.py:288
  86.2 4.5 %collective-permute-done.7 = f32[2,16,4,384]{3,2,1,0:T(4,128)S(1)} collective-permute-done((f32[2,16,4,384]{3,2,1,0:T(4,128)}, f32[2,16,4,384]{3,2,1,0:T(4,128)S(1)}, u32[]{:S(2)}, u32[]{:S(2)}) %collective-permute-start.7) | collective-permute-done | bytes 196640 | tf_op jit(solution)/shard_map/ppermute | solution.py:289
  90.7 1.9 %collective-permute-start.8 = (f32[2,16,4,384]{3,2,1,0:T(4,128)S(1)}, f32[2,16,4,384]{3,2,1,0:T(4,128)S(1)}, u32[]{:S(2)}, u32[]{:S(2)}) collective-permute-start(f32[2,16,4,384]{3,2,1,0:T(4,128)S(1)} %collective-permute-done.7), channel_id=1, source_target_pairs={{5,1},{1,3},{11,7},{7,9},{17,13},{13,15},{23,19},{19,21},{29,25},{... | collective-permute-start | bytes 589832 | tf_op jit(solution)/shard_map/ppermute | solution.py:290
  92.6 0.0 all-to-all-done.1
  92.7 0.1 slice_bitcast_fusion.6
  92.7 0.6 pad_maximum_fusion.5
  93.3 7.8 %collective-permute-done.8 = f32[2,16,4,384]{3,2,1,0:T(4,128)S(1)} collective-permute-done((f32[2,16,4,384]{3,2,1,0:T(4,128)S(1)}, f32[2,16,4,384]{3,2,1,0:T(4,128)S(1)}, u32[]{:S(2)}, u32[]{:S(2)}) %collective-permute-start.8) | collective-permute-done | bytes 196640 | tf_op jit(solution)/shard_map/ppermute | solution.py:290
  101.1 17.1 %collective-permute-done.6 = f32[2,16,4,1152]{3,2,1,0:T(4,128)S(1)} collective-permute-done((f32[2,16,4,1152]{3,2,1,0:T(4,128)S(1)}, f32[2,16,4,1152]{3,2,1,0:T(4,128)S(1)}, u32[]{:S(2)}, u32[]{:S(2)}) %collective-permute-start.6) | collective-permute-done | bytes 589856 | tf_op jit(solution)/shard_map/ppermute | solution.py:288
  118.3 1.1 fusion.6
  (24 shorter events, 0.3 us)
Async XLA Ops:
  0.6 30.4 %copy-start = (s32[6,128]{1,0:T(8,128)S(1)}, s32[6,128]{1,0:T(8,128)}, u32[]{:S(2)}) copy-start(s32[6,128]{1,0:T(8,128)} %param.7) | copy-start | bytes 9220
  0.6 15.3 %copy-start.1 = (f32[16,4,1536]{2,1,0:T(4,128)S(1)}, f32[16,4,1536]{2,1,0:T(4,128)}, u32[]{:S(2)}) copy-start(f32[16,4,1536]{2,1,0:T(4,128)} %phase.1) | copy-start | bytes 1179652
  0.7 15.3 %copy-start.2 = (f32[16,4,1536]{2,1,0:T(4,128)S(1)}, f32[16,4,1536]{2,1,0:T(4,128)}, u32[]{:S(2)}) copy-start(f32[16,4,1536]{2,1,0:T(4,128)} %solute.1) | copy-start | bytes 1179652
  1.7 30.3 %collective-permute-start.3 = (f32[2,2,4,1536]{3,2,1,0:T(4,128)S(1)}, f32[2,2,4,1536]{3,2,1,0:T(4,128)S(1)}, u32[]{:S(2)}, u32[]{:S(2)}) collective-permute-start(f32[2,2,4,1536]{3,2,1,0:T(4,128)S(1)} %get-tuple-element.16), channel_id=1, source_target_pairs={{0,5},{1,0},{2,1},{3,2},{4,3},{5,4},{6,11},{7,6},{8,7},{9,8},{10,9... | collective-permute-start | bytes 294920 | tf_op jit(solution)/shard_map/ppermute | solution.py:25
  14.1 17.9 %collective-permute-start.2 = (f32[2,2,4,1536]{3,2,1,0:T(4,128)S(1)}, f32[2,2,4,1536]{3,2,1,0:T(4,128)S(1)}, u32[]{:S(2)}, u32[]{:S(2)}) collective-permute-start(f32[2,2,4,1536]{3,2,1,0:T(4,128)S(1)} %get-tuple-element.17), channel_id=1, source_target_pairs={{0,1},{1,2},{2,3},{3,4},{4,5},{5,0},{6,7},{7,8},{8,9},{9,10},{10,1... | collective-permute-start | bytes 294920 | tf_op jit(solution)/shard_map/ppermute | solution.py:25
  16.3 29.2 %collective-permute-start = (f32[2,16,2,1536]{3,2,1,0:T(2,128)S(1)}, f32[2,16,2,1536]{3,2,1,0:T(2,128)S(1)}, u32[]{:S(2)}, u32[]{:S(2)}) collective-permute-start(f32[2,16,2,1536]{3,2,1,0:T(2,128)S(1)} %get-tuple-element.19), channel_id=1, source_target_pairs={{0,6},{6,12},{12,18},{18,24},{24,30},{30,36},{36,42},{42,48},{48,5... | collective-permute-start | bytes 1179656 | tf_op jit(solution)/shard_map/ppermute | solution.py:25
  20.0 25.5 %collective-permute-start.1 = (f32[2,16,2,1536]{3,2,1,0:T(2,128)S(1)}, f32[2,16,2,1536]{3,2,1,0:T(2,128)S(1)}, u32[]{:S(2)}, u32[]{:S(2)}) collective-permute-start(f32[2,16,2,1536]{3,2,1,0:T(2,128)S(1)} %get-tuple-element.18), channel_id=1, source_target_pairs={{0,762},{6,0},{12,6},{18,12},{24,18},{30,24},{36,30},{42,36},{48,4... | collective-permute-start | bytes 1179656 | tf_op jit(solution)/shard_map/ppermute | solution.py:25
  30.3 0.7 copy-start.5
  31.0 0.9 copy-start.4
  31.9 0.8 copy-start.3
  32.8 12.7 %collective-permute-start.4 = (f32[2,2,1,1536]{3,2,1,0:T(1,128)S(1)}, f32[2,2,1,1536]{3,2,1,0:T(1,128)S(1)}, u32[]{:S(2)}, u32[]{:S(2)}) collective-permute-start(f32[2,2,1,1536]{3,2,1,0:T(1,128)S(1)} %get-tuple-element.21), channel_id=1, source_target_pairs={{0,6},{6,12},{12,18},{18,24},{24,30},{30,36},{36,42},{42,48},{48,5... | collective-permute-start | bytes 73736 | tf_op jit(solution)/shard_map/ppermute | solution.py:25
  34.7 10.8 %collective-permute-start.5 = (f32[2,2,1,1536]{3,2,1,0:T(1,128)S(1)}, f32[2,2,1,1536]{3,2,1,0:T(1,128)S(1)}, u32[]{:S(2)}, u32[]{:S(2)}) collective-permute-start(f32[2,2,1,1536]{3,2,1,0:T(1,128)S(1)} %get-tuple-element.20), channel_id=1, source_target_pairs={{0,762},{6,0},{12,6},{18,12},{24,18},{30,24},{36,30},{42,36},{48,4... | collective-permute-start | bytes 73736 | tf_op jit(solution)/shard_map/ppermute | solution.py:25
  53.4 30.8 %copy-start.6 = (f32[2,16,4,1152]{3,2,1,0:T(4,128)S(1)}, f32[2,16,4,1152]{3,2,1,0:T(4,128)}, u32[]{:S(2)}) copy-start(f32[2,16,4,1152]{3,2,1,0:T(4,128)} %get-tuple-element.6) | copy-start | bytes 1769476
  53.4 11.4 %all-to-all-start = ((f32[8,2,3,4,128]{4,3,2,1,0:T(4,128)}), f32[8,2,3,4,128]{4,3,2,1,0:T(4,128)S(1)}, u32[]{:S(2)}, u32[]{:S(2)}) async-start(f32[8,2,3,4,128]{4,3,2,1,0:T(4,128)} %get-tuple-element.8), calls=%async_computation | async-start | bytes 196608 | tf_op jit(solution)/shard_map/all_to_all | solution.py:296
  64.8 5.0 %collective-permute-start.9 = (f32[8,3,4,128]{3,2,1,0:T(4,128)S(1)}, f32[8,3,4,128]{3,2,1,0:T(4,128)S(1)}, u32[]{:S(2)}, u32[]{:S(2)}) collective-permute-start(f32[8,3,4,128]{3,2,1,0:T(4,128)S(1)} %slice_bitcast_fusion), channel_id=1, source_target_pairs={{0,1},{6,7},{12,13},{18,19},{24,25},{30,31},{36,37},{42,43},{48,49... | collective-permute-start | bytes 147464 | tf_op jit(solution)/shard_map/ppermute | solution.py:297
  69.9 5.6 %collective-permute-start.10 = (f32[8,4,128]{2,1,0:T(4,128)S(1)}, f32[8,4,128]{2,1,0:T(4,128)S(1)}, u32[]{:S(2)}, u32[]{:S(2)}) collective-permute-start(f32[8,4,128]{2,1,0:T(4,128)S(1)} %get-tuple-element.22), channel_id=1, source_target_pairs={{0,2},{1,3},{6,8},{7,9},{12,14},{13,15},{18,20},{19,21},{24,26},{2... | collective-permute-start | bytes 49160 | tf_op jit(solution)/shard_map/ppermute | solution.py:301
  71.6 3.9 %collective-permute-start.11 = (f32[8,4,128]{2,1,0:T(4,128)S(1)}, f32[8,4,128]{2,1,0:T(4,128)S(1)}, u32[]{:S(2)}, u32[]{:S(2)}) collective-permute-start(f32[8,4,128]{2,1,0:T(4,128)S(1)} %get-tuple-element.23), channel_id=1, source_target_pairs={{0,4},{1,5},{6,10},{7,11},{12,16},{13,17},{18,22},{19,23},{24,28},... | collective-permute-start | bytes 49160 | tf_op jit(solution)/shard_map/ppermute | solution.py:301
  73.5 17.2 %collective-permute-start.7 = (f32[2,16,4,384]{3,2,1,0:T(4,128)}, f32[2,16,4,384]{3,2,1,0:T(4,128)S(1)}, u32[]{:S(2)}, u32[]{:S(2)}) collective-permute-start(f32[2,16,4,384]{3,2,1,0:T(4,128)} %get-tuple-element.7), channel_id=1, source_target_pairs={{1,0},{3,2},{5,4},{2,5},{4,1},{7,6},{9,8},{11,10},{8,11},{10,7},{1... | collective-permute-start | bytes 589832 | tf_op jit(solution)/shard_map/ppermute | solution.py:289
  76.3 16.3 %all-to-all-start.1 = ((f32[16,4,128]{2,1,0:T(4,128)}), f32[16,4,128]{2,1,0:T(4,128)S(1)}, u32[]{:S(2)}, u32[]{:S(2)}) async-start(f32[16,4,128]{2,1,0:T(4,128)} %select_reduce_fusion), calls=%async_computation.1 | async-start | bytes 65536 | tf_op jit(solution)/shard_map/all_to_all | solution.py:311
  84.2 34.1 %collective-permute-start.6 = (f32[2,16,4,1152]{3,2,1,0:T(4,128)S(1)}, f32[2,16,4,1152]{3,2,1,0:T(4,128)S(1)}, u32[]{:S(2)}, u32[]{:S(2)}) collective-permute-start(f32[2,16,4,1152]{3,2,1,0:T(4,128)S(1)} %copy-done.6), channel_id=1, source_target_pairs={{1,0},{2,1},{3,2},{4,3},{5,4},{7,6},{8,7},{9,8},{10,9},{11,10},{13... | collective-permute-start | bytes 1769480 | tf_op jit(solution)/shard_map/ppermute | solution.py:288
  90.7 10.4 %collective-permute-start.8 = (f32[2,16,4,384]{3,2,1,0:T(4,128)S(1)}, f32[2,16,4,384]{3,2,1,0:T(4,128)S(1)}, u32[]{:S(2)}, u32[]{:S(2)}) collective-permute-start(f32[2,16,4,384]{3,2,1,0:T(4,128)S(1)} %collective-permute-done.7), channel_id=1, source_target_pairs={{5,1},{1,3},{11,7},{7,9},{17,13},{13,15},{23,19},{19,21},{29,25},{... | collective-permute-start | bytes 589832 | tf_op jit(solution)/shard_map/ppermute | solution.py:290
